TPU v7x, 32 devices: a whole 2x2x4 slice. The times are simulated.
32 devices in a mesh: dp: 8 (over z, x), tensor: 4 (over y, core).
Axes of the slice: x: 2, y: 2, z: 4, core: 2. Of those that a mesh axis runs over, the one named last changes fastest.
Arguments:
- frames: bfloat16 [8, 512, 1024], P('dp', 'tensor'), may hold values from -6 to 6
- lengths: int32 [8], P('dp'), may hold values from 64 to 512, as said below
- pos_weight: bfloat16 [128, 64, 1024], P(None, None, 'tensor'), may hold values from -0.0625 to 0.0625
- pos_bias: bfloat16 [1024], P('tensor'), may hold values from -3 to 3
- query_key_value_weight: bfloat16 [1024, 3, 1024], P(None, None, 'tensor'), may hold values from -0.1875 to 0.1875
- qv_bias: bfloat16 [2, 1024], P(None, 'tensor'), may hold values from -2 to 2
- out_weight: bfloat16 [1024, 1024], P('tensor'), may hold values from -2 to 2
- out_bias: bfloat16 [1024], replicated, may hold values from -3 to 3
- norm1_gain: bfloat16 [1024], replicated, may hold values from 0.5 to 1.5
- norm1_bias: bfloat16 [1024], replicated, may hold values from -3 to 3
- norm2_gain: bfloat16 [1024], replicated, may hold values from 0.5 to 1.5
- norm2_bias: bfloat16 [1024], replicated, may hold values from -3 to 3
- inner_weight: bfloat16 [1024, 4096], P(None, 'tensor'), may hold values from -0.1875 to 0.1875
- inner_bias: bfloat16 [4096], P('tensor'), may hold values from -3 to 3
- outer_weight: bfloat16 [4096, 1024], P('tensor'), may hold values from -0.09375 to 0.09375
- outer_bias: bfloat16 [1024], replicated, may hold values from -3 to 3
- cotangent: bfloat16 [8, 512, 1024], P('dp', 'tensor'), may hold values from -6 to 6
Outputs:
- output: bfloat16 [8, 512, 1024], P('dp', 'tensor')
- frames_grad: float32 [8, 512, 1024], P('dp', 'tensor')
- pos_weight_grad: float32 [128, 64, 1024], P('dp', None, 'tensor')
- pos_bias_grad: float32 [1024], replicated
- qkv_weight_grad: float32 [1024, 3, 1024], P('dp', None, 'tensor')
- qv_bias_grad: float32 [2, 1024], replicated
- out_weight_grad: float32 [1024, 1024], P('tensor', 'dp')
- out_bias_grad: float32 [1024], replicated
- norm1_gain_grad: float32 [1024], replicated
- norm1_bias_grad: float32 [1024], replicated
- norm2_gain_grad: float32 [1024], replicated
- norm2_bias_grad: float32 [1024], replicated
- inner_weight_grad: float32 [1024, 4096], P('dp', 'tensor')
- inner_bias_grad: float32 [4096], replicated
- outer_weight_grad: float32 [4096, 1024], P('tensor', 'dp')
- outer_bias_grad: float32 [1024], replicated
Inputs may be any that keep to these rules, and one draw needn't show every extreme that they name: `lengths`: frames of each utterance; some utterance fills all 512 slots.
All inputs are finite; a program needn't handle non-finite values.
Results may differ from a plain program's by a relative error of at most 0.02.
Values may be sent and summed in bfloat16 or wider, within the bound.
A program may use at most 192 MiB of HBM per device.

v0:
```python
import jax
import jax.numpy as jnp
from jax import lax
from jax.sharding import PartitionSpec as P

HEAD = 64


EPSILON = 1e-05
NEGATIVE = -1e30


def layer_norm(stream, gain_vec, shift_vec):
    average = jnp.mean(stream, axis=-1, keepdims=True)
    centered = stream - average
    variance = jnp.mean(centered * centered, axis=-1, keepdims=True)
    return centered * lax.rsqrt(variance + EPSILON) * gain_vec + shift_vec


def exact_gelu(values):
    return jax.nn.gelu(values, approximate=False)


def gelu_back(pre_values, grad_values):
    return jax.vjp(exact_gelu, pre_values)[1](grad_values)[0]


def row_scores(query_row, key_row, mask_row):
    slot_count = query_row.shape[0]
    query_heads = query_row.reshape(slot_count, -1, HEAD)
    key_heads = key_row.reshape(slot_count, -1, HEAD)
    scores = jnp.einsum(
        "qhd,khd->hqk", query_heads, key_heads, preferred_element_type=jnp.float32
    ) * HEAD ** (-0.5)
    return (jnp.where(mask_row[None, None, :], scores, NEGATIVE), query_heads, key_heads)


def attend_rows(queries, key_rows, value_rows, row_mask):

    def one_row(operands):
        query_row, key_row, value_row, mask_row = operands
        slot_count = query_row.shape[0]
        scores, query_heads, key_heads = row_scores(query_row, key_row, mask_row)
        value_heads = value_row.reshape(slot_count, -1, HEAD)
        row_top = jnp.max(scores, axis=-1, keepdims=True)
        exponent = jnp.exp(scores - row_top)
        row_total = jnp.sum(exponent, axis=-1, keepdims=True)
        prob_low = (exponent / row_total).astype(jnp.bfloat16)
        context = jnp.einsum(
            "hqk,khd->qhd", prob_low, value_heads, preferred_element_type=jnp.float32
        )
        log_total = (row_top + jnp.log(row_total))[..., 0]
        return (context.reshape(slot_count, -1).astype(jnp.bfloat16), log_total)

    return lax.map(one_row, (queries, key_rows, value_rows, row_mask))


def attend_back(queries, key_rows, value_rows, row_mask, log_totals, grad_context):

    def one_row(operands):
        query_row, key_row, value_row, mask_row, log_total, grad_row = operands
        slot_count = query_row.shape[0]
        scores, query_heads, key_heads = row_scores(query_row, key_row, mask_row)
        value_heads = value_row.reshape(slot_count, -1, HEAD)
        grad_heads = grad_row.reshape(slot_count, -1, HEAD)
        probs_all = jnp.exp(scores - log_total[..., None])
        prob_low = probs_all.astype(jnp.bfloat16)
        grad_probs = jnp.einsum(
            "qhd,khd->hqk", grad_heads, value_heads, preferred_element_type=jnp.float32
        )
        delta = jnp.sum(probs_all * grad_probs, axis=-1, keepdims=True)
        grad_scores = (probs_all * (grad_probs - delta)).astype(jnp.bfloat16)
        grad_query = jnp.einsum(
            "hqk,khd->qhd", grad_scores, key_heads, preferred_element_type=jnp.float32
        ) * HEAD ** (-0.5)
        grad_key = jnp.einsum(
            "hqk,qhd->khd", grad_scores, query_heads, preferred_element_type=jnp.float32
        ) * HEAD ** (-0.5)
        grad_value = jnp.einsum(
            "hqk,qhd->khd", prob_low, grad_heads, preferred_element_type=jnp.float32
        )
        joined = jnp.concatenate(
            [
                grad_query.reshape(slot_count, -1),
                grad_key.reshape(slot_count, -1),
                grad_value.reshape(slot_count, -1),
            ],
            axis=-1,
        )
        return joined.astype(jnp.bfloat16)

    return lax.map(one_row, (queries, key_rows, value_rows, row_mask, log_totals, grad_context))


def spread(values, full_width):
    start_col = lax.axis_index("tensor") * values.shape[-1]
    blank = jnp.zeros(values.shape[:-1] + (full_width,), jnp.float32)
    return lax.dynamic_update_slice_in_dim(blank, values, start_col, axis=values.ndim - 1)


def forward_pass(frames, lengths, params):
    (
        pos_weight,
        pos_bias,
        query_key_value_weight,
        qv_bias,
        out_weight,
        out_bias,
        norm1_gain,
        norm1_bias,
        norm2_gain,
        norm2_bias,
        inner_weight,
        inner_bias,
        outer_weight,
        outer_bias,
    ) = params
    row_count, segment_length, model_width = frames.shape
    slot_count = segment_length * lax.axis_size("tensor")
    offset = lax.axis_index("tensor") * segment_length
    seg_mask = offset + jnp.arange(segment_length, dtype=jnp.int32)[None, :] < lengths[:, None]
    row_mask = jnp.arange(slot_count, dtype=jnp.int32)[None, :] < lengths[:, None]
    zeroed = jnp.where(seg_mask[..., None], frames, jnp.zeros_like(frames))
    channels = lax.all_to_all(zeroed, "tensor", split_axis=2, concat_axis=1, tiled=True)
    kernel = pos_weight.shape[0]
    local_groups = pos_weight.shape[2] // pos_weight.shape[1]
    conv_pre = lax.conv_general_dilated(
        channels,
        pos_weight,
        (1,),
        [(kernel // 2, kernel // 2 - 1)],
        dimension_numbers=("NWC", "WIO", "NWC"),
        feature_group_count=local_groups,
        preferred_element_type=jnp.float32,
    ) + pos_bias.astype(jnp.float32)
    position = exact_gelu(conv_pre).astype(jnp.bfloat16)
    pos_seq = lax.all_to_all(position, "tensor", split_axis=1, concat_axis=2, tiled=True)
    stream_one = zeroed.astype(jnp.float32) + pos_seq.astype(jnp.float32)
    first_normed = layer_norm(
        stream_one, norm1_gain.astype(jnp.float32), norm1_bias.astype(jnp.float32)
    ).astype(jnp.bfloat16)
    full_one = lax.all_gather(first_normed, "tensor", axis=1, tiled=True)
    local_width = query_key_value_weight.shape[2]
    proj_weight = query_key_value_weight.reshape(model_width, 3 * local_width)
    proj_bias = jnp.concatenate([qv_bias[0], jnp.zeros_like(qv_bias[0]), qv_bias[1]]).astype(
        jnp.float32
    )
    projected_frames = (
        jnp.einsum("rtd,de->rte", full_one, proj_weight, preferred_element_type=jnp.float32)
        + proj_bias
    ).astype(jnp.bfloat16)
    queries = projected_frames[..., :local_width]
    key_rows = projected_frames[..., local_width : 2 * local_width]
    value_rows = projected_frames[..., 2 * local_width :]
    context, log_totals = attend_rows(queries, key_rows, value_rows, row_mask)
    partial_one = jnp.einsum("rtc,cd->rtd", context, out_weight, preferred_element_type=jnp.float32)
    attended = lax.psum_scatter(
        partial_one.astype(jnp.bfloat16), "tensor", scatter_dimension=1, tiled=True
    ).astype(jnp.float32) + out_bias.astype(jnp.float32)
    stream_two = stream_one + attended
    normed_two = layer_norm(
        stream_two, norm2_gain.astype(jnp.float32), norm2_bias.astype(jnp.float32)
    ).astype(jnp.bfloat16)
    full_two = lax.all_gather(normed_two, "tensor", axis=1, tiled=True)
    inner_pre = jnp.einsum(
        "rtd,df->rtf", full_two, inner_weight, preferred_element_type=jnp.float32
    ) + inner_bias.astype(jnp.float32)
    hidden = exact_gelu(inner_pre).astype(jnp.bfloat16)
    partial_two = jnp.einsum(
        "rtf,fd->rtd", hidden, outer_weight, preferred_element_type=jnp.float32
    )
    branch = lax.psum_scatter(
        partial_two.astype(jnp.bfloat16), "tensor", scatter_dimension=1, tiled=True
    ).astype(jnp.float32) + outer_bias.astype(jnp.float32)
    output = (stream_two + branch).astype(jnp.bfloat16)
    return (
        seg_mask,
        row_mask,
        channels,
        conv_pre,
        stream_one,
        full_one,
        projected_frames,
        context,
        log_totals,
        stream_two,
        full_two,
        inner_pre,
        hidden,
        output,
    )


def shards(
    frames,
    lengths,
    pos_weight,
    pos_bias,
    query_key_value_weight,
    qv_bias,
    out_weight,
    out_bias,
    norm1_gain,
    norm1_bias,
    norm2_gain,
    norm2_bias,
    inner_weight,
    inner_bias,
    outer_weight,
    outer_bias,
    cotangent,
):
    params = (
        pos_weight,
        pos_bias,
        query_key_value_weight,
        qv_bias,
        out_weight,
        out_bias,
        norm1_gain,
        norm1_bias,
        norm2_gain,
        norm2_bias,
        inner_weight,
        inner_bias,
        outer_weight,
        outer_bias,
    )
    first_pass = forward_pass(frames, lengths, params)
    output = first_pass[-1]
    frames_again, grad_in = lax.optimization_barrier((frames, cotangent))
    saved = forward_pass(frames_again, lengths, params)
    (
        seg_mask,
        row_mask,
        channels,
        conv_pre,
        stream_one,
        full_one,
        projected_frames,
        context,
        log_totals,
        stream_two,
        full_two,
        inner_pre,
        hidden,
        unused_out,
    ) = saved
    model_width = frames.shape[2]
    local_width = query_key_value_weight.shape[2]
    proj_weight = query_key_value_weight.reshape(model_width, 3 * local_width)
    cot_full = lax.all_gather(grad_in, "tensor", axis=1, tiled=True)
    outer_grad = jnp.einsum("rtf,rtd->fd", hidden, cot_full, preferred_element_type=jnp.float32)
    grad_hidden = jnp.einsum(
        "rtd,fd->rtf", cot_full, outer_weight, preferred_element_type=jnp.float32
    )
    grad_inner = gelu_back(inner_pre, grad_hidden).astype(jnp.bfloat16)
    inner_grad = jnp.einsum("rtd,rtf->df", full_two, grad_inner, preferred_element_type=jnp.float32)
    inner_bias_part = jnp.sum(grad_inner, axis=(0, 1), dtype=jnp.float32)
    grad_normed_two = lax.psum_scatter(
        jnp.einsum(
            "rtf,df->rtd", grad_inner, inner_weight, preferred_element_type=jnp.float32
        ).astype(jnp.bfloat16),
        "tensor",
        scatter_dimension=1,
        tiled=True,
    ).astype(jnp.float32)
    norm_two_back = jax.vjp(
        layer_norm, stream_two, norm2_gain.astype(jnp.float32), norm2_bias.astype(jnp.float32)
    )[1]
    grad_stream_two, norm2_gain_part, norm2_bias_part = norm_two_back(grad_normed_two)
    grad_two = grad_stream_two + grad_in.astype(jnp.float32)
    grad_two_low = grad_two.astype(jnp.bfloat16)
    attention_full = lax.all_gather(grad_two_low, "tensor", axis=1, tiled=True)
    out_grad = jnp.einsum(
        "rtc,rtd->cd", context, attention_full, preferred_element_type=jnp.float32
    )
    grad_context = jnp.einsum(
        "rtd,cd->rtc", attention_full, out_weight, preferred_element_type=jnp.float32
    ).astype(jnp.bfloat16)
    queries = projected_frames[..., :local_width]
    key_rows = projected_frames[..., local_width : 2 * local_width]
    value_rows = projected_frames[..., 2 * local_width :]
    grad_projected = attend_back(queries, key_rows, value_rows, row_mask, log_totals, grad_context)
    qkv_grad = jnp.einsum(
        "rtd,rte->de", full_one, grad_projected, preferred_element_type=jnp.float32
    ).reshape(model_width, 3, local_width)
    bias_sums = jnp.sum(grad_projected, axis=(0, 1), dtype=jnp.float32)
    qv_part = jnp.stack([bias_sums[:local_width], bias_sums[2 * local_width :]])
    grad_normed_one = lax.psum_scatter(
        jnp.einsum(
            "rte,de->rtd", grad_projected, proj_weight, preferred_element_type=jnp.float32
        ).astype(jnp.bfloat16),
        "tensor",
        scatter_dimension=1,
        tiled=True,
    ).astype(jnp.float32)
    norm_one_back = jax.vjp(
        layer_norm, stream_one, norm1_gain.astype(jnp.float32), norm1_bias.astype(jnp.float32)
    )[1]
    grad_stream_one, norm1_gain_part, norm1_bias_part = norm_one_back(grad_normed_one)
    grad_one = grad_two + grad_stream_one
    grad_position = lax.all_to_all(
        grad_one.astype(jnp.bfloat16), "tensor", split_axis=2, concat_axis=1, tiled=True
    )
    grad_conv = gelu_back(conv_pre, grad_position.astype(jnp.float32)).astype(jnp.bfloat16)
    pos_bias_part = jnp.sum(grad_conv, axis=(0, 1), dtype=jnp.float32)
    kernel = pos_weight.shape[0]
    group_width = pos_weight.shape[1]
    local_groups = local_width // group_width
    pos_grad = lax.conv_general_dilated(
        channels,
        grad_conv,
        (1,),
        [(kernel // 2, kernel // 2 - 1)],
        dimension_numbers=("CWN", "IWO", "WNC"),
        batch_group_count=local_groups,
        preferred_element_type=jnp.float32,
    )
    flipped = pos_weight[::-1].reshape(kernel, group_width, local_groups, group_width)
    flipped = flipped.transpose(0, 3, 2, 1).reshape(kernel, group_width, local_width)
    grad_channels = lax.conv_general_dilated(
        grad_conv,
        flipped,
        (1,),
        [(kernel // 2 - 1, kernel // 2)],
        dimension_numbers=("NWC", "WIO", "NWC"),
        feature_group_count=local_groups,
        preferred_element_type=jnp.float32,
    ).astype(jnp.bfloat16)
    grad_from_conv = lax.all_to_all(
        grad_channels, "tensor", split_axis=1, concat_axis=2, tiled=True
    )
    frames_grad = jnp.where(seg_mask[..., None], grad_one + grad_from_conv.astype(jnp.float32), 0.0)
    summed = (
        lax.psum_scatter(pos_grad, "dp", scatter_dimension=0, tiled=True),
        lax.psum_scatter(qkv_grad, "dp", scatter_dimension=0, tiled=True),
        lax.psum_scatter(out_grad, "dp", scatter_dimension=1, tiled=True),
        lax.psum_scatter(inner_grad, "dp", scatter_dimension=0, tiled=True),
        lax.psum_scatter(outer_grad, "dp", scatter_dimension=1, tiled=True),
    )
    inner_full = inner_bias.shape[0] * lax.axis_size("tensor")
    small = lax.psum(
        (
            spread(pos_bias_part, model_width),
            spread(qv_part, model_width),
            jnp.sum(grad_two_low, axis=(0, 1), dtype=jnp.float32),
            norm1_gain_part,
            norm1_bias_part,
            norm2_gain_part,
            norm2_bias_part,
            spread(inner_bias_part, inner_full),
            jnp.sum(grad_in, axis=(0, 1), dtype=jnp.float32),
        ),
        ("dp", "tensor"),
    )
    return (
        output,
        frames_grad,
        summed[0],
        small[0],
        summed[1],
        small[1],
        summed[2],
        small[2],
        small[3],
        small[4],
        small[5],
        small[6],
        summed[3],
        small[7],
        summed[4],
        small[8],
    )


def solution(mesh):
    placed = (
        P("dp", "tensor", None),
        P("dp"),
        P(None, None, "tensor"),
        P("tensor"),
        P(None, None, "tensor"),
        P(None, "tensor"),
        P("tensor", None),
        P(),
        P(),
        P(),
        P(),
        P(),
        P(None, "tensor"),
        P("tensor"),
        P("tensor", None),
        P(),
        P("dp", "tensor", None),
    )
    return jax.shard_map(
        shards,
        mesh=mesh,
        in_specs=placed,
        out_specs=(
            P("dp", "tensor", None),
            P("dp", "tensor", None),
            P("dp", None, "tensor"),
            P(),
            P("dp", None, "tensor"),
            P(),
            P("tensor", "dp"),
            P(),
            P(),
            P(),
            P(),
            P(),
            P("dp", "tensor"),
            P(),
            P("tensor", "dp"),
            P(),
        ),
        check_vma=False,
    )
```

profile of v0, /device:TPU:0, one launch (start us, length us, event | category | flops | bytes accessed | tf_op | source)
XLA Modules:
  0.0 1124.7 jit_solution(1431736932525307140)
XLA Ops:
  10.0 2.1 reduce.23
  12.9 4.3 all-to-all-start.2
  17.6 2.8 reduce.24
  20.4 1.7 reshape.1380
  23.2 3.4 all-to-all-start
  27.2 6.9 copy.175
  34.1 13.0 %copy.177 = bf16[128,64,4,64]{3,1,2,0:T(8,128)(2,1)} copy(bf16[128,64,4,64]{0,3,2,1:T(8,128)(2,1)} %bitcast.181) | data formatting | bytes 8388608 | tf_op jit(solution)/shard_map/shard_map
  48.1 1.8 reshape.1377
  49.9 1.8 reshape.1376
  51.8 74.6 %fusion.186 = f32[1,512,4,64]{3,0,2,1:T(1,128)} fusion(bf16[1,512,4,64]{3,0,2,1:T(2,128)(2,1)} %reshape.1376, bf16[128,64,4,64]{3,1,2,0:T(8,128)(2,1)} %copy.177), kind=kOutput, calls=%fused_computation.301 | convolution fusion | flops 2013265920 | bytes 4980736 | tf_op jit(solution)/shard_map/conv_general_dilated | solution.py:127
  126.4 85.8 %fusion.187 = f32[1,512,4,64]{3,0,2,1:T(1,128)} fusion(bf16[1,512,4,64]{3,0,2,1:T(2,128)(2,1)S(1)} %copy-done.29, bf16[128,64,4,64]{3,1,2,0:T(8,128)(2,1)S(1)} %copy-done.7), kind=kOutput, calls=%fused_computation.302 | convolution fusion | flops 2013265920 | bytes 4980736 | tf_op jit(solution)/shard_map/conv_general_dilated | solution.py:127
  212.2 2.3 copy.190
  214.5 2.5 copy.178
  217.0 3.2 fusion.105
  221.6 2.8 reduce.25
  224.5 1.7 reshape.1386
  226.2 3.4 all-to-all-start.3
  230.0 2.1 reduce.26
  232.9 2.6 all-to-all-done.3
  235.6 4.0 all-to-all-start.1
  241.4 4.3 all-to-all-done.1
  252.2 2.6 copy.181
  254.9 14.9 %all-gather.7.cloned.1.call-done = bf16[1,512,1024]{2,1,0:T(8,128)(2,1)} async-done(((bf16[1,128,1024]{2,1,0:T(8,128)(2,1)}), bf16[1,512,1024]{2,1,0:T(8,128)(2,1)}) %all-gather.7.cloned.1.call-update) | async-done | bytes 1048592 | tf_op jit(solution)/shard_map/all_gather | solution.py:142
  269.9 2.7 fusion.33
  273.4 1.8 copy.184
  276.2 4.6 fusion.185
  280.8 2.7 fusion.41
  285.2 3.6 all-gather.11.cloned.1.call-done
  288.8 2.7 fusion.34
  293.7 1.9 copy.193
  301.7 14.4 %reduce-scatter.11.cloned.1.call-done = bf16[1,128,1024]{2,1,0:T(8,128)(2,1)} async-done(((bf16[1,512,1024]{2,1,0:T(8,128)(2,1)}), bf16[1,128,1024]{2,1,0:T(8,128)(2,1)}) %reduce-scatter.11.cloned.1.call-update) | async-done | bytes 262160 | tf_op jit(solution)/shard_map/reduce_scatter | solution.py:157
  316.1 27.2 %reduce-scatter.15.cloned.1.call-done = bf16[1,128,1024]{2,1,0:T(8,128)(2,1)} async-done(((bf16[1,512,1024]{2,1,0:T(8,128)(2,1)}), bf16[1,128,1024]{2,1,0:T(8,128)(2,1)}) %reduce-scatter.15.cloned.1.call-update) | async-done | bytes 262160 | tf_op jit(solution)/shard_map/reduce_scatter | solution.py:157
  347.3 16.2 %all-gather.13.cloned.1.call-done = bf16[1,512,1024]{2,1,0:T(8,128)(2,1)} async-done(((bf16[1,128,1024]{2,1,0:T(8,128)(2,1)}), bf16[1,512,1024]{2,1,0:T(8,128)(2,1)}) %all-gather.13.cloned.1.call-update) | async-done | bytes 1048592 | tf_op jit(solution)/shard_map/all_gather | solution.py:164
  363.5 8.0 fusion.7
  371.5 10.1 all-gather.15.cloned.1.call-done
  381.7 5.1 convert_reduce_fusion
  387.8 2.3 fusion.32
  390.9 24.1 %reduce-scatter.17.cloned.1.call-done = bf16[1,128,1024]{2,1,0:T(8,128)(2,1)} async-done(((bf16[1,512,1024]{2,1,0:T(8,128)(2,1)}), bf16[1,128,1024]{2,1,0:T(8,128)(2,1)}) %reduce-scatter.17.cloned.1.call-update) | async-done | bytes 262160 | tf_op jit(solution)/shard_map/reduce_scatter | solution.py:260
  415.0 1.8 fusion.106
  420.6 13.2 %all-gather.9.cloned.1.call-done = bf16[1,512,1024]{2,1,0:T(8,128)(2,1)} async-done(((bf16[1,128,1024]{2,1,0:T(8,128)(2,1)}), bf16[1,512,1024]{2,1,0:T(8,128)(2,1)}) %all-gather.9.cloned.1.call-update) | async-done | bytes 1048592 | tf_op jit(solution)/shard_map/all_gather | solution.py:164
  433.9 9.2 fusion.30
  443.1 9.6 all-gather.17.cloned.1.call-done
  454.5 3.3 multiply_reduce_fusion
  462.0 2.0 fusion.28
  464.1 2.8 fusion.45
  467.4 5.3 fusion.42
  474.2 3.2 fusion.53
  478.2 62.7 %rev.3 = bf16[128,64,256]{0,2,1:T(8,128)(2,1)} reverse(bf16[128,64,256]{0,2,1:T(8,128)(2,1)} %copy.175), dimensions={0} | reverse | bytes 8388608 | tf_op jit(solution)/shard_map/rev | solution.py:320
  540.9 13.1 %copy.207 = bf16[128,64,4,64]{3,1,2,0:T(8,128)(2,1)} copy(bf16[128,64,4,64]{0,3,2,1:T(8,128)(2,1)} %bitcast.183) | data formatting | bytes 8388608 | tf_op jit(solution)/shard_map/reshape | solution.py:320
  556.1 1.8 add_convert_fusion.5
  558.0 1.8 convert_reduce_fusion.2
  559.8 1.9 fusion.107
  561.6 2.6 fusion.176
  564.7 2.1 reduce.27
  567.6 3.4 all-to-all-start.4
  571.0 3.9 fusion.43
  578.1 2.0 convert_reduce_fusion.6
  581.0 201.1 %fusion.188 = f32[128,64,4,64]{3,1,2,0:T(8,128)} fusion(bf16[1,512,4,64]{3,0,2,1:T(2,128)(2,1)S(1)} %copy-done.30, bf16[1,512,4,64]{3,0,2,1:T(2,128)(2,1)S(1)} %copy.206), kind=kOutput, calls=%fused_computation.303 | convolution fusion | flops 2013265920 | bytes 8912896 | tf_op jit(solution)/shard_map/conv_general_dilated | solution.py:311
  782.1 14.6 %copy.214 = f32[128,64,4,64]{0,3,2,1:T(8,128)} copy(f32[128,64,4,64]{3,1,2,0:T(8,128)} %fusion.188) | data formatting | bytes 16777216 | tf_op jit(solution)/shard_map/conv_general_dilated | solution.py:311
  796.6 9.3 copy.215
  805.9 258.8 %convolution_convert_fusion.5 = bf16[1,512,4,64]{3,0,2,1:T(2,128)(2,1)S(1)} fusion(bf16[1,512,4,64]{3,0,2,1:T(2,128)(2,1)S(1)} %copy.206, bf16[128,64,4,64]{3,1,2,0:T(8,128)(2,1)} %copy.207), kind=kOutput, calls=%fused_computation.70 | convolution fusion | flops 2013396992 | bytes 4718592 | tf_op jit(solution)/shard_map/conv_general_dilated | solution.py:322
  1066.5 2.1 reduce.28
  1069.5 3.5 all-to-all-start.5
  1073.4 42.4 %all-reduce = (f32[1024]{0:T(1024)}, f32[2,1024]{1,0:T(2,128)}, f32[1024]{0:T(1024)}, f32[1024]{0:T(1024)}, f32[1024]{0:T(1024)}, /*index=5*/f32[1024]{0:T(1024)}, f32[1024]{0:T(1024)}, f32[4096]{0:T(1024)}, f32[1024]{0:T(1024)}) all-reduce(f32[1024]{0:T(1024)S(1)} %dynamic_update_slice.20, ...), channel_id=1, replica_groups=mesh['dp'=8,'tensor'=4] {'dp','tensor'}, use_global_device_ids=true, to_apply=%region_24.25 | all-reduce | flops 13312 | bytes 106496 | tf_op jit(solution)/shard_map/psum | solution.py:343
  (252 shorter events, 58.3 us)
Async XLA Ops:
  7.2 356.3 %copy-start = (bf16[1024,1024]{1,0:T(8,128)(2,1)S(1)}, bf16[1024,1024]{1,0:T(8,128)(2,1)}, u32[]{:S(2)}) copy-start(bf16[1024,1024]{1,0:T(8,128)(2,1)} %param.29) | copy-start | bytes 6291460
  9.1 11.3 %copy-start.5 = (bf16[1,128,1024]{2,1,0:T(8,128)(2,1)}, bf16[1,128,1024]{2,1,0:T(8,128)(2,1)S(1)}, u32[]{:S(2)}) copy-start(bf16[1,128,1024]{2,1,0:T(8,128)(2,1)S(1)} %get-tuple-element.149) | copy-start | bytes 786436
  9.1 11.3 %copy-start.19 = (bf16[1,128,1024]{2,1,0:T(8,128)(2,1)}, bf16[1,128,1024]{2,1,0:T(8,128)(2,1)S(1)}, u32[]{:S(2)}) copy-start(bf16[1,128,1024]{2,1,0:T(8,128)(2,1)S(1)} %get-tuple-element.148) | copy-start | bytes 786436
  10.0 16.6 %copy-start.54 = (bf16[256]{0:T(256)(128)(2,1)S(1)}, bf16[256]{0:T(256)(128)(2,1)}, u32[]{:S(2)}) copy-start(bf16[256]{0:T(256)(128)(2,1)} %param.20) | copy-start | bytes 1540
  12.9 10.3 all-to-all-start.2
  23.2 24.4 %all-to-all-start = ((bf16[4,2,16384]{2,1,0:T(2,128)(2,1)}), bf16[4,2,16384]{2,1,0:T(2,128)(2,1)S(1)}, u32[]{:S(2)}, u32[]{:S(2)}) async-start(bf16[4,2,16384]{2,1,0:T(2,128)(2,1)} %reshape.1380), calls=%async_computation | async-start | bytes 524288 | tf_op jit(solution)/shard_map/all_to_all | solution.py:124
  51.7 74.6 %copy-start.7 = (bf16[128,64,4,64]{3,1,2,0:T(8,128)(2,1)S(1)}, bf16[128,64,4,64]{3,1,2,0:T(8,128)(2,1)}, u32[]{:S(2)}) copy-start(bf16[128,64,4,64]{3,1,2,0:T(8,128)(2,1)} %copy.177) | copy-start | bytes 12582916
  51.7 74.6 %copy-start.29 = (bf16[1,512,4,64]{3,0,2,1:T(2,128)(2,1)S(1)}, bf16[1,512,4,64]{3,0,2,1:T(2,128)(2,1)}, u32[]{:S(2)}) copy-start(bf16[1,512,4,64]{3,0,2,1:T(2,128)(2,1)} %reshape.1377) | copy-start | bytes 786436
  212.2 4.8 copy-start.53
  214.5 9.9 copy-start.10
  221.6 18.1 %copy-start.44 = (bf16[1024]{0:T(1024)(128)(2,1)S(1)}, bf16[1024]{0:T(1024)(128)(2,1)}, u32[]{:S(2)}) copy-start(bf16[1024]{0:T(1024)(128)(2,1)} %param.25) | copy-start | bytes 6148
  221.6 18.1 %copy-start.45 = (bf16[1024]{0:T(1024)(128)(2,1)S(1)}, bf16[1024]{0:T(1024)(128)(2,1)}, u32[]{:S(2)}) copy-start(bf16[1024]{0:T(1024)(128)(2,1)} %param.26) | copy-start | bytes 6148
  226.2 9.4 all-to-all-start.3
  235.6 10.1 all-to-all-start.1
  239.6 30.3 %all-gather.7.cloned.1.call-start = ((), (), s32[]{:S(2)}) async-start(), calls=%async_computation.16 | async-start | bytes 1310720 | tf_op jit(solution)/shard_map/all_gather | solution.py:142
  240.3 9.0 copy-start.6
  249.3 2.8 copy-start.4
  252.1 2.7 copy-start.43
  252.2 36.6 %all-gather.11.cloned.1.call-start = ((), (), s32[]{:S(2)}) async-start(), calls=%async_computation.20 | async-start | bytes 1310720 | tf_op jit(solution)/shard_map/all_gather | solution.py:142
  254.9 61.2 %reduce-scatter.11.cloned.1.call-start = ((), (), s32[]{:S(2)}) async-start(), calls=%async_computation.17 | async-start | bytes 1310720 | tf_op jit(solution)/shard_map/reduce_scatter | solution.py:157
  280.8 2.7 copy-start.22
  285.0 58.4 %reduce-scatter.15.cloned.1.call-start = ((), (), s32[]{:S(2)}) async-start(), calls=%async_computation.21 | async-start | bytes 1310720 | tf_op jit(solution)/shard_map/reduce_scatter | solution.py:157
  292.5 4.1 copy-start.15
  293.7 2.9 copy-start.17
  296.6 1.9 copy-start.2
  299.4 2.3 copy-start.46
  299.4 2.3 copy-start.47
  299.4 2.3 copy-start.48
  301.6 61.9 %all-gather.13.cloned.1.call-start = ((), (), s32[]{:S(2)}) async-start(), calls=%async_computation.22 | async-start | bytes 1310720 | tf_op jit(solution)/shard_map/all_gather | solution.py:164
  344.8 2.5 copy-start.49
  346.7 35.0 %all-gather.15.cloned.1.call-start = ((), (), s32[]{:S(2)}) async-start(), calls=%async_computation.23 | async-start | bytes 1310720 | tf_op jit(solution)/shard_map/all_gather | solution.py:252
  347.2 67.8 %reduce-scatter.17.cloned.1.call-start = ((), (), s32[]{:S(2)}) async-start(), calls=%async_computation.24 | async-start | bytes 1310720 | tf_op jit(solution)/shard_map/reduce_scatter | solution.py:260
  390.0 28.9 %copy-start.20 = (bf16[1,128,1024]{2,1,0:T(8,128)(2,1)S(1)}, bf16[1,128,1024]{2,1,0:T(8,128)(2,1)}, u32[]{:S(2)}) copy-start(bf16[1,128,1024]{2,1,0:T(8,128)(2,1)} %param.33) | copy-start | bytes 786436
  390.1 43.8 %all-gather.9.cloned.1.call-start = ((), (), s32[]{:S(2)}) async-start(), calls=%async_computation.18 | async-start | bytes 1310720 | tf_op jit(solution)/shard_map/all_gather | solution.py:164
  390.8 61.9 %all-gather.17.cloned.1.call-start = ((), (), s32[]{:S(2)}) async-start(), calls=%async_computation.25 | async-start | bytes 1310720 | tf_op jit(solution)/shard_map/all_gather | solution.py:274
  420.4 32.4 %copy-start.24 = (bf16[256,1024]{1,0:T(8,128)(2,1)S(1)}, bf16[256,1024]{1,0:T(8,128)(2,1)}, u32[]{:S(2)}) copy-start(bf16[256,1024]{1,0:T(8,128)(2,1)} %param.23) | copy-start | bytes 1572868
  420.4 135.7 %reduce-scatter.13.cloned.1.call-start = ((), (), s32[]{:S(2)}) async-start(), calls=%async_computation.19 | async-start | bytes 1310720 | tf_op jit(solution)/shard_map/reduce_scatter | solution.py:172
  443.1 11.4 %copy-start.32 = (bf16[1,512,256]{1,2,0:T(8,128)(2,1)S(1)}, bf16[1,512,256]{1,2,0:T(8,128)(2,1)}, u32[]{:S(2)}) copy-start(bf16[1,512,256]{1,2,0:T(8,128)(2,1)} %copy.193) | copy-start | bytes 786436
  443.1 114.9 %reduce-scatter.19.cloned.1.call-start = ((), (), s32[]{:S(2)}) async-start(), calls=%async_computation.26 | async-start | bytes 1310720 | tf_op jit(solution)/shard_map/reduce_scatter | solution.py:290
  454.5 3.5 copy-start.3
  464.0 3.4 copy-start.14
  464.0 653.1 %reduce-scatter.25.cloned.1.call-start = ((), (), s32[]{:S(2)}) async-start(), calls=%async_computation.29 | async-start | bytes 1179648 | tf_op jit(solution)/shard_map/reduce_scatter | solution.py:338
  466.9 650.2 %reduce-scatter.29.cloned.1.call-start = ((), (), s32[]{:S(2)}) async-start(), calls=%async_computation.31 | async-start | bytes 4718592 | tf_op jit(solution)/shard_map/reduce_scatter | solution.py:340
  472.7 644.5 %reduce-scatter.27.cloned.1.call-start = ((), (), s32[]{:S(2)}) async-start(), calls=%async_computation.30 | async-start | bytes 4718592 | tf_op jit(solution)/shard_map/reduce_scatter | solution.py:339
  478.2 62.7 %copy-start.50 = (bf16[1024]{0:T(1024)(128)(2,1)S(1)}, bf16[1024]{0:T(1024)(128)(2,1)}, u32[]{:S(2)}) copy-start(bf16[1024]{0:T(1024)(128)(2,1)} %param.32) | copy-start | bytes 6148
  540.9 15.2 %copy-start.9 = (f32[1,128,1024]{2,1,0:T(8,128)S(1)}, f32[1,128,1024]{2,1,0:T(8,128)}, u32[]{:S(2)}) copy-start(f32[1,128,1024]{2,1,0:T(8,128)} %copy-done.8) | copy-start | bytes 1572868
  556.1 5.6 copy-start.13
  556.1 5.6 copy-start.21
  567.6 9.4 all-to-all-start.4
  571.0 546.2 %reduce-scatter.23.cloned.1.call-start = ((), (), s32[]{:S(2)}) async-start(), calls=%async_computation.28 | async-start | bytes 3538944 | tf_op jit(solution)/shard_map/reduce_scatter | solution.py:337
  575.0 3.2 copy-start.11
  575.0 542.2 %reduce-scatter.21.cloned.1.call-start = ((), (), s32[]{:S(2)}) async-start(), calls=%async_computation.27 | async-start | bytes 9437184 | tf_op jit(solution)/shard_map/reduce_scatter | solution.py:336
  577.8 3.2 copy-start.30
  1064.7 8.3 copy-start.41
  1064.8 8.3 copy-start.42
  1064.8 8.6 copy-start.35
  1064.8 8.6 copy-start.36
  1064.8 8.6 copy-start.37
  1064.8 8.6 copy-start.38
  1064.8 8.6 copy-start.39
  1064.8 8.6 copy-start.40
  1069.5 46.8 %copy-start.25 = (f32[1,128,1024]{2,1,0:T(8,128)S(1)}, f32[1,128,1024]{2,1,0:T(8,128)}, u32[]{:S(2)}) copy-start(f32[1,128,1024]{2,1,0:T(8,128)} %get-tuple-element.122) | copy-start | bytes 1572868
  1069.5 46.8 %copy-start.52 = (pred[128]{0:T(512)(128)(4,1)S(1)}, pred[128]{0:T(512)(128)(4,1)}, u32[]{:S(2)}) copy-start(pred[128]{0:T(512)(128)(4,1)} %copy-done.51) | copy-start | bytes 388
  1069.5 46.3 %all-to-all-start.5 = ((bf16[4,2,16384]{2,1,0:T(2,128)(2,1)}), bf16[4,2,16384]{2,1,0:T(2,128)(2,1)S(1)}, u32[]{:S(2)}, u32[]{:S(2)}) async-start(bf16[4,2,16384]{2,1,0:T(2,128)(2,1)} %reshape.1390), calls=%async_computation.10 | async-start | bytes 524288 | tf_op jit(solution)/shard_map/all_to_all | solution.py:331
  (14 other events, 16.7 us)
Sparse Core Ops, SparseCore 0:
  252.3 17.5 all-gather.6
  272.0 16.6 all-gather.10
  291.3 24.8 reduce-scatter.10
  318.5 24.7 reduce-scatter.14
  346.8 16.6 all-gather.12
  364.9 16.6 all-gather.14
  390.2 24.7 reduce-scatter.16
  417.1 16.6 all-gather.8
  436.0 16.6 all-gather.16
  455.1 24.8 reduce-scatter.12
  482.6 24.7 reduce-scatter.18
  511.2 64.7 reduce-scatter.24
  580.2 87.6 reduce-scatter.28
  671.9 87.9 reduce-scatter.26
  764.0 74.2 reduce-scatter.22
  842.4 146.6 reduce-scatter.20
where the time goes:
time: 1140 us; the launch traced here: 1120 us
  matrix products  687 us (60%)
  local copies, waits for them, and re-layouts  168 us (15%)
  waiting for transfers between devices  144 us (13%)
  other arithmetic  43.6 us (4%)
  blocking collectives  42.4 us (4%)
  starting transfers between devices  23.5 us (2%)
  between operations  16.2 us (1%)
    conv_general_dilated x1, matrix products, shards(): lax.conv_general_dilated(grad_conv, flipped, (1,), [(kernel // 2 - 1, ker...  259 us
    conv_general_dilated x1, matrix products, shards(): lax.conv_general_dilated(channels, grad_conv, (1,), [(kernel // 2, kernel...  201 us
    conv_general_dilated x2, matrix products, forward_pass(): lax.conv_general_dilated(channels, pos_weight, (1,), [(kernel // 2, kerne...  160 us
    rev x1, local copies, waits for them, and re-layouts, shards(): pos_weight[::-1].reshape(kernel, group_width, local_groups, group_width)  62.7 us
    psum x1, blocking collectives, shards(): lax.psum((spread(pos_bias_part, model_width), spread(qv_part, model_width...  42.4 us
    reduce_scatter x2, waiting for transfers between devices, forward_pass(): lax.psum_scatter(partial_one.astype(jnp.bfloat16), 'tensor', scatter_dime...  41.6 us
    all_gather x2, waiting for transfers between devices, forward_pass(): full_two = lax.all_gather(normed_two, 'tensor', axis=1, tiled=True)  29.4 us
    unnamed x129, local copies, waits for them, and re-layouts  27.2 us
  transfers between devices with their start and end apart: 22, of which 13 were waited for; matrix products, arithmetic and copies ran while one was open for 61% of the time, Pallas kernels for 0%

commit v1 on v0

v1 whole, which is shorter than its diff:
```python
import functools

import jax
import jax.numpy as jnp
from jax import lax
from jax.experimental import pallas as pl
from jax.experimental.pallas import tpu as pltpu
from jax.sharding import PartitionSpec as P

HEAD = 64
EPSILON = 1e-05
NEGATIVE = -1e30
F32 = jnp.float32
BF16 = jnp.bfloat16
PHASES = 4
PAD = 16
VMEM_LIMIT = 67043328


def nn(a, b):
    return lax.dot_general(a, b, (((1,), (0,)), ((), ())), preferred_element_type=F32)


def nt(a, b):
    return lax.dot_general(a, b, (((1,), (1,)), ((), ())), preferred_element_type=F32)


def tn(a, b):
    return lax.dot_general(a, b, (((0,), (0,)), ((), ())), preferred_element_type=F32)


def aligned(start, size, unit):
    return pl.ds(pl.multiple_of(start, unit), size)


def gelu_pair(x):
    cdf = 0.5 + 0.5 * lax.erf(x * 0.7071067811865476)
    return x * cdf, cdf + x * (0.3989422804014327 * jnp.exp(-0.5 * x * x))


def norm_stats(x):
    centered = x - jnp.mean(x, axis=-1, keepdims=True)
    scale = lax.rsqrt(jnp.mean(centered * centered, axis=-1, keepdims=True) + EPSILON)
    return centered * scale, scale


def low_half(rows):
    return lax.broadcasted_iota(jnp.int32, (rows, 128), 1) < HEAD


def swap_halves(x):
    return pltpu.roll(x, HEAD, 1)


def split_phases(flat):
    steps = flat.shape[1] // PHASES
    low = low_half(steps)
    rows = [[flat[v, pl.ds(q, steps, stride=PHASES), :] for v in range(2)] for q in range(PHASES)]
    groups = []
    for g in range(4):
        v, h = g // 2, g % 2

        def piece(q, half):
            return rows[q][v] if h == half else swap_halves(rows[q][v])

        groups.append((jnp.where(low, piece(0, 0), piece(1, 1)), jnp.where(low, piece(2, 0), piece(3, 1))))
    return groups


def join_phases(groups, flat):
    steps = flat.shape[1] // PHASES
    low = low_half(steps)
    for v in range(2):
        for s in range(PHASES):
            first, second = groups[2 * v][s // 2], groups[2 * v + 1][s // 2]
            first = first if s % 2 == 0 else swap_halves(first)
            second = second if s % 2 == 1 else swap_halves(second)
            flat[v, pl.ds(s, steps, stride=PHASES), :] = jnp.where(low, first, second)


def tap_tile(taps, swapped, g, block):
    v, h = g // 2, g % 2
    columns = slice(v * 128, (v + 1) * 128)
    low = low_half(256)

    def source(half, s):
        ref = taps if h == half else swapped
        return ref[aligned((PHASES * block - s + 3) * HEAD, 256, HEAD), columns]

    return jnp.concatenate(
        [jnp.where(low, source(0, 0), source(1, 1)), jnp.where(low, source(0, 2), source(1, 3))], axis=1
    )


def shift_copies(padded, shifts, rows):
    for g in range(4):
        for v in range(2):

            def one(b, carry):
                shifts[b, g, :, v * 128 : (v + 1) * 128] = padded[g, v, pl.ds(b, rows), :].astype(BF16)
                return carry

            lax.fori_loop(0, PAD, one, 0)


def store_padded(groups, padded):
    steps = groups[0][0].shape[0]
    for g in range(4):
        for v in range(2):
            padded[g, v, pl.ds(PAD, steps), :] = groups[g][v]


def layer_kernel(sizes, *refs):
    slots, seg, width, local, hid, taps_n = sizes
    (
        len_ref,
        frames_in,
        cot_in,
        taps_in,
        qkv_in,
        out_in,
        inner_in,
        outer_in,
        vec,
        output_o,
        frames_grad_o,
        small_o,
        gouter_o,
        ginner_o,
        gout_o,
        gqkv_o,
        x4_o,
        gc4_o,
        xflat_o,
        gcflat_o,
        taps,
        swapped,
        w_qkv,
        w_out,
        w_inner,
        w_outer,
        frames_v,
        cot_full,
        x_raw,
        flat,
        padded,
        shifts,
        gelu_grad,
        pos_send,
        pos_recv,
        s1,
        full1,
        proj,
        probs,
        ctx,
        keep,
        rs_send,
        rs_core,
        rs_mid,
        rs_y,
        rf_send,
        rf_core,
        rf_mid,
        rf_y,
        s2,
        full2,
        hidden,
        grad_in,
        full3,
        gctx,
        gproj,
        gscore,
        grad_one,
        ga_send,
        ga_recv,
        gx_send,
        gx_recv,
        small,
        stage,
        send_sem,
        recv_sem,
        local_sem,
    ) = refs
    me = lax.axis_index("tensor")
    core = lax.rem(me, 2)
    mate = me + 1 - 2 * core
    across = lax.rem(me + 2, 4)
    diag = lax.rem(mate + 2, 4)
    peers = (mate, across, diag)
    counter = {"remote": 0, "local": 0}
    pending = []

    def rows_of(owner):
        return aligned(owner * seg, seg, seg)

    def columns_of(owner):
        return aligned(owner * local, local, local)

    def send(src, dst, peer):
        index = counter["remote"]
        counter["remote"] += 1
        copy = pltpu.make_async_remote_copy(
            src_ref=src,
            dst_ref=dst,
            send_sem=send_sem.at[index],
            recv_sem=recv_sem.at[index],
            device_id={"tensor": peer},
            device_id_type=pl.DeviceIdType.MESH,
        )
        copy.start()
        pending.append(copy)
        return index

    def arrive(index, region):
        pltpu.make_async_remote_copy(
            src_ref=region,
            dst_ref=region,
            send_sem=send_sem.at[index],
            recv_sem=recv_sem.at[index],
            device_id={"tensor": mate},
            device_id_type=pl.DeviceIdType.MESH,
        ).wait_recv()

    def fetch(src, dst):
        index = counter["local"]
        counter["local"] += 1
        copy = pltpu.make_async_copy(src, dst, local_sem.at[index])
        copy.start()
        return copy

    c_frames = fetch(frames_in, frames_v)
    c_own = fetch(frames_in.at[:, columns_of(me)], x_raw.at[rows_of(me), :])
    c_taps = fetch(taps_in, taps.at[pl.ds(3 * HEAD, taps_n * HEAD), :])
    c_cot = fetch(cot_in, cot_full.at[rows_of(me), :])
    c_qkv = fetch(qkv_in, w_qkv)
    c_out = fetch(out_in, w_out)
    c_inner = fetch(inner_in, w_inner)
    c_outer = fetch(outer_in, w_outer)

    barrier = pltpu.get_barrier_semaphore()
    for peer in peers:
        pl.semaphore_signal(barrier, inc=1, device_id={"tensor": peer}, device_id_type=pl.DeviceIdType.MESH)
    pl.semaphore_wait(barrier, 3)

    i_frames = [send(frames_in.at[:, columns_of(p)], x_raw.at[rows_of(me), :], p) for p in peers]
    i_cot = [send(cot_in, cot_full.at[rows_of(me), :], p) for p in (mate, across)]

    taps[pl.ds(0, 3 * HEAD), :] = jnp.zeros((3 * HEAD, local), BF16)
    taps[pl.ds((3 + taps_n) * HEAD, 4 * HEAD), :] = jnp.zeros((4 * HEAD, local), BF16)
    for g in range(4):
        for v in range(2):
            padded[g, v, pl.ds(0, PAD), :] = jnp.zeros((PAD, 128), F32)
            padded[g, v, pl.ds(PAD + slots // PHASES, 2 * PAD), :] = jnp.zeros((2 * PAD, 128), F32)
    c_taps.wait()

    def swap_rows(b, carry):
        part = taps[aligned(b * HEAD * 9, HEAD * 9, HEAD), :]
        swapped[aligned(b * HEAD * 9, HEAD * 9, HEAD), :] = jnp.concatenate(
            [swap_halves(part[:, :128]), swap_halves(part[:, 128:])], axis=1
        )
        return carry

    lax.fori_loop(0, (taps_n + 7) // 9, swap_rows, 0)

    length = len_ref[0]
    c_own.wait()
    for index, p in zip(i_frames, peers):
        arrive(index, x_raw.at[rows_of(p), :])

    live_all = lax.broadcasted_iota(jnp.int32, (slots, 128), 0) < length
    for v in range(2):
        flat[v] = jnp.where(live_all, x_raw[:, v * 128 : (v + 1) * 128].astype(F32), 0.0)
    store_padded(split_phases(flat), padded)
    steps = slots // PHASES
    shift_copies(padded, shifts, steps + 2 * PAD)
    for g in range(4):
        x4_o[g] = shifts[0, g, pl.ds(PAD, steps), :]
    xflat_o[...] = jnp.concatenate([flat[0], flat[1]], axis=1).astype(BF16)

    blocks = taps_n // PHASES

    def shifted(g, low_part, high_part):
        return shifts[low_part, g, pl.ds(high_part * PAD, steps), :]

    pos_groups = []
    for g in range(4):

        def forward(b, total):
            for high in range(2):
                total = total + nn(shifted(g, b, high), tap_tile(taps, swapped, g, b + PAD * high))
            return total

        total = nn(shifted(g, 0, 2), tap_tile(taps, swapped, g, blocks))
        total = lax.fori_loop(0, PAD, forward, total)
        value, slope = gelu_pair(total + vec[pl.ds(8, 1), g * 256 : (g + 1) * 256])
        gelu_grad[g] = slope
        pos_groups.append((value[:, :128], value[:, 128:]))
    join_phases(pos_groups, flat)
    pos_send[...] = jnp.concatenate([flat[0], flat[1]], axis=1).astype(BF16)
    i_pos = [send(pos_send.at[rows_of(p), :], pos_recv.at[:, columns_of(me)], p) for p in peers]
    arrive(i_cot[1], cot_full.at[rows_of(across), :])
    i_cot.append(send(cot_full.at[rows_of(across), :], cot_full.at[rows_of(across), :], mate))
    pos_recv[:, columns_of(me)] = pos_send[rows_of(me), :]
    for index, p in zip(i_pos, peers):
        arrive(index, pos_recv.at[:, columns_of(p)])

    chunk = 32
    c_frames.wait()
    seg_start = me * seg

    def live_rows(b):
        return seg_start + b * chunk + lax.broadcasted_iota(jnp.int32, (chunk, 1), 0) < length

    def norm_one(b, carry):
        rows = aligned(b * chunk, chunk, chunk)
        x = jnp.where(live_rows(b), frames_v[rows, :].astype(F32), 0.0) + pos_recv[rows, :].astype(F32)
        s1[rows, :] = x
        unit, _ = norm_stats(x)
        full1[aligned(seg_start + b * chunk, chunk, chunk), :] = (unit * vec[pl.ds(1, 1), :] + vec[pl.ds(2, 1), :]).astype(BF16)
        return carry

    lax.fori_loop(0, seg // chunk, norm_one, 0)

    def gather_start(full):
        return [send(full.at[rows_of(me), :], full.at[rows_of(me), :], p) for p in (mate, across)]

    def gather_relay(ids, full):
        arrive(ids[1], full.at[rows_of(across), :])
        ids.append(send(full.at[rows_of(across), :], full.at[rows_of(across), :], mate))

    pair = aligned((me - core) * seg, 2 * seg, 2 * seg)
    far_pair = aligned(lax.rem(me - core + 2, 4) * seg, 2 * seg, 2 * seg)

    ids1 = gather_start(full1)
    c_qkv.wait()

    def project(rows):
        for part in range(3):
            columns = slice(part * local, (part + 1) * local)
            proj[rows, columns] = (nn(full1[rows, :], w_qkv[:, columns]) + vec[pl.ds(7, 1), columns]).astype(BF16)

    arrive(ids1[0], full1.at[rows_of(mate), :])
    project(pair)
    gather_relay(ids1, full1)
    arrive(ids1[2], full1.at[rows_of(diag), :])
    project(far_pair)

    block = 128
    scale = HEAD**-0.5
    live_keys = lax.broadcasted_iota(jnp.int32, (1, slots), 1) < length

    def head_columns(part, head):
        return slice(part * local + head * HEAD, part * local + (head + 1) * HEAD)

    for hp in range(2):

        def attend(b, carry):
            rows = aligned(b * block, block, block)
            outs = []
            for head in (2 * hp, 2 * hp + 1):
                scores = nt(proj[rows, head_columns(0, head)], proj[:, head_columns(1, head)]) * scale
                scores = jnp.where(live_keys, scores, NEGATIVE)
                weights = jnp.exp(scores - jnp.max(scores, axis=-1, keepdims=True))
                low = (weights * (1.0 / jnp.sum(weights, axis=-1, keepdims=True))).astype(BF16)
                probs[head, rows, :] = low
                outs.append(nn(low, proj[:, head_columns(2, head)]))
            ctx[rows, hp * 128 : (hp + 1) * 128] = jnp.concatenate(outs, axis=1).astype(BF16)
            return carry

        lax.fori_loop(0, slots // block, attend, 0)

    def scatter_start(partial, bufs):
        send_buf, core_buf = bufs[0], bufs[1]
        send_buf[1] = partial(diag).astype(BF16)
        first = send(send_buf.at[1], core_buf.at[1], mate)
        send_buf[0] = partial(mate).astype(BF16)
        return [first, send(send_buf.at[0], core_buf.at[0], mate)]

    def scatter_mid(ids, partial, bufs):
        _, core_buf, mid_buf, y_buf = bufs
        value = partial(across)
        arrive(ids[0], core_buf.at[1])
        mid_buf[...] = (value + core_buf[1].astype(F32)).astype(BF16)
        ids.append(send(mid_buf, y_buf, across))

    def scatter_own(ids, partial, bufs):
        keep[...] = partial(me)
        arrive(ids[1], bufs[1].at[0])
        arrive(ids[2], bufs[3])

    main_bufs = (rs_send, rs_core, rs_mid, rs_y)
    ff_bufs = (rf_send, rf_core, rf_mid, rf_y)
    c_out.wait()

    def attended(owner):
        return nn(ctx[rows_of(owner), :], w_out[...])

    ids = scatter_start(attended, main_bufs)
    scatter_mid(ids, attended, main_bufs)
    scatter_own(ids, attended, main_bufs)
    sends_rs = pending[-3:]

    def norm_two(b, carry):
        rows = aligned(b * chunk, chunk, chunk)
        total = keep[rows, :] + rs_core[0, rows, :].astype(F32) + rs_y[rows, :].astype(F32)
        x = s1[rows, :] + total + vec[pl.ds(0, 1), :]
        s2[rows, :] = x
        unit, _ = norm_stats(x)
        full2[aligned(seg_start + b * chunk, chunk, chunk), :] = (unit * vec[pl.ds(3, 1), :] + vec[pl.ds(4, 1), :]).astype(BF16)
        return carry

    lax.fori_loop(0, seg // chunk, norm_two, 0)

    ids2 = gather_start(full2)
    c_inner.wait()
    c_outer.wait()
    c_cot.wait()
    arrive(i_cot[0], cot_full.at[rows_of(mate), :])
    arrive(i_cot[2], cot_full.at[rows_of(diag), :])

    def feed(rows):
        def tile(b, carry):
            columns = aligned(b * 256, 256, 256)
            pre = nn(full2[rows, :], w_inner[:, columns]) + vec[pl.ds(6, 1), columns]
            value, slope = gelu_pair(pre)
            hidden[rows, columns] = value.astype(BF16)
            grad_in[rows, columns] = (nt(cot_full[rows, :], w_outer[columns, :]) * slope).astype(BF16)
            return carry

        lax.fori_loop(0, hid // 256, tile, 0)

    arrive(ids2[0], full2.at[rows_of(mate), :])
    feed(pair)
    gather_relay(ids2, full2)
    arrive(ids2[2], full2.at[rows_of(diag), :])
    feed(far_pair)

    def wide(make, buf_rows):
        def tile(b, carry):
            columns = aligned(b * 256, 256, 256)
            stage[:, columns] = make(columns)
            return carry

        lax.fori_loop(0, width // 256, tile, 0)
        return stage[...]

    def grad_two_part(owner):
        return wide(lambda columns: nt(grad_in[rows_of(owner), :], w_inner[columns, :]), None)

    def branch_part(owner):
        return wide(lambda columns: nn(hidden[rows_of(owner), :], w_outer[:, columns]), None)

    for copy in sends_rs:
        copy.wait_send()
    ids = scatter_start(grad_two_part, main_bufs)
    scatter_mid(ids, grad_two_part, main_bufs)
    sends_rs2 = pending[-3:]
    keep2 = frames_v
    scatter_own(ids, grad_two_part, main_bufs)

    def put_sum(row, value):
        small[pl.ds(row, 1), :] = small[pl.ds(row, 1), :] + jnp.sum(value, axis=0, keepdims=True)

    small[...] = jnp.zeros_like(small)

    def back_two(b, carry):
        rows = aligned(b * chunk, chunk, chunk)
        grad = keep[rows, :] + rs_core[0, rows, :].astype(F32) + rs_y[rows, :].astype(F32)
        unit, inv = norm_stats(s2[rows, :])
        put_sum(3, grad * unit)
        put_sum(4, grad)
        w = grad * vec[pl.ds(3, 1), :]
        own = aligned(seg_start + b * chunk, chunk, chunk)
        cot = cot_full[own, :].astype(F32)
        put_sum(5, cot)
        grad_two = cot + inv * (w - jnp.mean(w, axis=-1, keepdims=True) - unit * jnp.mean(w * unit, axis=-1, keepdims=True))
        grad_one[rows, :] = grad_two
        low = grad_two.astype(BF16)
        full3[own, :] = low
        put_sum(0, low.astype(F32))
        return carry

    lax.fori_loop(0, seg // chunk, back_two, 0)
    ids3 = gather_start(full3)

    idf = scatter_start(branch_part, ff_bufs)
    gather_relay(ids3, full3)
    scatter_mid(idf, branch_part, ff_bufs)

    arrive(ids3[0], full3.at[rows_of(mate), :])
    arrive(ids3[2], full3.at[rows_of(diag), :])
    gctx[...] = nt(full3[...], w_out[...]).astype(BF16)

    for hp in range(2):
        columns = slice(hp * 128, (hp + 1) * 128)

        def back_scores(b, carry):
            rows = aligned(b * block, block, block)
            outs = []
            for j, head in enumerate((2 * hp, 2 * hp + 1)):
                p = probs[head, rows, :].astype(F32)
                gp = nt(gctx[rows, head_columns(0, head)], proj[:, head_columns(2, head)])
                gs = (p * (gp - jnp.sum(p * gp, axis=-1, keepdims=True))).astype(BF16)
                gscore[j, rows, :] = gs
                outs.append(nn(gs, proj[:, head_columns(1, head)]))
            gproj[rows, hp * 128 : (hp + 1) * 128] = (jnp.concatenate(outs, axis=1) * scale).astype(BF16)
            return carry

        lax.fori_loop(0, slots // block, back_scores, 0)
        gk = [tn(gscore[j], proj[:, head_columns(0, 2 * hp + j)]) for j in range(2)]
        gproj[:, local + hp * 128 : local + (hp + 1) * 128] = (jnp.concatenate(gk, axis=1) * scale).astype(BF16)
        gv = [tn(probs[2 * hp + j], gctx[:, head_columns(0, 2 * hp + j)]) for j in range(2)]
        gproj[:, 2 * local + hp * 128 : 2 * local + (hp + 1) * 128] = jnp.concatenate(gv, axis=1).astype(BF16)

    def grad_one_part(owner):
        return wide(lambda columns: nt(gproj[rows_of(owner), :], w_qkv[columns, :]), None)

    for copy in sends_rs2:
        copy.wait_send()
    ids = scatter_start(grad_one_part, main_bufs)
    scatter_mid(ids, grad_one_part, main_bufs)
    scatter_own(ids, grad_one_part, main_bufs)

    def back_one(b, carry):
        rows = aligned(b * chunk, chunk, chunk)
        grad = keep[rows, :] + rs_core[0, rows, :].astype(F32) + rs_y[rows, :].astype(F32)
        unit, inv = norm_stats(s1[rows, :])
        put_sum(1, grad * unit)
        put_sum(2, grad)
        w = grad * vec[pl.ds(1, 1), :]
        total = grad_one[rows, :] + inv * (w - jnp.mean(w, axis=-1, keepdims=True) - unit * jnp.mean(w * unit, axis=-1, keepdims=True))
        grad_one[rows, :] = total
        ga_send[rows, :] = total.astype(BF16)
        return carry

    lax.fori_loop(0, seg // chunk, back_one, 0)
    i_ga = [send(ga_send.at[:, columns_of(p)], ga_recv.at[rows_of(me), :], p) for p in peers]
    ga_recv[rows_of(me), :] = ga_send[:, columns_of(me)]

    keep[...] = branch_part(me)
    arrive(idf[1], rf_core.at[0])
    arrive(idf[2], rf_y)

    def finish(b, carry):
        rows = aligned(b * chunk, chunk, chunk)
        total = keep[rows, :] + rf_core[0, rows, :].astype(F32) + rf_y[rows, :].astype(F32)
        output_o[rows, :] = (s2[rows, :] + total + vec[pl.ds(5, 1), :]).astype(BF16)
        return carry

    lax.fori_loop(0, seg // chunk, finish, 0)

    for index, p in zip(i_ga, peers):
        arrive(index, ga_recv.at[rows_of(p), :])
    for v in range(2):
        flat[v] = ga_recv[:, v * 128 : (v + 1) * 128].astype(F32)
    grads = []
    for g, (lo, hi) in enumerate(split_phases(flat)):
        both = [
            (part * gelu_grad[g, :, v * 128 : (v + 1) * 128]).astype(BF16).astype(F32) for v, part in enumerate((lo, hi))
        ]
        grads.append(tuple(both))
        for v in range(2):
            small[pl.ds(6, 1), g * 256 + v * 128 : g * 256 + (v + 1) * 128] = jnp.sum(both[v], axis=0, keepdims=True)
    store_padded(grads, padded)
    join_phases(grads, flat)
    gcflat_o[...] = jnp.concatenate([flat[0], flat[1]], axis=1).astype(BF16)
    shift_copies(padded, shifts, steps + 2 * PAD)
    for g in range(4):
        gc4_o[g] = shifts[0, g, pl.ds(PAD, steps), :]
    in_groups = []
    for g in range(4):

        def backward(b, total):
            for high in range(2):
                total = total + nt(shifted(g, b, high), tap_tile(taps, swapped, g, blocks - (b + PAD * high)))
            return total

        total = nt(shifted(g, 0, 2), tap_tile(taps, swapped, g, 0))
        total = lax.fori_loop(0, PAD, backward, total)
        in_groups.append((total[:, :128], total[:, 128:]))
    join_phases(in_groups, flat)
    gx_send[...] = jnp.concatenate([flat[0], flat[1]], axis=1).astype(BF16)
    i_gx = [send(gx_send.at[rows_of(p), :], gx_recv.at[:, columns_of(me)], p) for p in peers]
    gx_recv[:, columns_of(me)] = gx_send[rows_of(me), :]

    def rows_loop(count, body):
        def tile(b, carry):
            body(aligned(b * 256, 256, 256))
            return carry

        lax.fori_loop(0, count // 256, tile, 0)

    def outer_tile(rows):
        gouter_o[rows, :] = tn(hidden[:, rows], cot_full[...]).astype(BF16)

    rows_loop(hid, outer_tile)

    def inner_tile(rows):
        ginner_o[rows, :] = tn(full2[:, rows], grad_in[...]).astype(BF16)

    rows_loop(width, inner_tile)
    gout_o[...] = tn(ctx[...], full3[...]).astype(BF16)

    def qkv_tile(rows):
        gqkv_o[rows, :] = tn(full1[:, rows], gproj[...]).astype(BF16)

    rows_loop(width, qkv_tile)

    ones = jnp.ones((8, slots), BF16)
    sums = nn(ones, gproj[...])
    small[pl.ds(7, 1), 0:local] = sums[0:1, 0:local]
    small[pl.ds(7, 1), local : 2 * local] = sums[0:1, 2 * local :]
    small[pl.ds(8, 1), :] = nn(ones, grad_in[...])[0:1, :]

    for index, p in zip(i_gx, peers):
        arrive(index, gx_recv.at[:, columns_of(p)])

    def frames_back(b, carry):
        rows = aligned(b * chunk, chunk, chunk)
        frames_grad_o[rows, :] = jnp.where(live_rows(b), grad_one[rows, :] + gx_recv[rows, :].astype(F32), 0.0)
        return carry

    lax.fori_loop(0, seg // chunk, frames_back, 0)
    small_o[...] = small[...]
    done = [id(copy) for copy in sends_rs + sends_rs2]
    for copy in pending:
        if id(copy) not in done:
            copy.wait_send()


def run_layer(lengths, frames, cot, taps, qkv, out_w, inner_w, outer_w, vec):
    seg, width = frames.shape
    slots = seg * 4
    local = taps.shape[1]
    hid = inner_w.shape[1]
    taps_n = taps.shape[0] // HEAD
    steps = slots // PHASES
    any_spec = pl.BlockSpec(memory_space=pl.ANY)
    vmem = pl.BlockSpec(memory_space=pltpu.VMEM)
    sds = jax.ShapeDtypeStruct
    rs = [((2, seg, width), BF16), ((2, seg, width), BF16), ((seg, width), BF16), ((seg, width), BF16)]
    scratch = [
        (((taps_n + 7) * HEAD, local), BF16),
        (((taps_n + 7) * HEAD, local), BF16),
        ((width, 3 * local), BF16),
        ((local, width), BF16),
        ((width, hid), BF16),
        ((hid, width), BF16),
        ((seg, width), BF16),
        ((slots, width), BF16),
        ((slots, local), BF16),
        ((2, slots, 128), F32),
        ((4, 2, steps + 3 * PAD, 128), F32),
        ((PAD, 4, steps + 2 * PAD, 256), BF16),
        ((4, steps, 256), F32),
        ((slots, local), BF16),
        ((seg, width), BF16),
        ((seg, width), F32),
        ((slots, width), BF16),
        ((slots, 3 * local), BF16),
        ((4, slots, slots), BF16),
        ((slots, local), BF16),
        ((seg, width), F32),
        *rs,
        *rs,
        ((seg, width), F32),
        ((slots, width), BF16),
        ((slots, hid), BF16),
        ((slots, hid), BF16),
        ((slots, width), BF16),
        ((slots, local), BF16),
        ((slots, 3 * local), BF16),
        ((2, slots, slots), BF16),
        ((seg, width), F32),
        ((seg, width), BF16),
        ((slots, local), BF16),
        ((slots, local), BF16),
        ((seg, width), BF16),
        ((16, width), F32),
        ((seg, width), F32),
    ]
    outs = [
        sds((seg, width), BF16),
        sds((seg, width), F32),
        sds((16, width), F32),
        sds((hid, width), BF16),
        sds((width, hid), BF16),
        sds((local, width), BF16),
        sds((width, 3 * local), BF16),
        sds((4, steps, 256), BF16),
        sds((4, steps, 256), BF16),
        sds((slots, local), BF16),
        sds((slots, local), BF16),
    ]
    return pl.pallas_call(
        functools.partial(layer_kernel, (slots, seg, width, local, hid, taps_n)),
        out_shape=outs,
        in_specs=[pl.BlockSpec(memory_space=pltpu.SMEM)] + [any_spec] * 7 + [vmem],
        out_specs=[vmem] * len(outs),
        scratch_shapes=[pltpu.VMEM(s, d) for s, d in scratch]
        + [pltpu.SemaphoreType.DMA((40,)), pltpu.SemaphoreType.DMA((40,)), pltpu.SemaphoreType.DMA((10,))],
        compiler_params=pltpu.CompilerParams(collective_id=0, has_side_effects=True, vmem_limit_bytes=VMEM_LIMIT),
        name="layer",
    )(lengths, frames, cot, taps, qkv, out_w, inner_w, outer_w, vec)


def spread(values, full_width):
    start_col = lax.axis_index("tensor") * values.shape[-1]
    blank = jnp.zeros(values.shape[:-1] + (full_width,), jnp.float32)
    return lax.dynamic_update_slice_in_dim(blank, values, start_col, axis=values.ndim - 1)


def shards(
    frames,
    lengths,
    pos_weight,
    pos_bias,
    query_key_value_weight,
    qv_bias,
    out_weight,
    out_bias,
    norm1_gain,
    norm1_bias,
    norm2_gain,
    norm2_bias,
    inner_weight,
    inner_bias,
    outer_weight,
    outer_bias,
    cotangent,
):
    _, seg, width = frames.shape
    kernel, group_width, local = pos_weight.shape
    local_groups = local // group_width
    zero = jnp.zeros((local,), BF16)
    vec = jnp.stack(
        [
            out_bias,
            norm1_gain,
            norm1_bias,
            norm2_gain,
            norm2_bias,
            outer_bias,
            inner_bias,
            jnp.concatenate([qv_bias[0], zero, qv_bias[1], zero]),
            jnp.tile(pos_bias.reshape(local_groups, 1, group_width), (1, PHASES, 1)).reshape(-1),
        ]
        + [jnp.zeros((width,), BF16)] * 7
    ).astype(F32)
    (output, frames_grad, small, g_outer, g_inner, g_out, g_qkv, x4, gc4, xflat, gcflat) = run_layer(
        lengths,
        frames[0],
        cotangent[0],
        pos_weight.reshape(kernel * group_width, local),
        query_key_value_weight.reshape(width, 3 * local),
        out_weight,
        inner_weight,
        outer_weight,
        vec,
    )
    channels, grad_conv = xflat[None], gcflat[None]
    pos_grad = lax.conv_general_dilated(
        channels,
        grad_conv,
        (1,),
        [(kernel // 2, kernel // 2 - 1)],
        dimension_numbers=("CWN", "IWO", "WNC"),
        batch_group_count=local_groups,
        preferred_element_type=jnp.float32,
    )
    summed = (
        lax.psum_scatter(pos_grad, "dp", scatter_dimension=0, tiled=True),
        lax.psum_scatter(g_qkv.reshape(width, 3, local), "dp", scatter_dimension=0, tiled=True).astype(F32),
        lax.psum_scatter(g_out, "dp", scatter_dimension=1, tiled=True).astype(F32),
        lax.psum_scatter(g_inner, "dp", scatter_dimension=0, tiled=True).astype(F32),
        lax.psum_scatter(g_outer, "dp", scatter_dimension=1, tiled=True).astype(F32),
    )
    pos_bias_part = small[6].reshape(local_groups, PHASES, group_width).sum(1).reshape(-1)
    qv_part = jnp.stack([small[7, :local], small[7, local : 2 * local]])
    total = lax.psum(
        (
            spread(pos_bias_part, width),
            spread(qv_part, width),
            small[0],
            small[1],
            small[2],
            small[3],
            small[4],
            spread(small[8], 4 * inner_bias.shape[0]),
            small[5],
        ),
        ("dp", "tensor"),
    )
    return (
        output[None],
        frames_grad[None],
        summed[0],
        total[0],
        summed[1],
        total[1],
        summed[2],
        total[2],
        total[3],
        total[4],
        total[5],
        total[6],
        summed[3],
        total[7],
        summed[4],
        total[8],
    )


def solution(mesh):
    placed = (
        P("dp", "tensor", None),
        P("dp"),
        P(None, None, "tensor"),
        P("tensor"),
        P(None, None, "tensor"),
        P(None, "tensor"),
        P("tensor", None),
        P(),
        P(),
        P(),
        P(),
        P(),
        P(None, "tensor"),
        P("tensor"),
        P("tensor", None),
        P(),
        P("dp", "tensor", None),
    )
    return jax.shard_map(
        shards,
        mesh=mesh,
        in_specs=placed,
        out_specs=(
            P("dp", "tensor", None),
            P("dp", "tensor", None),
            P("dp", None, "tensor"),
            P(),
            P("dp", None, "tensor"),
            P(),
            P("tensor", "dp"),
            P(),
            P(),
            P(),
            P(),
            P(),
            P("dp", "tensor"),
            P(),
            P("tensor", "dp"),
            P(),
        ),
        check_vma=False,
    )
```

time: 1140 us -> 603 us (0.53)
  matrix products: 687 us -> 211 us
  Pallas kernels: 0 us -> 140 us
  local copies, waits for them, and re-layouts: 168 us -> 47.6 us
  other arithmetic: 43.6 us -> 3.99 us
  starting transfers between devices: 23.5 us -> 0.2 us
    conv_general_dilated x3 -> x0, matrix products: 419 us -> none  [the longest x1 259 us: shards(): lax.conv_general_dilated(grad_conv, flipped, (1,), [(kernel // 2 - 1, ker...]
    pallas_call x0 -> x1, Pallas kernels: none -> 140 us  [run_layer(): pl.pallas_call(functools.partial(layer_kernel, (slots, seg, width, local,...]
    reduce_scatter x1, waiting for transfers between devices: 0.02 us -> 132 us  [shards(): lax.psum_scatter(pos_grad, 'dp', scatter_dimension=0, tiled=True)]
    all_gather x6 -> x0, waiting for transfers between devices: 67.7 us -> none  [the longest x2 29.4 us: forward_pass(): full_two = lax.all_gather(normed_two, 'tensor', axis=1, tiled=True)]
    reduce_scatter x9 -> x1, waiting for transfers between devices: 65.8 us -> 0.01 us  [shards(): lax.psum_scatter(g_inner, 'dp', scatter_dimension=0, tiled=True).astype(F32)]
    rev x1 -> x0, local copies, waits for them, and re-layouts: 62.7 us -> none  [shards(): pos_weight[::-1].reshape(kernel, group_width, local_groups, group_width)]
    dot_general x21 -> x0, matrix products: 61.9 us -> none  [the longest x1 9.18 us: forward_pass(): jnp.einsum('rtf,fd->rtd', hidden, outer_weight, preferred_element_type=jn...]
    all_to_all x6 -> x0, starting transfers between devices: 22.1 us -> none  [the longest x2 7.67 us: forward_pass(): lax.all_to_all(zeroed, 'tensor', split_axis=2, concat_axis=1, tiled=True)]
  transfers between devices with their start and end apart: 22 -> 5, of which waited for: 13 -> 1; matrix products, arithmetic and copies ran while one was open for 61% -> 42% of each run, Pallas kernels for 0% -> 0%
where the time goes in v1:
time: 603 us; the launch traced here: 593 us
  matrix products  211 us (35%)
  Pallas kernels  140 us (23%)
  waiting for transfers between devices  133 us (22%)
  local copies, waits for them, and re-layouts  47.6 us (8%)
  blocking collectives  42 us (7%)
  between operations  15.1 us (3%)
    conv_general_dilated x1, matrix products, shards(): lax.conv_general_dilated(channels, grad_conv, (1,), [(kernel // 2, kernel...  211 us
    pallas_call x1, Pallas kernels, run_layer(): pl.pallas_call(functools.partial(layer_kernel, (slots, seg, width, local,...  140 us
    reduce_scatter x1, waiting for transfers between devices, shards(): lax.psum_scatter(pos_grad, 'dp', scatter_dimension=0, tiled=True)  132 us
    psum x1, blocking collectives, shards(): lax.psum((spread(pos_bias_part, width), spread(qv_part, width), small[0],...  42 us
    conv_general_dilated x2, local copies, waits for them, and re-layouts, shards(): lax.conv_general_dilated(channels, grad_conv, (1,), [(kernel // 2, kernel...  23.8 us
    unnamed x21, local copies, waits for them, and re-layouts  13.1 us
  transfers between devices with their start and end apart: 5, of which 1 were waited for; matrix products, arithmetic and copies ran while one was open for 42% of the time, Pallas kernels for 0%

profile of v1, /device:TPU:0, one launch (start us, length us, event | category | flops | bytes accessed | tf_op | source)
XLA Modules:
  0.0 593.2 jit_solution(13985595442091168273)
XLA Ops:
  7.2 0.0 reduce-scatter.18.cloned.1.call-start
  7.9 0.7 tile.9
  8.6 0.8 slice_reduce_fusion.2
  9.4 0.1 tile.11
  9.5 0.7 stack.36
  10.2 0.7 stack.37
  10.9 0.7 stack.38
  11.6 0.7 stack.39
  12.3 0.7 stack.40
  12.9 0.7 stack.42
  13.6 0.7 stack.41
  14.3 0.1 stack.46
  14.4 0.6 convert_element_type.15.refs_8_
  15.1 1.7 copy.47
  16.8 1.6 copy.48.refs_4_
  18.4 139.9 %layer.1 = (bf16[128,1024]{1,0:T(8,128)(2,1)}, f32[128,1024]{1,0:T(8,128)}, f32[16,1024]{1,0:T(8,128)}, bf16[1024,1024]{1,0:T(8,128)(2,1)}, bf16[1024,1024]{1,0:...) custom-call(s32[1]{0:T(128)S(6)} %copy.70.refs_0_, ...), custom_call_target="tpu_custom_call" | custom-call | tf_op jit(solution)/shard_map/layer/pallas_call | solution.py:695
  158.2 0.0 copy-start
  158.3 2.2 copy.59
  160.4 0.0 reduce-scatter.18.cloned.1.call-update
  160.5 0.0 reduce-scatter.16.cloned.1.call-start
  160.5 0.7 reduce-scatter.16.cloned.1.call-update
  161.2 0.0 reduce-scatter.20.cloned.1.call-start
  161.3 0.0 copy-done
  161.3 2.6 copy.61
  163.9 0.0 copy-start.4
  163.9 0.0 copy-start.3
  163.9 0.0 reduce-scatter.20.cloned.1.call-update
  163.9 0.0 reduce-scatter.14.cloned.1.call-start
  163.9 0.5 reduce-scatter.14.cloned.1.call-update
  164.5 0.0 reduce-scatter.12.cloned.1.call-start
  164.5 0.3 copy-done.4
  164.8 0.1 copy.49
  165.0 0.0 copy-done.3
  165.0 0.1 copy.50
  165.1 0.8 copy.52
  165.9 0.8 copy.51
  166.7 210.9 %fusion.2 = f32[128,64,4,64]{3,1,2,0:T(8,128)} fusion(bf16[1,512,4,64]{3,0,2,1:T(2,128)(2,1)S(1)} %copy.51, bf16[1,512,4,64]{3,0,2,1:T(2,128)(2,1)S(1)} %copy.52), kind=kOutput, calls=%fused_computation.7 | convolution fusion | flops 2013265920 | bytes 8912896 | tf_op jit(solution)/shard_map/conv_general_dilated | solution.py:762
  377.7 14.5 %copy.53 = f32[128,64,4,64]{0,3,2,1:T(8,128)} copy(f32[128,64,4,64]{3,1,2,0:T(8,128)} %fusion.2) | data formatting | bytes 16777216 | tf_op jit(solution)/shard_map/conv_general_dilated | solution.py:762
  392.2 9.3 %copy.54 = f32[128,64,256]{2,1,0:T(8,128)} copy(f32[128,64,256]{0,2,1:T(8,128)} %bitcast.29) | data formatting | bytes 16777216 | tf_op jit(solution)/shard_map/conv_general_dilated | solution.py:762
  401.4 0.0 copy-start.5
  401.4 0.0 reduce-scatter.12.cloned.1.call-update
  401.5 0.0 copy-start.2
  401.5 0.0 copy-start.1
  401.5 0.8 copy-done.5
  402.3 0.1 reshape_squeeze.3
  402.4 0.1 reshape.57
  402.5 0.2 dynamic_update_slice.11
  402.7 0.2 dynamic_update_slice.9
  403.0 42.0 %all-reduce = (f32[1024]{0:T(1024)}, f32[2,1024]{1,0:T(2,128)}, f32[1024]{0:T(1024)}, f32[1024]{0:T(1024)}, f32[1024]{0:T(1024)}, /*index=5*/f32[1024]{0:T(1024)}, f32[1024]{0:T(1024)}, f32[4096]{0:T(1024)}, f32[1024]{0:T(1024)}) all-reduce(f32[1024]{0:T(1024)S(1)} %dynamic_update_slice.9, ...), channel_id=1, replica_groups=mesh['dp'=8,'tensor'=4] {'dp','tensor'}, use_global_device_ids=true, to_apply=%region_2.0 | all-reduce | flops 13312 | bytes 106496 | tf_op jit(solution)/shard_map/psum | solution.py:780
  445.1 0.0 reduce-scatter.18.cloned.1.call-done
  445.1 1.0 copy.60
  446.0 0.7 convert_element_type.17
  446.7 0.0 reduce-scatter.16.cloned.1.call-done
  446.7 1.1 copy.64
  447.8 0.9 copy.56
  448.7 0.0 reduce-scatter.20.cloned.1.call-done
  448.7 1.1 copy.62
  449.8 0.8 convert_element_type.19
  450.6 1.8 convert_element_type.18
  452.4 132.2 %reduce-scatter.12.cloned.1.call-done = f32[16,64,256]{2,1,0:T(8,128)} async-done(((f32[128,64,256]{2,1,0:T(8,128)}), f32[16,64,256]{2,1,0:T(8,128)}) %reduce-scatter.12.cloned.1.call-update) | async-done | bytes 1048592 | tf_op jit(solution)/shard_map/reduce_scatter | solution.py:772
  584.6 0.0 copy-done.2
  584.6 0.7 copy.71
  585.3 0.0 copy-done.1
  585.3 0.8 copy.72
  (15 shorter events, 0.1 us)
Async XLA Ops:
  7.2 437.9 %reduce-scatter.18.cloned.1.call-start = ((), (), s32[]{:S(2)}) async-start(), calls=%async_computation.8 | async-start | bytes 589824
  158.2 3.0 copy-start
  160.5 286.2 %reduce-scatter.16.cloned.1.call-start = ((), (), s32[]{:S(2)}) async-start(), calls=%async_computation.7 | async-start | bytes 1769472
  161.2 287.5 %reduce-scatter.20.cloned.1.call-start = ((), (), s32[]{:S(2)}) async-start(), calls=%async_computation.9 | async-start | bytes 2359296
  163.9 0.9 copy-start.4
  163.9 1.1 copy-start.3
  163.9 286.8 %reduce-scatter.14.cloned.1.call-start = ((), (), s32[]{:S(2)}) async-start(), calls=%async_computation.6 | async-start | bytes 2359296 | tf_op jit(solution)/shard_map/reduce_scatter | solution.py:775
  164.5 420.2 %reduce-scatter.12.cloned.1.call-start = ((), (), s32[]{:S(2)}) async-start(), calls=%async_computation.5 | async-start | bytes 9437184 | tf_op jit(solution)/shard_map/reduce_scatter | solution.py:772
  401.4 0.8 copy-start.5
  401.5 183.2 %copy-start.2 = (bf16[128,1024]{1,0:T(8,128)(2,1)S(1)}, bf16[128,1024]{1,0:T(8,128)(2,1)}, u32[]{:S(2)}) copy-start(bf16[128,1024]{1,0:T(8,128)(2,1)} %get-tuple-element.25) | copy-start | bytes 786436
  401.5 183.9 %copy-start.1 = (f32[128,1024]{1,0:T(8,128)S(1)}, f32[128,1024]{1,0:T(8,128)}, u32[]{:S(2)}) copy-start(f32[128,1024]{1,0:T(8,128)} %get-tuple-element.26) | copy-start | bytes 1572868
Sparse Core Ops, SparseCore 0:
  160.6 63.5 reduce-scatter.17
  227.6 64.5 reduce-scatter.15
  295.8 67.1 reduce-scatter.19
  366.3 67.8 reduce-scatter.13
  438.2 146.3 reduce-scatter.11

commit v2 on v1

v2 whole, which is shorter than its diff:
```python
import functools

import jax
import jax.numpy as jnp
from jax import lax
from jax.experimental import pallas as pl
from jax.experimental.pallas import tpu as pltpu
from jax.sharding import PartitionSpec as P

HEAD = 64
EPSILON = 1e-05
NEGATIVE = -1e30
F32 = jnp.float32
BF16 = jnp.bfloat16
PHASES = 4
PAD = 16
VMEM_LIMIT = 67043328


def nn(a, b):
    return lax.dot_general(a, b, (((1,), (0,)), ((), ())), preferred_element_type=F32)


def nt(a, b):
    return lax.dot_general(a, b, (((1,), (1,)), ((), ())), preferred_element_type=F32)


def tn(a, b):
    return lax.dot_general(a, b, (((0,), (0,)), ((), ())), preferred_element_type=F32)


def aligned(start, size, unit):
    return pl.ds(pl.multiple_of(start, unit), size)


def gelu_pair(x):
    cdf = 0.5 + 0.5 * lax.erf(x * 0.7071067811865476)
    return x * cdf, cdf + x * (0.3989422804014327 * jnp.exp(-0.5 * x * x))


def norm_stats(x):
    centered = x - jnp.mean(x, axis=-1, keepdims=True)
    scale = lax.rsqrt(jnp.mean(centered * centered, axis=-1, keepdims=True) + EPSILON)
    return centered * scale, scale


def low_half(rows):
    return lax.broadcasted_iota(jnp.int32, (rows, 128), 1) < HEAD


def swap_halves(x):
    return pltpu.roll(x, HEAD, 1)


def split_phases(flat):
    steps = flat.shape[1] // PHASES
    low = low_half(steps)
    rows = [[flat[v, pl.ds(q, steps, stride=PHASES), :] for v in range(2)] for q in range(PHASES)]
    groups = []
    for g in range(4):
        v, h = g // 2, g % 2

        def piece(q, half):
            return rows[q][v] if h == half else swap_halves(rows[q][v])

        groups.append((jnp.where(low, piece(0, 0), piece(1, 1)), jnp.where(low, piece(2, 0), piece(3, 1))))
    return groups


def join_phases(groups, flat):
    steps = flat.shape[1] // PHASES
    low = low_half(steps)
    for v in range(2):
        for s in range(PHASES):
            first, second = groups[2 * v][s // 2], groups[2 * v + 1][s // 2]
            first = first if s % 2 == 0 else swap_halves(first)
            second = second if s % 2 == 1 else swap_halves(second)
            flat[v, pl.ds(s, steps, stride=PHASES), :] = jnp.where(low, first, second)


def tap_tile(taps, g, block):
    v, h = g // 2, g % 2
    columns = slice(v * 128, (v + 1) * 128)
    low = low_half(256)

    def source(s):
        part = taps[aligned((PHASES * block - s + 3) * HEAD, 256, HEAD), columns]
        return part if s % 2 == h else swap_halves(part)

    return jnp.concatenate([jnp.where(low, source(0), source(1)), jnp.where(low, source(2), source(3))], axis=1)


def shift_copies(padded, shifts, rows):
    for g in range(4):
        for v in range(2):

            def one(b, carry):
                shifts[b, g, :, v * 128 : (v + 1) * 128] = padded[g, v, pl.ds(b, rows), :].astype(BF16)
                return carry

            lax.fori_loop(0, PAD, one, 0)


def store_padded(groups, padded):
    steps = groups[0][0].shape[0]
    for g in range(4):
        for v in range(2):
            padded[g, v, pl.ds(PAD, steps), :] = groups[g][v]


class Named:
    def __init__(self, names, refs):
        self.__dict__.update(zip(names, refs, strict=True))


def layer_kernel(sizes, names, inside, *refs):
    slots, seg, width, local, hid, taps_n = sizes
    r = Named(names, refs)
    steps = slots // PHASES
    blocks = taps_n // PHASES
    chunk = 32
    me = lax.axis_index("tensor")
    core = lax.rem(me, 2)
    mate = me + 1 - 2 * core
    across = lax.rem(me + 2, 4)
    diag = lax.rem(mate + 2, 4)
    peers = (mate, across, diag)
    row = lax.axis_index("dp")
    x = lax.rem(row, 2)
    z = row // 2
    x_mate = row + 1 - 2 * x
    ups = [lax.rem(z + k, 4) for k in (1, 2, 3)]
    downs = [lax.rem(z + 4 - k, 4) for k in (1, 2, 3)]
    counter = {"remote": 0, "local": 0}
    pending = {}

    def rows_of(owner):
        return aligned(owner * seg, seg, seg)

    def columns_of(owner):
        return aligned(owner * local, local, local)

    def send(src, dst, peer, axis="tensor"):
        index = counter["remote"]
        counter["remote"] += 1
        copy = pltpu.make_async_remote_copy(
            src_ref=src,
            dst_ref=dst,
            send_sem=r.send_sem.at[index],
            recv_sem=r.recv_sem.at[index],
            device_id={axis: peer},
            device_id_type=pl.DeviceIdType.MESH,
        )
        copy.start()
        pending[index] = copy
        return index

    def sent(ids):
        for index in ids:
            pending.pop(index).wait_send()

    def arrive(index, region):
        pltpu.make_async_remote_copy(
            src_ref=region,
            dst_ref=region,
            send_sem=r.send_sem.at[index],
            recv_sem=r.recv_sem.at[index],
            device_id={"tensor": mate},
            device_id_type=pl.DeviceIdType.MESH,
        ).wait_recv()

    def fetch(src, dst):
        index = counter["local"]
        counter["local"] += 1
        copy = pltpu.make_async_copy(src, dst, r.local_sem.at[index])
        copy.start()
        return copy

    c_own = fetch(r.frames_in.at[:, columns_of(me)], r.x_raw.at[rows_of(me), :])
    c_taps = fetch(r.taps_in, r.taps.at[pl.ds(3 * HEAD, taps_n * HEAD), :])
    c_frames = fetch(r.frames_in, r.frames_v)
    c_cot = fetch(r.cot_in, r.cot_full.at[rows_of(me), :])
    c_qkv = fetch(r.qkv_in, r.w_qkv)
    c_out = fetch(r.out_in, r.w_out)
    c_inner = fetch(r.inner_in, r.w_inner)
    c_outer = fetch(r.outer_in, r.w_outer)

    barrier = pltpu.get_barrier_semaphore()
    greet = [("tensor", p) for p in peers]
    if inside:
        greet += [("dp", x_mate)] + [("dp", 2 * k + x) for k in ups]
    for axis, peer in greet:
        pl.semaphore_signal(barrier, inc=1, device_id={axis: peer}, device_id_type=pl.DeviceIdType.MESH)
    pl.semaphore_wait(barrier, len(greet))

    i_frames = [send(r.frames_in.at[:, columns_of(p)], r.x_raw.at[rows_of(me), :], p) for p in peers]
    i_cot = [send(r.cot_in, r.cot_full.at[rows_of(me), :], p) for p in (mate, across)]

    r.taps[pl.ds(0, 3 * HEAD), :] = jnp.zeros((3 * HEAD, local), BF16)
    r.taps[pl.ds((3 + taps_n) * HEAD, 4 * HEAD), :] = jnp.zeros((4 * HEAD, local), BF16)
    for g in range(4):
        for v in range(2):
            r.padded[g, v, pl.ds(0, PAD), :] = jnp.zeros((PAD, 128), F32)
            r.padded[g, v, pl.ds(PAD + steps, 2 * PAD), :] = jnp.zeros((2 * PAD, 128), F32)
    r.small[...] = jnp.zeros_like(r.small)

    def dp_gather(slot):
        ids = [send(slot(row), slot(row), 2 * k + x, "dp") for k in ups]
        return ids, [send(slot(row), slot(row), x_mate, "dp")]

    def dp_relay(ids, slot):
        for index, k in zip(ids[0], downs):
            arrive(index, slot(2 * k + x))
            ids[1].append(send(slot(2 * k + x), slot(2 * k + x), x_mate, "dp"))

    def dp_gathered(ids, slot):
        for index, k in zip(ids[1], [z] + downs):
            arrive(index, slot(2 * k + 1 - x))

    def dp_first(buf, from_x):
        return [send(buf.at[1 - x], from_x, x_mate, "dp")]

    def dp_second(ids, buf, from_x, from_z):
        arrive(ids[0], from_x)

        def add(k, carry):
            buf[x, k] = (buf[x, k].astype(F32) + from_x[k].astype(F32)).astype(BF16)
            return carry

        lax.fori_loop(0, 4, add, 0)
        for slot, k in enumerate(ups):
            ids.append(send(buf.at[x, k], from_z.at[slot], 2 * k + x, "dp"))

    def dp_third(ids, buf, from_z, out):
        total = buf[x, z].astype(F32)
        for slot in range(3):
            arrive(ids[1 + slot], from_z.at[slot])
            total = total + from_z[slot].astype(F32)
        out[...] = total

    length = r.len_ref[0]
    c_own.wait()
    for index, p in zip(i_frames, peers):
        arrive(index, r.x_raw.at[rows_of(p), :])

    live_all = lax.broadcasted_iota(jnp.int32, (slots, 128), 0) < length
    for v in range(2):
        r.flat[v] = jnp.where(live_all, r.x_raw[:, v * 128 : (v + 1) * 128].astype(F32), 0.0)
    phased = split_phases(r.flat)
    store_padded(phased, r.padded)
    if inside:
        for g in range(4):
            for v in range(2):
                r.xg[row, g, :, v * 128 : (v + 1) * 128] = phased[g][v].astype(BF16)
        ids_x = dp_gather(lambda e: r.xg.at[e])
    else:
        r.xflat_o[...] = jnp.concatenate([r.flat[0], r.flat[1]], axis=1).astype(BF16)
    shift_copies(r.padded, r.shifts, steps + 2 * PAD)
    c_taps.wait()

    def shifted(g, low_part, high_part):
        return r.shifts[low_part, g, pl.ds(high_part * PAD, steps), :]

    pos_groups = []
    for g in range(4):

        def forward(b, total):
            for high in range(2):
                total = total + nn(shifted(g, b, high), tap_tile(r.taps, g, b + PAD * high))
            return total

        total = nn(shifted(g, 0, 2), tap_tile(r.taps, g, blocks))
        total = lax.fori_loop(0, PAD, forward, total)
        value, slope = gelu_pair(total + r.vec[pl.ds(8, 1), g * 256 : (g + 1) * 256])
        r.gelu_grad[g] = slope
        pos_groups.append((value[:, :128], value[:, 128:]))
    join_phases(pos_groups, r.flat)
    r.pos_send[...] = jnp.concatenate([r.flat[0], r.flat[1]], axis=1).astype(BF16)
    i_pos = [send(r.pos_send.at[rows_of(p), :], r.pos_recv.at[:, columns_of(me)], p) for p in peers]
    arrive(i_cot[1], r.cot_full.at[rows_of(across), :])
    i_cot.append(send(r.cot_full.at[rows_of(across), :], r.cot_full.at[rows_of(across), :], mate))
    r.pos_recv[:, columns_of(me)] = r.pos_send[rows_of(me), :]
    c_frames.wait()
    for index, p in zip(i_pos, peers):
        arrive(index, r.pos_recv.at[:, columns_of(p)])

    seg_start = me * seg

    def own(b):
        return aligned(b * chunk, chunk, chunk)

    def shared(b):
        return aligned(seg_start + b * chunk, chunk, chunk)

    def each_chunk(body):
        def step(b, carry):
            body(b)
            return carry

        lax.fori_loop(0, seg // chunk, step, 0)

    def live_rows(b):
        return seg_start + b * chunk + lax.broadcasted_iota(jnp.int32, (chunk, 1), 0) < length

    def vec_row(k):
        return r.vec[pl.ds(k, 1), :]

    def norm_one(b):
        rows = own(b)
        value = jnp.where(live_rows(b), r.frames_v[rows, :].astype(F32), 0.0) + r.pos_recv[rows, :].astype(F32)
        r.s1[rows, :] = value
        unit, _ = norm_stats(value)
        r.full1[shared(b), :] = (unit * vec_row(1) + vec_row(2)).astype(BF16)

    each_chunk(norm_one)

    def gather_start(full):
        return [send(full.at[rows_of(me), :], full.at[rows_of(me), :], p) for p in (mate, across)]

    def gather_relay(ids, full):
        arrive(ids[1], full.at[rows_of(across), :])
        ids.append(send(full.at[rows_of(across), :], full.at[rows_of(across), :], mate))

    pair = aligned((me - core) * seg, 2 * seg, 2 * seg)
    far_pair = aligned(lax.rem(me - core + 2, 4) * seg, 2 * seg, 2 * seg)

    ids1 = gather_start(r.full1)
    c_qkv.wait()

    def project(rows):
        for part in range(3):
            columns = slice(part * local, (part + 1) * local)
            value = nn(r.full1[rows, :], r.w_qkv[:, columns]) + r.vec[pl.ds(7, 1), columns]
            r.proj[rows, columns] = value.astype(BF16)

    arrive(ids1[0], r.full1.at[rows_of(mate), :])
    project(pair)
    gather_relay(ids1, r.full1)
    arrive(ids1[2], r.full1.at[rows_of(diag), :])
    project(far_pair)

    block = 128
    scale = HEAD**-0.5
    live_keys = lax.broadcasted_iota(jnp.int32, (1, slots), 1) < length

    def head_columns(part, head):
        return slice(part * local + head * HEAD, part * local + (head + 1) * HEAD)

    for hp in range(2):

        def attend(b, carry):
            rows = aligned(b * block, block, block)
            outs = []
            for head in (2 * hp, 2 * hp + 1):
                scores = nt(r.proj[rows, head_columns(0, head)], r.proj[:, head_columns(1, head)]) * scale
                scores = jnp.where(live_keys, scores, NEGATIVE)
                weights = jnp.exp(scores - jnp.max(scores, axis=-1, keepdims=True))
                low = (weights * (1.0 / jnp.sum(weights, axis=-1, keepdims=True))).astype(BF16)
                r.probs[head, rows, :] = low
                outs.append(nn(low, r.proj[:, head_columns(2, head)]))
            r.ctx[rows, hp * 128 : (hp + 1) * 128] = jnp.concatenate(outs, axis=1).astype(BF16)
            return carry

        lax.fori_loop(0, slots // block, attend, 0)

    def tiles(count, body):
        def step(b, carry):
            body(aligned(b * 256, 256, 256))
            return carry

        lax.fori_loop(0, count // 256, step, 0)

    def scatter_start(partial, bufs):
        send_buf, core_buf, mid_buf, y_buf = bufs

        def to(slot, owner):
            def tile(columns):
                send_buf[slot, :, columns] = partial(owner, columns).astype(BF16)

            tiles(width, tile)
            return send(send_buf.at[slot], core_buf.at[slot], mate)

        ids = [to(1, diag), to(0, mate)]
        arrive(ids[0], core_buf.at[1])

        def tile(columns):
            mid_buf[:, columns] = (partial(across, columns) + core_buf[1, :, columns].astype(F32)).astype(BF16)

        tiles(width, tile)
        ids.append(send(mid_buf, y_buf, across))

        return ids

    def scatter_own(partial):
        def tile(columns):
            r.keep[:, columns] = partial(me, columns)

        tiles(width, tile)

    def scatter_end(ids, bufs):
        arrive(ids[1], bufs[1].at[0])
        arrive(ids[2], bufs[3])

    main_bufs = (r.rs_send, r.rs_core, r.rs_mid, r.rs_y)
    ff_bufs = (r.rf_send, r.rf_core, r.rf_mid, r.rf_y)

    def summed(rows, bufs):
        return r.keep[rows, :] + bufs[1][0, rows, :].astype(F32) + bufs[3][rows, :].astype(F32)

    c_out.wait()

    def attended(owner, columns):
        return nn(r.ctx[rows_of(owner), :], r.w_out[:, columns])

    ids_a = scatter_start(attended, main_bufs)
    scatter_own(attended)
    if inside:
        dp_relay(ids_x, lambda e: r.xg.at[e])
    scatter_end(ids_a, main_bufs)

    def norm_two(b):
        rows = own(b)
        value = r.s1[rows, :] + summed(rows, main_bufs) + vec_row(0)
        r.s2[rows, :] = value
        unit, _ = norm_stats(value)
        r.full2[shared(b), :] = (unit * vec_row(3) + vec_row(4)).astype(BF16)

    each_chunk(norm_two)

    ids2 = gather_start(r.full2)
    c_inner.wait()
    c_outer.wait()
    c_cot.wait()
    arrive(i_cot[0], r.cot_full.at[rows_of(mate), :])
    arrive(i_cot[2], r.cot_full.at[rows_of(diag), :])

    def feed(rows):
        def tile(columns):
            pre = nn(r.full2[rows, :], r.w_inner[:, columns]) + r.vec[pl.ds(6, 1), columns]
            value, slope = gelu_pair(pre)
            r.hidden[rows, columns] = value.astype(BF16)
            r.grad_in[rows, columns] = (nt(r.cot_full[rows, :], r.w_outer[columns, :]) * slope).astype(BF16)

        tiles(hid, tile)

    arrive(ids2[0], r.full2.at[rows_of(mate), :])
    feed(pair)
    gather_relay(ids2, r.full2)
    arrive(ids2[2], r.full2.at[rows_of(diag), :])
    feed(far_pair)

    def grad_two_part(owner, columns):
        return nt(r.grad_in[rows_of(owner), :], r.w_inner[columns, :])

    def branch_part(owner, columns):
        return nn(r.hidden[rows_of(owner), :], r.w_outer[:, columns])

    sent(ids_a)
    ids_b = scatter_start(grad_two_part, main_bufs)
    scatter_own(grad_two_part)

    def store_columns(dst, rows, value):
        for k in range(4):
            for j in range(2):
                start = (2 * k + j) * 128
                dst[j, k, rows, :] = value[:, start : start + 128].astype(BF16)

    def outer_tile(rows):
        value = tn(r.hidden[:, rows], r.cot_full[...])
        if inside:
            store_columns(r.g_outer, rows, value)
        else:
            r.g_outer[rows, :] = value.astype(BF16)

    def grouped_rows(dst, left, right):
        def tile(b, carry):
            rows = aligned(b * 256, 256, 256)
            value = tn(left[:, rows], right[...])
            if inside:
                dst[0, b] = value[:128].astype(BF16)
                dst[1, b] = value[128:].astype(BF16)
            else:
                dst[rows, :] = value.astype(BF16)
            return carry

        lax.fori_loop(0, width // 256, tile, 0)

    tiles(hid, outer_tile)
    if inside:
        ids_outer = dp_first(r.g_outer, r.x_outer)
    scatter_end(ids_b, main_bufs)

    def put_sum(k, value):
        r.small[pl.ds(k, 1), :] = r.small[pl.ds(k, 1), :] + jnp.sum(value, axis=0, keepdims=True)

    def norm_back(grad, stream, gain, gain_row, bias_row):
        unit, inv = norm_stats(stream)
        put_sum(gain_row, grad * unit)
        put_sum(bias_row, grad)
        w = grad * gain
        return inv * (w - jnp.mean(w, axis=-1, keepdims=True) - unit * jnp.mean(w * unit, axis=-1, keepdims=True))

    def back_two(b):
        rows = own(b)
        cot = r.cot_full[shared(b), :].astype(F32)
        put_sum(5, cot)
        grad_two = cot + norm_back(summed(rows, main_bufs), r.s2[rows, :], vec_row(3), 3, 4)
        r.grad_one[rows, :] = grad_two
        low = grad_two.astype(BF16)
        r.full3[shared(b), :] = low
        put_sum(0, low.astype(F32))

    each_chunk(back_two)
    ids3 = gather_start(r.full3)

    grouped_rows(r.g_inner, r.full2, r.grad_in)
    if inside:
        ids_inner = dp_first(r.g_inner, r.x_inner)
    gather_relay(ids3, r.full3)
    ids_f = scatter_start(branch_part, ff_bufs)

    arrive(ids3[0], r.full3.at[rows_of(mate), :])
    arrive(ids3[2], r.full3.at[rows_of(diag), :])
    r.gctx[...] = nt(r.full3[...], r.w_out[...]).astype(BF16)
    g_out = tn(r.ctx[...], r.full3[...])
    if inside:
        store_columns(r.g_out, pl.ds(0, local), g_out)
        ids_out = dp_first(r.g_out, r.x_out)
    else:
        r.g_out[...] = g_out.astype(BF16)

    for hp in range(2):

        def back_scores(b, carry):
            rows = aligned(b * block, block, block)
            outs = []
            for j, head in enumerate((2 * hp, 2 * hp + 1)):
                p = r.probs[head, rows, :].astype(F32)
                gp = nt(r.gctx[rows, head_columns(0, head)], r.proj[:, head_columns(2, head)])
                gs = (p * (gp - jnp.sum(p * gp, axis=-1, keepdims=True))).astype(BF16)
                r.gscore[j, rows, :] = gs
                outs.append(nn(gs, r.proj[:, head_columns(1, head)]))
            r.gproj[rows, hp * 128 : (hp + 1) * 128] = (jnp.concatenate(outs, axis=1) * scale).astype(BF16)
            return carry

        lax.fori_loop(0, slots // block, back_scores, 0)
        gk = [tn(r.gscore[j], r.proj[:, head_columns(0, 2 * hp + j)]) for j in range(2)]
        r.gproj[:, local + hp * 128 : local + (hp + 1) * 128] = (jnp.concatenate(gk, axis=1) * scale).astype(BF16)
        gv = [tn(r.probs[2 * hp + j], r.gctx[:, head_columns(0, 2 * hp + j)]) for j in range(2)]
        r.gproj[:, 2 * local + hp * 128 : 2 * local + (hp + 1) * 128] = jnp.concatenate(gv, axis=1).astype(BF16)

    def grad_one_part(owner, columns):
        return nt(r.gproj[rows_of(owner), :], r.w_qkv[columns, :])

    sent(ids_b)
    ids_c = scatter_start(grad_one_part, main_bufs)
    scatter_own(grad_one_part)
    grouped_rows(r.g_qkv, r.full1, r.gproj)
    if inside:
        ids_qkv = dp_first(r.g_qkv, r.x_qkv)
    scatter_end(ids_c, main_bufs)

    def back_one(b):
        rows = own(b)
        total = r.grad_one[rows, :] + norm_back(summed(rows, main_bufs), r.s1[rows, :], vec_row(1), 1, 2)
        r.grad_one[rows, :] = total
        r.ga_send[rows, :] = total.astype(BF16)

    each_chunk(back_one)
    i_ga = [send(r.ga_send.at[:, columns_of(p)], r.ga_recv.at[rows_of(me), :], p) for p in peers]
    r.ga_recv[rows_of(me), :] = r.ga_send[:, columns_of(me)]

    if inside:
        dp_second(ids_outer, r.g_outer, r.x_outer, r.z_outer)

    scatter_own(branch_part)
    scatter_end(ids_f, ff_bufs)

    def finish(b):
        rows = own(b)
        r.output_o[rows, :] = (r.s2[rows, :] + summed(rows, ff_bufs) + vec_row(5)).astype(BF16)

    each_chunk(finish)
    ones = jnp.ones((8, slots), BF16)
    sums = nn(ones, r.gproj[...])
    r.small[pl.ds(7, 1), 0:local] = sums[0:1, 0:local]
    r.small[pl.ds(7, 1), local : 2 * local] = sums[0:1, 2 * local :]
    r.small[pl.ds(8, 1), :] = nn(ones, r.grad_in[...])[0:1, :]

    for index, p in zip(i_ga, peers):
        arrive(index, r.ga_recv.at[rows_of(p), :])
    for v in range(2):
        r.flat[v] = r.ga_recv[:, v * 128 : (v + 1) * 128].astype(F32)
    grads = []
    for g, halves in enumerate(split_phases(r.flat)):
        both = []
        for v in range(2):
            lanes = slice(v * 128, (v + 1) * 128)
            low = (halves[v] * r.gelu_grad[g, :, lanes]).astype(BF16)
            value = low.astype(F32)
            both.append(value)
            r.small[pl.ds(6, 1), g * 256 + v * 128 : g * 256 + (v + 1) * 128] = jnp.sum(value, axis=0, keepdims=True)
            if inside:
                r.gt[g, lanes, aligned(row * steps, steps, steps)] = value.T.astype(BF16)
        grads.append(both)

    def gt_slot(e):
        return r.gt.at[:, :, aligned(e * steps, steps, steps)]

    store_padded(grads, r.padded)
    if inside:
        ids_g = dp_gather(gt_slot)
        i_mini = [send(r.small.at[pl.ds(0, 8), columns_of(p)], r.mini_t.at[me], p) for p in peers]
        r.mini_t[me] = r.small[pl.ds(0, 8), columns_of(me)]
    else:
        join_phases(grads, r.flat)
        r.gcflat_o[...] = jnp.concatenate([r.flat[0], r.flat[1]], axis=1).astype(BF16)
    shift_copies(r.padded, r.shifts, steps + 2 * PAD)
    in_groups = []
    for g in range(4):

        def backward(b, total):
            for high in range(2):
                total = total + nt(shifted(g, b, high), tap_tile(r.taps, g, blocks - (b + PAD * high)))
            return total

        total = nt(shifted(g, 0, 2), tap_tile(r.taps, g, 0))
        total = lax.fori_loop(0, PAD, backward, total)
        in_groups.append((total[:, :128], total[:, 128:]))
    join_phases(in_groups, r.flat)
    r.gx_send[...] = jnp.concatenate([r.flat[0], r.flat[1]], axis=1).astype(BF16)
    i_gx = [send(r.gx_send.at[rows_of(p), :], r.gx_recv.at[:, columns_of(me)], p) for p in peers]
    r.gx_recv[:, columns_of(me)] = r.gx_send[rows_of(me), :]

    if inside:
        dp_second(ids_inner, r.g_inner, r.x_inner, r.z_inner)
        dp_second(ids_out, r.g_out, r.x_out, r.z_out)

        for index, p in zip(i_mini, peers):
            arrive(index, r.mini_t.at[p])
        quarter = r.mini_t[0] + r.mini_t[1] + r.mini_t[2] + r.mini_t[3]
        folded = []
        for v in range(2):
            parts = []
            for g in (2 * v, 2 * v + 1):
                both = r.small[pl.ds(6, 1), g * 256 : g * 256 + 128] + r.small[pl.ds(6, 1), g * 256 + 128 : (g + 1) * 256]
                both = jnp.broadcast_to(both, (8, 128))
                parts.append(both + swap_halves(both))
            folded.append(jnp.where(low_half(8), parts[0], parts[1])[0:1])
        r.mini[pl.ds(0, 8), :] = quarter
        r.mini[pl.ds(6, 1), :] = jnp.concatenate(folded, axis=1)
        r.mini[pl.ds(7, 1), :] = r.small[pl.ds(7, 1), 0:local]
        r.mini[pl.ds(8, 1), :] = r.small[pl.ds(7, 1), local : 2 * local]
        for k in range(4):
            r.mini[pl.ds(9 + k, 1), :] = r.small[pl.ds(8, 1), k * 256 : (k + 1) * 256]
        r.mini[pl.ds(13, 3), :] = jnp.zeros((3, 256), F32)
        i_mx = send(r.mini, r.mini_x, x_mate, "dp")

        dp_second(ids_qkv, r.g_qkv, r.x_qkv, r.z_qkv)
        arrive(i_mx, r.mini_x)
        r.mini_s[...] = r.mini[...] + r.mini_x[...]
        i_mz = [send(r.mini_s, r.mini_z.at[slot], 2 * k + x, "dp") for slot, k in enumerate(ups)]
        dp_relay(ids_g, gt_slot)
        dp_gathered(ids_x, lambda e: r.xg.at[e])

    for index, p in zip(i_gx, peers):
        arrive(index, r.gx_recv.at[:, columns_of(p)])

    def frames_back(b):
        rows = own(b)
        r.frames_grad_o[rows, :] = jnp.where(live_rows(b), r.grad_one[rows, :] + r.gx_recv[rows, :].astype(F32), 0.0)

    each_chunk(frames_back)

    if inside:
        for slot in range(3):
            arrive(i_mz[slot], r.mini_z.at[slot])
        r.small_o[me] = r.mini_s[...] + r.mini_z[0] + r.mini_z[1] + r.mini_z[2]
        i_mt = [send(r.small_o.at[me], r.small_o.at[me], p) for p in peers]

        reach = 5
        count = taps_n // 8

        def build(column):
            for k in range(4):
                e = 2 * k + column
                for g in range(4):
                    for v in range(2):
                        lanes = slice(v * 128, (v + 1) * 128)
                        r.padded[g, v, pl.ds(PAD, steps), :] = r.xg[e, g, :, lanes].astype(F32)
                for a in range(reach):
                    for g in range(4):
                        for v in range(2):
                            lanes = slice(v * 128, (v + 1) * 128)
                            moved = r.padded[g, v, pl.ds(row * (count // PHASES) + a, steps), :]
                            r.taken[a, g, k * steps : (k + 1) * steps, lanes] = moved.astype(BF16)

        def accumulate(column, first):
            def one(index, carry):
                g = index // reach
                a = index % reach
                left = jnp.concatenate([r.gt[g, :, aligned((2 * k + column) * steps, steps, steps)] for k in range(4)], axis=1)
                value = nn(left, r.taken[a, g])
                for s in range(PHASES):
                    parity = s % 2
                    start = (PHASES * a - s + 3 + (1 - parity)) * HEAD
                    lanes = aligned(start, 256, 128)
                    r.tap_acc[g, parity, :, lanes] = r.tap_acc[g, parity, :, lanes] + value[s * HEAD : (s + 1) * HEAD, :]
                return carry

            lax.fori_loop(0, 4 * reach, one, 0)

        r.tap_acc[...] = jnp.zeros_like(r.tap_acc)
        build(x)
        accumulate(x, True)
        build(1 - x)
        dp_gathered(ids_g, gt_slot)
        accumulate(1 - x, False)
        taps_width = count * HEAD
        for v in range(2):
            both = []
            for g in (2 * v, 2 * v + 1):
                even = r.tap_acc[g, 0, :, 256 : 256 + taps_width]
                odd = pltpu.roll(r.tap_acc[g, 1], r.tap_acc.shape[3] - HEAD, 1)[:, 128 : 128 + taps_width]
                both.append(even + odd)
            r.pos_o[:, v * 128 : (v + 1) * 128] = jnp.concatenate(both, axis=0).T

        dp_third(ids_outer, r.g_outer, r.z_outer, r.outer_o)
        dp_third(ids_inner, r.g_inner, r.z_inner, r.inner_o)
        dp_third(ids_out, r.g_out, r.z_out, r.out_o)
        dp_third(ids_qkv, r.g_qkv, r.z_qkv, r.qkv_o)
        for index, p in zip(i_mt, peers):
            arrive(index, r.small_o.at[p])
    else:
        r.small_o[...] = r.small[...]
    sent(list(pending))


def run_layer(inside, lengths, frames, cot, taps, qkv, out_w, inner_w, outer_w, vec):
    seg, width = frames.shape
    slots = seg * 4
    local = taps.shape[1]
    hid = inner_w.shape[1]
    taps_n = taps.shape[0] // HEAD
    steps = slots // PHASES
    any_spec = pl.BlockSpec(memory_space=pl.ANY)
    vmem = pl.BlockSpec(memory_space=pltpu.VMEM)
    inputs = ["len_ref", "frames_in", "cot_in", "taps_in", "qkv_in", "out_in", "inner_in", "outer_in", "vec"]
    outs = [("output_o", (seg, width), BF16), ("frames_grad_o", (seg, width), F32)]
    grads = {
        "outer": ((hid, 128), (hid, width)),
        "inner": ((128, hid), (width, hid)),
        "out": ((local, 128), (local, width)),
        "qkv": ((128, 3 * local), (width, 3 * local)),
    }
    sums = []
    if inside:
        outs += [("small_o", (4, 16, local), F32), ("pos_o", (taps_n // 8 * HEAD, local), F32)]
        for name, (part, _) in grads.items():
            outs.append((name + "_o", part, F32))
            sums += [("g_" + name, (2, 4) + part, BF16), ("x_" + name, (4,) + part, BF16), ("z_" + name, (3,) + part, BF16)]
        sums += [
            ("xg", (8, 4, steps, 256), BF16),
            ("gt", (4, 256, 8 * steps), BF16),
            ("taken", (5, 4, 4 * steps, 256), BF16),
            ("tap_acc", (4, 2, HEAD, 12 * 128), F32),
            ("mini_t", (4, 8, local), F32),
            ("mini", (16, local), F32),
            ("mini_x", (16, local), F32),
            ("mini_s", (16, local), F32),
            ("mini_z", (3, 16, local), F32),
        ]
    else:
        outs += [("small_o", (16, width), F32), ("xflat_o", (slots, local), BF16), ("gcflat_o", (slots, local), BF16)]
        outs += [("g_" + name, whole, BF16) for name, (_, whole) in grads.items()]
    main = [("send", (2, seg, width)), ("core", (2, seg, width)), ("mid", (seg, width)), ("y", (seg, width))]
    scratch = [
        ("taps", ((taps_n + 7) * HEAD, local), BF16),
        ("w_qkv", (width, 3 * local), BF16),
        ("w_out", (local, width), BF16),
        ("w_inner", (width, hid), BF16),
        ("w_outer", (hid, width), BF16),
        ("frames_v", (seg, width), BF16),
        ("cot_full", (slots, width), BF16),
        ("x_raw", (slots, local), BF16),
        ("flat", (2, slots, 128), F32),
        ("padded", (4, 2, steps + 3 * PAD, 128), F32),
        ("shifts", (PAD, 4, steps + 2 * PAD, 256), BF16),
        ("gelu_grad", (4, steps, 256), F32),
        ("pos_send", (slots, local), BF16),
        ("pos_recv", (seg, width), BF16),
        ("s1", (seg, width), F32),
        ("full1", (slots, width), BF16),
        ("proj", (slots, 3 * local), BF16),
        ("probs", (4, slots, slots), BF16),
        ("ctx", (slots, local), BF16),
        ("keep", (seg, width), F32),
        *[("rs_" + name, shape, BF16) for name, shape in main],
        *[("rf_" + name, shape, BF16) for name, shape in main],
        ("s2", (seg, width), F32),
        ("full2", (slots, width), BF16),
        ("hidden", (slots, hid), BF16),
        ("grad_in", (slots, hid), BF16),
        ("full3", (slots, width), BF16),
        ("gctx", (slots, local), BF16),
        ("gproj", (slots, 3 * local), BF16),
        ("gscore", (2, slots, slots), BF16),
        ("grad_one", (seg, width), F32),
        ("ga_send", (seg, width), BF16),
        ("ga_recv", (slots, local), BF16),
        ("gx_send", (slots, local), BF16),
        ("gx_recv", (seg, width), BF16),
        ("small", (16, width), F32),
        *sums,
    ]
    copies = 100 if inside else 40
    names = inputs + [o[0] for o in outs] + [s[0] for s in scratch] + ["send_sem", "recv_sem", "local_sem"]
    return pl.pallas_call(
        functools.partial(layer_kernel, (slots, seg, width, local, hid, taps_n), names, inside),
        out_shape=[jax.ShapeDtypeStruct(shape, kind) for _, shape, kind in outs],
        in_specs=[pl.BlockSpec(memory_space=pltpu.SMEM)] + [any_spec] * 7 + [vmem],
        out_specs=[vmem] * len(outs),
        scratch_shapes=[pltpu.VMEM(shape, kind) for _, shape, kind in scratch]
        + [pltpu.SemaphoreType.DMA((copies,)), pltpu.SemaphoreType.DMA((copies,)), pltpu.SemaphoreType.DMA((10,))],
        compiler_params=pltpu.CompilerParams(collective_id=0, has_side_effects=True, vmem_limit_bytes=VMEM_LIMIT),
        name="layer",
    )(lengths, frames, cot, taps, qkv, out_w, inner_w, outer_w, vec)


def spread(values, full_width):
    start_col = lax.axis_index("tensor") * values.shape[-1]
    blank = jnp.zeros(values.shape[:-1] + (full_width,), jnp.float32)
    return lax.dynamic_update_slice_in_dim(blank, values, start_col, axis=values.ndim - 1)


def shards(
    frames,
    lengths,
    pos_weight,
    pos_bias,
    query_key_value_weight,
    qv_bias,
    out_weight,
    out_bias,
    norm1_gain,
    norm1_bias,
    norm2_gain,
    norm2_bias,
    inner_weight,
    inner_bias,
    outer_weight,
    outer_bias,
    cotangent,
):
    _, seg, width = frames.shape
    kernel, group_width, local = pos_weight.shape
    local_groups = local // group_width
    zero = jnp.zeros((local,), BF16)
    vec = jnp.stack(
        [
            out_bias,
            norm1_gain,
            norm1_bias,
            norm2_gain,
            norm2_bias,
            outer_bias,
            inner_bias,
            jnp.concatenate([qv_bias[0], zero, qv_bias[1], zero]),
            jnp.tile(pos_bias.reshape(local_groups, 1, group_width), (1, PHASES, 1)).reshape(-1),
        ]
        + [jnp.zeros((width,), BF16)] * 7
    ).astype(F32)
    inside = lax.axis_size("dp") == 8
    results = run_layer(
        inside,
        lengths,
        frames[0],
        cotangent[0],
        pos_weight.reshape(kernel * group_width, local),
        query_key_value_weight.reshape(width, 3 * local),
        out_weight,
        inner_weight,
        outer_weight,
        vec,
    )
    output, frames_grad, small = results[:3]
    if inside:
        pos_grad, g_outer, g_inner, g_out, g_qkv = results[3:]
        rows = [small[:, k].reshape(-1) for k in range(9)]
        return (
            output[None],
            frames_grad[None],
            pos_grad.reshape(kernel // 8, group_width, local),
            rows[6],
            g_qkv.reshape(width // 8, 3, local),
            jnp.stack([rows[7], rows[8]]),
            g_out,
            rows[0],
            rows[1],
            rows[2],
            rows[3],
            rows[4],
            g_inner,
            small[:, 9:13].reshape(-1),
            g_outer,
            rows[5],
        )
    xflat, gcflat, g_outer, g_inner, g_out, g_qkv = results[3:]
    pos_grad = lax.conv_general_dilated(
        xflat[None],
        gcflat[None],
        (1,),
        [(kernel // 2, kernel // 2 - 1)],
        dimension_numbers=("CWN", "IWO", "WNC"),
        batch_group_count=local_groups,
        preferred_element_type=jnp.float32,
    )
    summed = (
        lax.psum_scatter(pos_grad, "dp", scatter_dimension=0, tiled=True),
        lax.psum_scatter(g_qkv.reshape(width, 3, local), "dp", scatter_dimension=0, tiled=True).astype(F32),
        lax.psum_scatter(g_out, "dp", scatter_dimension=1, tiled=True).astype(F32),
        lax.psum_scatter(g_inner, "dp", scatter_dimension=0, tiled=True).astype(F32),
        lax.psum_scatter(g_outer, "dp", scatter_dimension=1, tiled=True).astype(F32),
    )
    pos_bias_part = small[6].reshape(local_groups, PHASES, group_width).sum(1).reshape(-1)
    qv_part = jnp.stack([small[7, :local], small[7, local : 2 * local]])
    total = lax.psum(
        (
            spread(pos_bias_part, width),
            spread(qv_part, width),
            small[0],
            small[1],
            small[2],
            small[3],
            small[4],
            spread(small[8], 4 * inner_bias.shape[0]),
            small[5],
        ),
        ("dp", "tensor"),
    )
    return (
        output[None],
        frames_grad[None],
        summed[0],
        total[0],
        summed[1],
        total[1],
        summed[2],
        total[2],
        total[3],
        total[4],
        total[5],
        total[6],
        summed[3],
        total[7],
        summed[4],
        total[8],
    )


def solution(mesh):
    placed = (
        P("dp", "tensor", None),
        P("dp"),
        P(None, None, "tensor"),
        P("tensor"),
        P(None, None, "tensor"),
        P(None, "tensor"),
        P("tensor", None),
        P(),
        P(),
        P(),
        P(),
        P(),
        P(None, "tensor"),
        P("tensor"),
        P("tensor", None),
        P(),
        P("dp", "tensor", None),
    )
    return jax.shard_map(
        shards,
        mesh=mesh,
        in_specs=placed,
        out_specs=(
            P("dp", "tensor", None),
            P("dp", "tensor", None),
            P("dp", None, "tensor"),
            P(),
            P("dp", None, "tensor"),
            P(),
            P("tensor", "dp"),
            P(),
            P(),
            P(),
            P(),
            P(),
            P("dp", "tensor"),
            P(),
            P("tensor", "dp"),
            P(),
        ),
        check_vma=False,
    )
```

time: 603 us -> 253 us (0.42); the launches traced: 593 us -> 253 us
  matrix products: 211 us -> 0 us
  waiting for transfers between devices: 133 us -> 0 us
  Pallas kernels: 140 us -> 229 us
  blocking collectives: 42 us -> 0 us
  local copies, waits for them, and re-layouts: 47.6 us -> 21 us
  between operations: 15.1 us -> 1.4 us
    conv_general_dilated x1 -> x0, matrix products: 211 us -> none  [shards(): lax.conv_general_dilated(channels, grad_conv, (1,), [(kernel // 2, kernel...]
    reduce_scatter x2 -> x0, waiting for transfers between devices: 132 us -> none  [the longest x1 132 us: shards(): lax.psum_scatter(pos_grad, 'dp', scatter_dimension=0, tiled=True)]
    pallas_call x1, Pallas kernels: 140 us -> 229 us  [run_layer(): pl.pallas_call(functools.partial(layer_kernel, (slots, seg, width, local,...]
    psum x1 -> x0, blocking collectives: 42 us -> none  [shards(): lax.psum((spread(pos_bias_part, width), spread(qv_part, width), small[0],...]
    conv_general_dilated x2 -> x0, local copies, waits for them, and re-layouts: 23.8 us -> none  [shards(): lax.conv_general_dilated(channels, grad_conv, (1,), [(kernel // 2, kernel...]
    unnamed x21 -> x20, local copies, waits for them, and re-layouts: 13.1 us -> 9.87 us
  transfers between devices with their start and end apart: 5 -> 0, of which waited for: 1 -> 0; matrix products, arithmetic and copies ran while one was open for 42% -> 0% of each run, Pallas kernels for 0% -> 0%
where the time goes in v2:
time: 253 us
  Pallas kernels  229 us (91%)
  local copies, waits for them, and re-layouts  21 us (8%)
    pallas_call x1, Pallas kernels, run_layer(): pl.pallas_call(functools.partial(layer_kernel, (slots, seg, width, local,...  229 us
    unnamed x20, local copies, waits for them, and re-layouts  9.87 us

profile of v2, /device:TPU:0, one launch (start us, length us, event | category | flops | bytes accessed | tf_op | source)
XLA Modules:
  0.0 252.6 jit_solution(10583418752790838722)
XLA Ops:
  1.3 0.7 tile.9
  2.0 0.8 slice_reduce_fusion.1
  2.9 0.1 tile.11
  2.9 0.7 stack.36
  3.6 0.7 stack.37
  4.3 0.7 stack.38
  5.0 0.7 stack.39
  5.7 0.7 stack.40
  6.4 0.7 stack.42
  7.1 0.7 stack.41
  7.8 0.1 stack.46
  7.9 0.6 convert_element_type.3.refs_8_
  8.5 1.7 copy.35
  10.2 1.6 copy.36.refs_4_
  11.8 229.0 %layer.1 = (bf16[128,1024]{1,0:T(8,128)(2,1)}, f32[128,1024]{1,0:T(8,128)}, f32[4,16,256]{2,1,0:T(8,128)}, f32[1024,256]{1,0:T(8,128)}, f32[1024,128]{1,0:T(8,12...) custom-call(s32[1]{0:T(128)S(6)} %copy.46.refs_0_, bf16[128,1024]{1,0:T(8,128)(2,1)} %bitcast.27, ...), custom_call_target="tpu_custom_call" | custom-call | tf_op jit(solution)/shard_map/layer/pallas_call | solution.py:818
  240.8 0.0 copy-start.3
  240.8 0.0 copy-start
  240.8 0.9 slice_bitcast_fusion
  241.7 1.9 fusion
  243.6 0.6 copy.39
  244.2 0.6 pad_maximum_fusion
  244.8 1.1 copy.37
  245.9 0.0 copy-start.4
  245.9 0.9 copy.38
  246.9 0.0 copy-start.2
  246.9 1.7 copy.47
  248.6 0.0 copy-done.3
  248.6 0.0 copy-start.1
  248.6 0.8 copy.48
  249.4 0.0 copy-done
  249.4 1.0 copy.49
  250.4 0.0 copy-done.4
  250.4 0.7 copy.50
  251.0 0.0 copy-done.2
  251.0 0.8 copy.51
  251.8 0.0 copy-done.1
  251.8 0.8 copy.52
  (7 shorter events, 0.0 us)
Async XLA Ops:
  240.8 7.8 %copy-start.3 = (f32[128,1024]{1,0:T(8,128)S(1)}, f32[128,1024]{1,0:T(8,128)}, u32[]{:S(2)}) copy-start(f32[128,1024]{1,0:T(8,128)} %get-tuple-element.25) | copy-start | bytes 1572868
  240.8 8.6 %copy-start = (f32[1024,256]{1,0:T(8,128)S(1)}, f32[1024,256]{1,0:T(8,128)}, u32[]{:S(2)}) copy-start(f32[1024,256]{1,0:T(8,128)} %get-tuple-element.26) | copy-start | bytes 3145732
  245.9 4.4 %copy-start.4 = (f32[256,128]{1,0:T(8,128)S(1)}, f32[256,128]{1,0:T(8,128)}, u32[]{:S(2)}) copy-start(f32[256,128]{1,0:T(8,128)} %get-tuple-element.97) | copy-start | bytes 393220
  246.9 4.2 %copy-start.2 = (f32[128,1024]{1,0:T(8,128)S(1)}, f32[128,1024]{1,0:T(8,128)}, u32[]{:S(2)}) copy-start(f32[128,1024]{1,0:T(8,128)} %get-tuple-element.103) | copy-start | bytes 1572868
  248.6 3.2 %copy-start.1 = (f32[1024,128]{1,0:T(8,128)S(1)}, f32[1024,128]{1,0:T(8,128)}, u32[]{:S(2)}) copy-start(f32[1024,128]{1,0:T(8,128)} %get-tuple-element.105) | copy-start | bytes 1572868

commit v3 on v2

--- a/solution.py
+++ b/solution.py
@@ -14,6 +14,7 @@
 BF16 = jnp.bfloat16
 PHASES = 4
 PAD = 16
+UNROLL = 2
 VMEM_LIMIT = 67043328
 
 
@@ -78,24 +79,46 @@
             flat[v, pl.ds(s, steps, stride=PHASES), :] = jnp.where(low, first, second)
 
 
-def tap_tile(taps, g, block):
-    v, h = g // 2, g % 2
-    columns = slice(v * 128, (v + 1) * 128)
-    low = low_half(256)
-
-    def source(s):
-        part = taps[aligned((PHASES * block - s + 3) * HEAD, 256, HEAD), columns]
-        return part if s % 2 == h else swap_halves(part)
-
-    return jnp.concatenate([jnp.where(low, source(0), source(1)), jnp.where(low, source(2), source(3))], axis=1)
-
-
-def shift_copies(padded, shifts, rows):
+def tap_tile(paired, g, block):
+    start = PHASES * block * HEAD
+    return jnp.concatenate(
+        [paired[g, aligned(start + 3 * HEAD, 256, HEAD), :], paired[g, aligned(start + HEAD, 256, HEAD), :]], axis=1
+    )
+
+
+def pair_taps(raw, taps_n, paired):
+    blank = jnp.zeros((3 * HEAD, 128), BF16)
+
+    def emit(start, count, has_low, has_high):
+        low = low_half(count)
+        none = jnp.zeros((count, 128), BF16)
+        for v in range(2):
+            lanes = slice(v * 128, (v + 1) * 128)
+            first = raw[aligned(start - 3 * HEAD, count, HEAD), lanes] if has_low else none
+            second = raw[aligned(start - 4 * HEAD, count, HEAD), lanes] if has_high else none
+            paired[2 * v, aligned(start, count, HEAD), :] = jnp.where(low, first, swap_halves(second))
+            paired[2 * v + 1, aligned(start, count, HEAD), :] = jnp.where(low, swap_halves(first), second)
+
+    for g in range(4):
+        paired[g, pl.ds(0, 3 * HEAD), :] = blank
+        paired[g, pl.ds((taps_n + 4) * HEAD, 3 * HEAD), :] = blank
+    emit(3 * HEAD, HEAD, True, False)
+    emit((taps_n + 3) * HEAD, HEAD, False, True)
+    emit((taps_n + 2) * HEAD, HEAD, True, True)
+
+    def step(i, carry):
+        emit((4 + 3 * i) * HEAD, 3 * HEAD, True, True)
+        return carry
+
+    lax.fori_loop(0, (taps_n - 2) // 3, step, 0)
+
+
+def shift_copies(padded, wide, rows):
     for g in range(4):
         for v in range(2):
 
             def one(b, carry):
-                shifts[b, g, :, v * 128 : (v + 1) * 128] = padded[g, v, pl.ds(b, rows), :].astype(BF16)
+                wide[aligned((b * 4 + g) * rows, rows, 32), v * 128 : (v + 1) * 128] = padded[g, v, pl.ds(b, rows), :].astype(BF16)
                 return carry
 
             lax.fori_loop(0, PAD, one, 0)
@@ -111,6 +134,9 @@
 class Named:
     def __init__(self, names, refs):
         self.__dict__.update(zip(names, refs, strict=True))
+
+    def get(self, name):
+        return self.__dict__[name]
 
 
 def layer_kernel(sizes, names, inside, *refs):
@@ -129,8 +155,11 @@
     x = lax.rem(row, 2)
     z = row // 2
     x_mate = row + 1 - 2 * x
-    ups = [lax.rem(z + k, 4) for k in (1, 2, 3)]
-    downs = [lax.rem(z + 4 - k, 4) for k in (1, 2, 3)]
+    z_low = lax.rem(z, 2)
+    z_high = z // 2
+    near = z + 1 - 2 * z_low
+    far = lax.rem(z + 2, 4)
+    opposite = lax.rem(near + 2, 4)
     counter = {"remote": 0, "local": 0}
     pending = {}
 
@@ -177,10 +206,10 @@
         return copy
 
     c_own = fetch(r.frames_in.at[:, columns_of(me)], r.x_raw.at[rows_of(me), :])
-    c_taps = fetch(r.taps_in, r.taps.at[pl.ds(3 * HEAD, taps_n * HEAD), :])
+    c_taps = fetch(r.taps_in, r.wide.at[pl.ds(0, taps_n * HEAD), :])
     c_frames = fetch(r.frames_in, r.frames_v)
     c_cot = fetch(r.cot_in, r.cot_full.at[rows_of(me), :])
-    c_qkv = fetch(r.qkv_in, r.w_qkv)
+    c_qkv = [fetch(r.qkv_in.at[part], r.w_qkv.at[:, pl.ds(part * local, local)]) for part in range(3)]
     c_out = fetch(r.out_in, r.w_out)
     c_inner = fetch(r.inner_in, r.w_inner)
     c_outer = fetch(r.outer_in, r.w_outer)
@@ -188,7 +217,7 @@
     barrier = pltpu.get_barrier_semaphore()
     greet = [("tensor", p) for p in peers]
     if inside:
-        greet += [("dp", x_mate)] + [("dp", 2 * k + x) for k in ups]
+        greet += [("dp", x_mate)] + [("dp", 2 * k + x) for k in (near, far)]
     for axis, peer in greet:
         pl.semaphore_signal(barrier, inc=1, device_id={axis: peer}, device_id_type=pl.DeviceIdType.MESH)
     pl.semaphore_wait(barrier, len(greet))
@@ -196,52 +225,89 @@
     i_frames = [send(r.frames_in.at[:, columns_of(p)], r.x_raw.at[rows_of(me), :], p) for p in peers]
     i_cot = [send(r.cot_in, r.cot_full.at[rows_of(me), :], p) for p in (mate, across)]
 
-    r.taps[pl.ds(0, 3 * HEAD), :] = jnp.zeros((3 * HEAD, local), BF16)
-    r.taps[pl.ds((3 + taps_n) * HEAD, 4 * HEAD), :] = jnp.zeros((4 * HEAD, local), BF16)
     for g in range(4):
         for v in range(2):
             r.padded[g, v, pl.ds(0, PAD), :] = jnp.zeros((PAD, 128), F32)
             r.padded[g, v, pl.ds(PAD + steps, 2 * PAD), :] = jnp.zeros((2 * PAD, 128), F32)
     r.small[...] = jnp.zeros_like(r.small)
+    for k in range(7):
+        r.vec[pl.ds(k, 1), :] = r.get("v" + str(k))[...].astype(F32).reshape(1, width)
+    r.vec[pl.ds(7, 1), :] = jnp.zeros((1, width), F32)
+    r.vec[pl.ds(7, 1), 0:local] = r.qv_in[0:1, :].astype(F32)
+    r.vec[pl.ds(7, 1), 2 * local : 3 * local] = r.qv_in[1:2, :].astype(F32)
+    pos_bias = r.pos_in[...].astype(F32).reshape(1, local)
+    for g in range(4):
+        v, h = g // 2, g % 2
+        half = jnp.broadcast_to(pos_bias[:, v * 128 : (v + 1) * 128], (8, 128))
+        other = swap_halves(half)
+        both = (jnp.where(low_half(8), half, other) if h == 0 else jnp.where(low_half(8), other, half))[0:1]
+        r.vec[pl.ds(8, 1), g * 256 : (g + 1) * 256] = jnp.concatenate([both, both], axis=1)
+    c_taps.wait()
+    pair_taps(r.wide, taps_n, r.paired)
 
     def dp_gather(slot):
-        ids = [send(slot(row), slot(row), 2 * k + x, "dp") for k in ups]
-        return ids, [send(slot(row), slot(row), x_mate, "dp")]
+        return [send(slot(row), slot(row), peer, "dp") for peer in (2 * far + x, 2 * near + x, x_mate)]
 
     def dp_relay(ids, slot):
-        for index, k in zip(ids[0], downs):
-            arrive(index, slot(2 * k + x))
-            ids[1].append(send(slot(2 * k + x), slot(2 * k + x), x_mate, "dp"))
+        got = slot(2 * far + x)
+        arrive(ids[0], got)
+        ids.append(send(got, got, 2 * near + x, "dp"))
+        ids.append(send(got, got, x_mate, "dp"))
+        got = slot(2 * near + x)
+        arrive(ids[1], got)
+        ids.append(send(got, got, x_mate, "dp"))
+
+    def dp_relay_last(ids, slot):
+        got = slot(2 * opposite + x)
+        arrive(ids[3], got)
+        ids.append(send(got, got, x_mate, "dp"))
 
     def dp_gathered(ids, slot):
-        for index, k in zip(ids[1], [z] + downs):
+        for index, k in zip((ids[2], ids[4], ids[5], ids[6]), (z, far, near, opposite)):
             arrive(index, slot(2 * k + 1 - x))
 
-    def dp_first(buf, from_x):
-        return [send(buf.at[1 - x], from_x, x_mate, "dp")]
-
-    def dp_second(ids, buf, from_x, from_z):
+    def dp_first(name):
+        return [send(r.get("g_" + name).at[1 - x], r.get("x_" + name), x_mate, "dp")]
+
+    def dp_second(ids, name):
+        buf, from_x = r.get("g_" + name), r.get("x_" + name)
         arrive(ids[0], from_x)
 
-        def add(k, carry):
-            buf[x, k] = (buf[x, k].astype(F32) + from_x[k].astype(F32)).astype(BF16)
-            return carry
-
-        lax.fori_loop(0, 4, add, 0)
-        for slot, k in enumerate(ups):
-            ids.append(send(buf.at[x, k], from_z.at[slot], 2 * k + x, "dp"))
-
-    def dp_third(ids, buf, from_z, out):
-        total = buf[x, z].astype(F32)
-        for slot in range(3):
-            arrive(ids[1 + slot], from_z.at[slot])
-            total = total + from_z[slot].astype(F32)
-        out[...] = total
+        def add_pair(half):
+            def add(k, carry):
+                buf[x, half, k] = (buf[x, half, k].astype(F32) + from_x[half, k].astype(F32)).astype(BF16)
+                return carry
+
+            lax.fori_loop(0, 2, add, 0)
+
+        add_pair(1 - z_low)
+        ids.append(send(buf.at[x, 1 - z_low], r.get("z_" + name).at[pl.ds(0, 2)], 2 * near + x, "dp"))
+        add_pair(z_low)
+
+    def dp_third(ids, name):
+        buf, from_z = r.get("g_" + name), r.get("z_" + name)
+        arrive(ids[1], from_z.at[pl.ds(0, 2)])
+        given = 1 - z_high
+        buf[x, z_low, given] = (buf[x, z_low, given].astype(F32) + from_z[given].astype(F32)).astype(BF16)
+        ids.append(send(buf.at[x, z_low, given], from_z.at[2], 2 * far + x, "dp"))
+
+    def dp_last(ids, name):
+        buf, from_z, out = r.get("g_" + name), r.get("z_" + name), r.get(name + "_o")
+        arrive(ids[2], from_z.at[2])
+        total = buf[x, z_low, z_high].astype(F32) + from_z[z_high].astype(F32) + from_z[2].astype(F32)
+        if name == "qkv":
+            for part in range(3):
+                out[part] = total[:, part * local : (part + 1) * local]
+        else:
+            out[...] = total
 
     length = r.len_ref[0]
     c_own.wait()
     for index, p in zip(i_frames, peers):
         arrive(index, r.x_raw.at[rows_of(p), :])
+
+    def xg_slot(e):
+        return r.xg.at[e]
 
     live_all = lax.broadcasted_iota(jnp.int32, (slots, 128), 0) < length
     for v in range(2):
@@ -252,25 +318,31 @@
         for g in range(4):
             for v in range(2):
                 r.xg[row, g, :, v * 128 : (v + 1) * 128] = phased[g][v].astype(BF16)
-        ids_x = dp_gather(lambda e: r.xg.at[e])
+        ids_x = dp_gather(xg_slot)
     else:
         r.xflat_o[...] = jnp.concatenate([r.flat[0], r.flat[1]], axis=1).astype(BF16)
-    shift_copies(r.padded, r.shifts, steps + 2 * PAD)
-    c_taps.wait()
+    shift_copies(r.padded, r.wide, steps + 2 * PAD)
 
     def shifted(g, low_part, high_part):
-        return r.shifts[low_part, g, pl.ds(high_part * PAD, steps), :]
+        return r.wide[aligned((low_part * 4 + g) * (steps + 2 * PAD) + high_part * PAD, steps, PAD), :]
+
+    def block_sum(g, flip):
+        def products(pairs):
+            left = jnp.concatenate([shifted(g, low, high) for low, high in pairs], axis=1)
+            if flip:
+                tiles = [tap_tile(r.paired, g, blocks - (low + PAD * high)) for low, high in pairs]
+                return nt(left, jnp.concatenate(tiles, axis=1))
+            tiles = [tap_tile(r.paired, g, low + PAD * high) for low, high in pairs]
+            return nn(left, jnp.concatenate(tiles, axis=0))
+
+        def step(b, total):
+            return total + products([(UNROLL * b + i, high) for i in range(UNROLL) for high in range(2)])
+
+        return lax.fori_loop(0, PAD // UNROLL, step, products([(0, 2)]))
 
     pos_groups = []
     for g in range(4):
-
-        def forward(b, total):
-            for high in range(2):
-                total = total + nn(shifted(g, b, high), tap_tile(r.taps, g, b + PAD * high))
-            return total
-
-        total = nn(shifted(g, 0, 2), tap_tile(r.taps, g, blocks))
-        total = lax.fori_loop(0, PAD, forward, total)
+        total = block_sum(g, False)
         value, slope = gelu_pair(total + r.vec[pl.ds(8, 1), g * 256 : (g + 1) * 256])
         r.gelu_grad[g] = slope
         pos_groups.append((value[:, :128], value[:, 128:]))
@@ -325,7 +397,8 @@
     far_pair = aligned(lax.rem(me - core + 2, 4) * seg, 2 * seg, 2 * seg)
 
     ids1 = gather_start(r.full1)
-    c_qkv.wait()
+    for copy in c_qkv:
+        copy.wait()
 
     def project(rows):
         for part in range(3):
@@ -415,7 +488,7 @@
     ids_a = scatter_start(attended, main_bufs)
     scatter_own(attended)
     if inside:
-        dp_relay(ids_x, lambda e: r.xg.at[e])
+        dp_relay(ids_x, xg_slot)
     scatter_end(ids_a, main_bufs)
 
     def norm_two(b):
@@ -446,6 +519,8 @@
     arrive(ids2[0], r.full2.at[rows_of(mate), :])
     feed(pair)
     gather_relay(ids2, r.full2)
+    if inside:
+        dp_relay_last(ids_x, xg_slot)
     arrive(ids2[2], r.full2.at[rows_of(diag), :])
     feed(far_pair)
 
@@ -463,7 +538,7 @@
         for k in range(4):
             for j in range(2):
                 start = (2 * k + j) * 128
-                dst[j, k, rows, :] = value[:, start : start + 128].astype(BF16)
+                dst[j, k % 2, k // 2, rows, :] = value[:, start : start + 128].astype(BF16)
 
     def outer_tile(rows):
         value = tn(r.hidden[:, rows], r.cot_full[...])
@@ -477,8 +552,8 @@
             rows = aligned(b * 256, 256, 256)
             value = tn(left[:, rows], right[...])
             if inside:
-                dst[0, b] = value[:128].astype(BF16)
-                dst[1, b] = value[128:].astype(BF16)
+                dst[0, lax.rem(b, 2), b // 2] = value[:128].astype(BF16)
+                dst[1, lax.rem(b, 2), b // 2] = value[128:].astype(BF16)
             else:
                 dst[rows, :] = value.astype(BF16)
             return carry
@@ -487,7 +562,7 @@
 
     tiles(hid, outer_tile)
     if inside:
-        ids_outer = dp_first(r.g_outer, r.x_outer)
+        ids_outer = dp_first("outer")
     scatter_end(ids_b, main_bufs)
 
     def put_sum(k, value):
@@ -515,7 +590,7 @@
 
     grouped_rows(r.g_inner, r.full2, r.grad_in)
     if inside:
-        ids_inner = dp_first(r.g_inner, r.x_inner)
+        ids_inner = dp_first("inner")
     gather_relay(ids3, r.full3)
     ids_f = scatter_start(branch_part, ff_bufs)
 
@@ -525,7 +600,7 @@
     g_out = tn(r.ctx[...], r.full3[...])
     if inside:
         store_columns(r.g_out, pl.ds(0, local), g_out)
-        ids_out = dp_first(r.g_out, r.x_out)
+        ids_out = dp_first("out")
     else:
         r.g_out[...] = g_out.astype(BF16)
 
@@ -548,6 +623,8 @@
         r.gproj[:, local + hp * 128 : local + (hp + 1) * 128] = (jnp.concatenate(gk, axis=1) * scale).astype(BF16)
         gv = [tn(r.probs[2 * hp + j], r.gctx[:, head_columns(0, 2 * hp + j)]) for j in range(2)]
         r.gproj[:, 2 * local + hp * 128 : 2 * local + (hp + 1) * 128] = jnp.concatenate(gv, axis=1).astype(BF16)
+        if inside and hp == 0:
+            dp_second(ids_outer, "outer")
 
     def grad_one_part(owner, columns):
         return nt(r.gproj[rows_of(owner), :], r.w_qkv[columns, :])
@@ -557,7 +634,7 @@
     scatter_own(grad_one_part)
     grouped_rows(r.g_qkv, r.full1, r.gproj)
     if inside:
-        ids_qkv = dp_first(r.g_qkv, r.x_qkv)
+        ids_qkv = dp_first("qkv")
     scatter_end(ids_c, main_bufs)
 
     def back_one(b):
@@ -571,7 +648,7 @@
     r.ga_recv[rows_of(me), :] = r.ga_send[:, columns_of(me)]
 
     if inside:
-        dp_second(ids_outer, r.g_outer, r.x_outer, r.z_outer)
+        dp_third(ids_outer, "outer")
 
     scatter_own(branch_part)
     scatter_end(ids_f, ff_bufs)
@@ -608,24 +685,26 @@
         return r.gt.at[:, :, aligned(e * steps, steps, steps)]
 
     store_padded(grads, r.padded)
+    between = [lambda: None] * 4
     if inside:
         ids_g = dp_gather(gt_slot)
+        dp_second(ids_inner, "inner")
+        between = [
+            lambda: dp_second(ids_out, "out"),
+            lambda: dp_third(ids_inner, "inner"),
+            lambda: dp_relay(ids_g, gt_slot),
+            lambda: dp_third(ids_out, "out"),
+        ]
         i_mini = [send(r.small.at[pl.ds(0, 8), columns_of(p)], r.mini_t.at[me], p) for p in peers]
         r.mini_t[me] = r.small[pl.ds(0, 8), columns_of(me)]
     else:
         join_phases(grads, r.flat)
         r.gcflat_o[...] = jnp.concatenate([r.flat[0], r.flat[1]], axis=1).astype(BF16)
-    shift_copies(r.padded, r.shifts, steps + 2 * PAD)
+    shift_copies(r.padded, r.wide, steps + 2 * PAD)
     in_groups = []
     for g in range(4):
-
-        def backward(b, total):
-            for high in range(2):
-                total = total + nt(shifted(g, b, high), tap_tile(r.taps, g, blocks - (b + PAD * high)))
-            return total
-
-        total = nt(shifted(g, 0, 2), tap_tile(r.taps, g, 0))
-        total = lax.fori_loop(0, PAD, backward, total)
+        total = block_sum(g, True)
+        between[g]()
         in_groups.append((total[:, :128], total[:, 128:]))
     join_phases(in_groups, r.flat)
     r.gx_send[...] = jnp.concatenate([r.flat[0], r.flat[1]], axis=1).astype(BF16)
@@ -633,8 +712,7 @@
     r.gx_recv[:, columns_of(me)] = r.gx_send[rows_of(me), :]
 
     if inside:
-        dp_second(ids_inner, r.g_inner, r.x_inner, r.z_inner)
-        dp_second(ids_out, r.g_out, r.x_out, r.z_out)
+        dp_relay_last(ids_g, gt_slot)
 
         for index, p in zip(i_mini, peers):
             arrive(index, r.mini_t.at[p])
@@ -656,12 +734,14 @@
         r.mini[pl.ds(13, 3), :] = jnp.zeros((3, 256), F32)
         i_mx = send(r.mini, r.mini_x, x_mate, "dp")
 
-        dp_second(ids_qkv, r.g_qkv, r.x_qkv, r.z_qkv)
         arrive(i_mx, r.mini_x)
         r.mini_s[...] = r.mini[...] + r.mini_x[...]
-        i_mz = [send(r.mini_s, r.mini_z.at[slot], 2 * k + x, "dp") for slot, k in enumerate(ups)]
-        dp_relay(ids_g, gt_slot)
-        dp_gathered(ids_x, lambda e: r.xg.at[e])
+        i_mz = [send(r.mini_s, r.mini_z.at[0], 2 * near + x, "dp")]
+        dp_second(ids_qkv, "qkv")
+        arrive(i_mz[0], r.mini_z.at[0])
+        r.mini_z[2] = r.mini_s[...] + r.mini_z[0]
+        i_mz.append(send(r.mini_z.at[2], r.mini_z.at[1], 2 * far + x, "dp"))
+        dp_gathered(ids_x, xg_slot)
 
     for index, p in zip(i_gx, peers):
         arrive(index, r.gx_recv.at[:, columns_of(p)])
@@ -673,9 +753,8 @@
     each_chunk(frames_back)
 
     if inside:
-        for slot in range(3):
-            arrive(i_mz[slot], r.mini_z.at[slot])
-        r.small_o[me] = r.mini_s[...] + r.mini_z[0] + r.mini_z[1] + r.mini_z[2]
+        arrive(i_mz[1], r.mini_z.at[1])
+        r.small_o[me] = r.mini_z[2] + r.mini_z[1]
         i_mt = [send(r.small_o.at[me], r.small_o.at[me], p) for p in peers]
 
         reach = 5
@@ -693,14 +772,15 @@
                         for v in range(2):
                             lanes = slice(v * 128, (v + 1) * 128)
                             moved = r.padded[g, v, pl.ds(row * (count // PHASES) + a, steps), :]
-                            r.taken[a, g, k * steps : (k + 1) * steps, lanes] = moved.astype(BF16)
+                            start = ((a * 4 + g) * 4 + k) * steps
+                            r.wide[start : start + steps, lanes] = moved.astype(BF16)
 
         def accumulate(column, first):
             def one(index, carry):
                 g = index // reach
                 a = index % reach
                 left = jnp.concatenate([r.gt[g, :, aligned((2 * k + column) * steps, steps, steps)] for k in range(4)], axis=1)
-                value = nn(left, r.taken[a, g])
+                value = nn(left, r.wide[aligned((a * 4 + g) * 4 * steps, 4 * steps, steps), :])
                 for s in range(PHASES):
                     parity = s % 2
                     start = (PHASES * a - s + 3 + (1 - parity)) * HEAD
@@ -713,6 +793,7 @@
         r.tap_acc[...] = jnp.zeros_like(r.tap_acc)
         build(x)
         accumulate(x, True)
+        dp_third(ids_qkv, "qkv")
         build(1 - x)
         dp_gathered(ids_g, gt_slot)
         accumulate(1 - x, False)
@@ -725,10 +806,10 @@
                 both.append(even + odd)
             r.pos_o[:, v * 128 : (v + 1) * 128] = jnp.concatenate(both, axis=0).T
 
-        dp_third(ids_outer, r.g_outer, r.z_outer, r.outer_o)
-        dp_third(ids_inner, r.g_inner, r.z_inner, r.inner_o)
-        dp_third(ids_out, r.g_out, r.z_out, r.out_o)
-        dp_third(ids_qkv, r.g_qkv, r.z_qkv, r.qkv_o)
+        dp_last(ids_outer, "outer")
+        dp_last(ids_inner, "inner")
+        dp_last(ids_out, "out")
+        dp_last(ids_qkv, "qkv")
         for index, p in zip(i_mt, peers):
             arrive(index, r.small_o.at[p])
     else:
@@ -736,7 +817,7 @@
     sent(list(pending))
 
 
-def run_layer(inside, lengths, frames, cot, taps, qkv, out_w, inner_w, outer_w, vec):
+def run_layer(inside, lengths, frames, cot, taps, qkv, out_w, inner_w, outer_w, vectors):
     seg, width = frames.shape
     slots = seg * 4
     local = taps.shape[1]
@@ -745,7 +826,8 @@
     steps = slots // PHASES
     any_spec = pl.BlockSpec(memory_space=pl.ANY)
     vmem = pl.BlockSpec(memory_space=pltpu.VMEM)
-    inputs = ["len_ref", "frames_in", "cot_in", "taps_in", "qkv_in", "out_in", "inner_in", "outer_in", "vec"]
+    inputs = ["len_ref", "frames_in", "cot_in", "taps_in", "qkv_in", "out_in", "inner_in", "outer_in"]
+    inputs += ["v" + str(k) for k in range(7)] + ["qv_in", "pos_in"]
     outs = [("output_o", (seg, width), BF16), ("frames_grad_o", (seg, width), F32)]
     grads = {
         "outer": ((hid, 128), (hid, width)),
@@ -757,12 +839,11 @@
     if inside:
         outs += [("small_o", (4, 16, local), F32), ("pos_o", (taps_n // 8 * HEAD, local), F32)]
         for name, (part, _) in grads.items():
-            outs.append((name + "_o", part, F32))
-            sums += [("g_" + name, (2, 4) + part, BF16), ("x_" + name, (4,) + part, BF16), ("z_" + name, (3,) + part, BF16)]
+            outs.append((name + "_o", (3, part[0], local) if name == "qkv" else part, F32))
+            sums += [("g_" + name, (2, 2, 2) + part, BF16), ("x_" + name, (2, 2) + part, BF16), ("z_" + name, (3,) + part, BF16)]
         sums += [
             ("xg", (8, 4, steps, 256), BF16),
             ("gt", (4, 256, 8 * steps), BF16),
-            ("taken", (5, 4, 4 * steps, 256), BF16),
             ("tap_acc", (4, 2, HEAD, 12 * 128), F32),
             ("mini_t", (4, 8, local), F32),
             ("mini", (16, local), F32),
@@ -775,7 +856,7 @@
         outs += [("g_" + name, whole, BF16) for name, (_, whole) in grads.items()]
     main = [("send", (2, seg, width)), ("core", (2, seg, width)), ("mid", (seg, width)), ("y", (seg, width))]
     scratch = [
-        ("taps", ((taps_n + 7) * HEAD, local), BF16),
+        ("paired", (4, (taps_n + 7) * HEAD, 128), BF16),
         ("w_qkv", (width, 3 * local), BF16),
         ("w_out", (local, width), BF16),
         ("w_inner", (width, hid), BF16),
@@ -785,7 +866,7 @@
         ("x_raw", (slots, local), BF16),
         ("flat", (2, slots, 128), F32),
         ("padded", (4, 2, steps + 3 * PAD, 128), F32),
-        ("shifts", (PAD, 4, steps + 2 * PAD, 256), BF16),
+        ("wide", (PAD * 4 * (steps + 2 * PAD), 256), BF16),
         ("gelu_grad", (4, steps, 256), F32),
         ("pos_send", (slots, local), BF16),
         ("pos_recv", (seg, width), BF16),
@@ -811,6 +892,7 @@
         ("gx_send", (slots, local), BF16),
         ("gx_recv", (seg, width), BF16),
         ("small", (16, width), F32),
+        ("vec", (16, width), F32),
         *sums,
     ]
     copies = 100 if inside else 40
@@ -818,13 +900,56 @@
     return pl.pallas_call(
         functools.partial(layer_kernel, (slots, seg, width, local, hid, taps_n), names, inside),
         out_shape=[jax.ShapeDtypeStruct(shape, kind) for _, shape, kind in outs],
-        in_specs=[pl.BlockSpec(memory_space=pltpu.SMEM)] + [any_spec] * 7 + [vmem],
+        in_specs=[pl.BlockSpec(memory_space=pltpu.SMEM)] + [any_spec] * 7 + [vmem] * 9,
         out_specs=[vmem] * len(outs),
         scratch_shapes=[pltpu.VMEM(shape, kind) for _, shape, kind in scratch]
-        + [pltpu.SemaphoreType.DMA((copies,)), pltpu.SemaphoreType.DMA((copies,)), pltpu.SemaphoreType.DMA((10,))],
+        + [pltpu.SemaphoreType.DMA((copies,)), pltpu.SemaphoreType.DMA((copies,)), pltpu.SemaphoreType.DMA((16,))],
         compiler_params=pltpu.CompilerParams(collective_id=0, has_side_effects=True, vmem_limit_bytes=VMEM_LIMIT),
         name="layer",
-    )(lengths, frames, cot, taps, qkv, out_w, inner_w, outer_w, vec)
+    )(lengths, frames, cot, taps, qkv, out_w, inner_w, outer_w, *vectors)
+
+
+def finish_kernel(count, *refs):
+    ins, small = refs[:count], refs[count]
+    outs, bias = refs[count + 1 : 2 * count + 1], refs[2 * count + 1 : 2 * count + 10]
+    staged, sems = refs[2 * count + 10 : -1], refs[-1]
+    loads = [pltpu.make_async_copy(a, b, sems.at[k]) for k, (a, b) in enumerate(zip(ins, staged))]
+    stores = [pltpu.make_async_copy(a, b, sems.at[count + k]) for k, (a, b) in enumerate(zip(staged, outs))]
+    for copy in loads:
+        copy.start()
+    for load, store in zip(loads, stores):
+        load.wait()
+        store.start()
+    local = small.shape[2]
+    for t in range(small.shape[0]):
+        for k in range(7):
+            bias[k][0:1, t * local : (t + 1) * local] = small[t, pl.ds(k, 1), :]
+        for k in range(2):
+            bias[7][pl.ds(k, 1), t * local : (t + 1) * local] = small[t, pl.ds(7 + k, 1), :]
+        for k in range(4):
+            start = (4 * t + k) * local
+            bias[8][0:1, start : start + local] = small[t, pl.ds(9 + k, 1), :]
+    for store in stores:
+        store.wait()
+
+
+def finish(arrays, small):
+    any_spec = pl.BlockSpec(memory_space=pl.ANY)
+    vmem = pl.BlockSpec(memory_space=pltpu.VMEM)
+    width = small.shape[0] * small.shape[2]
+    shapes = [jax.ShapeDtypeStruct(a.shape, a.dtype) for a in arrays]
+    shapes += [jax.ShapeDtypeStruct((1, width), F32)] * 7
+    shapes += [jax.ShapeDtypeStruct((2, width), F32), jax.ShapeDtypeStruct((1, 4 * width), F32)]
+    results = pl.pallas_call(
+        functools.partial(finish_kernel, len(arrays)),
+        out_shape=shapes,
+        in_specs=[any_spec] * len(arrays) + [vmem],
+        out_specs=[any_spec] * len(arrays) + [vmem] * 9,
+        scratch_shapes=[pltpu.VMEM(a.shape, a.dtype) for a in arrays] + [pltpu.SemaphoreType.DMA((2 * len(arrays),))],
+        compiler_params=pltpu.CompilerParams(vmem_limit_bytes=VMEM_LIMIT),
+        name="finish",
+    )(*arrays, small)
+    return results[: len(arrays)], results[len(arrays) :]
 
 
 def spread(values, full_width):
@@ -855,21 +980,7 @@
     _, seg, width = frames.shape
     kernel, group_width, local = pos_weight.shape
     local_groups = local // group_width
-    zero = jnp.zeros((local,), BF16)
-    vec = jnp.stack(
-        [
-            out_bias,
-            norm1_gain,
-            norm1_bias,
-            norm2_gain,
-            norm2_bias,
-            outer_bias,
-            inner_bias,
-            jnp.concatenate([qv_bias[0], zero, qv_bias[1], zero]),
-            jnp.tile(pos_bias.reshape(local_groups, 1, group_width), (1, PHASES, 1)).reshape(-1),
-        ]
-        + [jnp.zeros((width,), BF16)] * 7
-    ).astype(F32)
+    vectors = [out_bias, norm1_gain, norm1_bias, norm2_gain, norm2_bias, outer_bias, inner_bias, qv_bias, pos_bias]
     inside = lax.axis_size("dp") == 8
     results = run_layer(
         inside,
@@ -877,23 +988,25 @@
         frames[0],
         cotangent[0],
         pos_weight.reshape(kernel * group_width, local),
-        query_key_value_weight.reshape(width, 3 * local),
+        query_key_value_weight.transpose(1, 0, 2),
         out_weight,
         inner_weight,
         outer_weight,
-        vec,
+        vectors,
     )
     output, frames_grad, small = results[:3]
     if inside:
         pos_grad, g_outer, g_inner, g_out, g_qkv = results[3:]
-        rows = [small[:, k].reshape(-1) for k in range(9)]
+        arrays = [output, frames_grad, pos_grad, g_outer, g_inner, g_out, g_qkv]
+        (output, frames_grad, pos_grad, g_outer, g_inner, g_out, g_qkv), bias = finish(arrays, small)
+        rows = [b.reshape(-1) for b in bias[:7]]
         return (
             output[None],
             frames_grad[None],
             pos_grad.reshape(kernel // 8, group_width, local),
             rows[6],
-            g_qkv.reshape(width // 8, 3, local),
-            jnp.stack([rows[7], rows[8]]),
+            g_qkv.transpose(1, 0, 2),
+            bias[7],
             g_out,
             rows[0],
             rows[1],
@@ -901,7 +1014,7 @@
             rows[3],
             rows[4],
             g_inner,
-            small[:, 9:13].reshape(-1),
+            bias[8].reshape(-1),
             g_outer,
             rows[5],
         )

time: 253 us -> 209 us (0.83)
  Pallas kernels: 229 us -> 208 us
  local copies, waits for them, and re-layouts: 21 us -> 0 us
    pallas_call x1, Pallas kernels: 229 us -> 203 us  [run_layer(): pl.pallas_call(functools.partial(layer_kernel, (slots, seg, width, local,...]
    unnamed x20 -> x0, local copies, waits for them, and re-layouts: 9.87 us -> none
    another operation x15 -> x0, local copies, waits for them, and re-layouts: 5.74 us -> none  [the longest x12 4.92 us: shards(): jnp.stack([out_bias, norm1_gain, norm1_bias, norm2_gain, norm2_bias, oute...]
    pallas_call x0 -> x1, Pallas kernels: none -> 4.56 us  [finish(): pl.pallas_call(functools.partial(finish_kernel, len(arrays)), out_shape=s...]
    slice x2 -> x0, local copies, waits for them, and re-layouts: 2.64 us -> none  [the longest x1 1.87 us: shards(): rows = [small[:, k].reshape(-1) for k in range(9)]]
where the time goes in v3:
time: 209 us
  Pallas kernels  208 us (100%)
    pallas_call x1, Pallas kernels, run_layer(): pl.pallas_call(functools.partial(layer_kernel, (slots, seg, width, local,...  203 us
    pallas_call x1, Pallas kernels, finish(): pl.pallas_call(functools.partial(finish_kernel, len(arrays)), out_shape=s...  4.56 us

profile of v3, /device:TPU:0, one launch (start us, length us, event | category | flops | bytes accessed | tf_op | source)
XLA Modules:
  0.0 209.0 jit_solution(16817583285445892672)
XLA Ops:
  1.3 203.0 %layer.1 = (bf16[128,1024]{1,0:T(8,128)(2,1)}, f32[128,1024]{1,0:T(8,128)}, f32[4,16,256]{2,1,0:T(8,128)}, f32[1024,256]{1,0:T(8,128)}, f32[1024,128]{1,0:T(8,12...) custom-call(s32[1]{0:T(128)S(6)} %copy.33.refs_0_, bf16[128,1024]{1,0:T(8,128)(2,1)} %bitcast.18, ...), custom_call_target="tpu_custom_call" | custom-call | tf_op jit(solution)/shard_map/layer/pallas_call | solution.py:900
  204.3 4.6 %finish.1 = (bf16[128,1024]{1,0:T(8,128)(2,1)}, f32[128,1024]{1,0:T(8,128)}, f32[1024,256]{1,0:T(8,128)}, f32[1024,128]{1,0:T(8,128)}, f32[128,1024]{1,0:T(8,128...) custom-call(bf16[128,1024]{1,0:T(8,128)(2,1)} %get-tuple-element.40., ...), custom_call_target="tpu_custom_call" | custom-call | tf_op jit(solution)/shard_map/finish/pallas_call | solution.py:943

commit v4 on v3

--- a/solution.py
+++ b/solution.py
@@ -15,6 +15,7 @@
 PHASES = 4
 PAD = 16
 UNROLL = 2
+PAIR_STEP = 2
 VMEM_LIMIT = 67043328
 
 
@@ -89,28 +90,34 @@
 def pair_taps(raw, taps_n, paired):
     blank = jnp.zeros((3 * HEAD, 128), BF16)
 
-    def emit(start, count, has_low, has_high):
-        low = low_half(count)
-        none = jnp.zeros((count, 128), BF16)
+    low = low_half(HEAD)
+    none = jnp.zeros((HEAD, 128), BF16)
+
+    def emit(row, now, before):
         for v in range(2):
-            lanes = slice(v * 128, (v + 1) * 128)
-            first = raw[aligned(start - 3 * HEAD, count, HEAD), lanes] if has_low else none
-            second = raw[aligned(start - 4 * HEAD, count, HEAD), lanes] if has_high else none
-            paired[2 * v, aligned(start, count, HEAD), :] = jnp.where(low, first, swap_halves(second))
-            paired[2 * v + 1, aligned(start, count, HEAD), :] = jnp.where(low, swap_halves(first), second)
+            first, first_moved = now[2 * v : 2 * v + 2]
+            second, second_moved = before[2 * v : 2 * v + 2]
+            paired[2 * v, aligned(row, HEAD, HEAD), :] = jnp.where(low, first, second_moved)
+            paired[2 * v + 1, aligned(row, HEAD, HEAD), :] = jnp.where(low, first_moved, second)
 
     for g in range(4):
         paired[g, pl.ds(0, 3 * HEAD), :] = blank
         paired[g, pl.ds((taps_n + 4) * HEAD, 3 * HEAD), :] = blank
-    emit(3 * HEAD, HEAD, True, False)
-    emit((taps_n + 3) * HEAD, HEAD, False, True)
-    emit((taps_n + 2) * HEAD, HEAD, True, True)
-
-    def step(i, carry):
-        emit((4 + 3 * i) * HEAD, 3 * HEAD, True, True)
-        return carry
-
-    lax.fori_loop(0, (taps_n - 2) // 3, step, 0)
+
+    def step(i, before):
+        for k in range(PAIR_STEP):
+            block = PAIR_STEP * i + k
+            rows = aligned(block * HEAD, HEAD, HEAD)
+            now = []
+            for v in range(2):
+                part = raw[rows, v * 128 : (v + 1) * 128]
+                now += [part, swap_halves(part)]
+            emit((block + 3) * HEAD, now, before)
+            before = now
+        return tuple(before)
+
+    last = lax.fori_loop(0, taps_n // PAIR_STEP, step, (none,) * 4)
+    emit((taps_n + 3) * HEAD, (none,) * 4, last)
 
 
 def shift_copies(padded, wide, rows):
@@ -246,60 +253,68 @@
     pair_taps(r.wide, taps_n, r.paired)
 
     def dp_gather(slot):
-        return [send(slot(row), slot(row), peer, "dp") for peer in (2 * far + x, 2 * near + x, x_mate)]
+        return [send(slot(z), slot(z), 2 * peer + x, "dp") for peer in (far, near)]
 
     def dp_relay(ids, slot):
-        got = slot(2 * far + x)
+        arrive(ids[0], slot(far))
+        ids.append(send(slot(far), slot(far), 2 * near + x, "dp"))
+        arrive(ids[1], slot(near))
+
+    def dp_relay_last(ids, slot):
+        arrive(ids[2], slot(opposite))
+
+    x_order = ((x, x_mate), (z_low, 2 * near + x), (z_high, 2 * far + x))
+    z_order = (x_order[1], x_order[2], x_order[0])
+    orders = {"outa": x_order, "outb": z_order, "inner": x_order, "out": x_order, "qkv": x_order}
+    sum_ids = {}
+
+    def dp_first(name):
+        (bit, peer), _, _ = orders[name]
+        sum_ids[name] = [send(r.get("g_" + name).at[1 - bit], r.get("x_" + name), peer, "dp")]
+
+    def dp_second(name):
+        buf, got, ids = r.get("g_" + name), r.get("x_" + name), sum_ids[name]
+        (bit, _), (other, peer), _ = orders[name]
         arrive(ids[0], got)
-        ids.append(send(got, got, 2 * near + x, "dp"))
-        ids.append(send(got, got, x_mate, "dp"))
-        got = slot(2 * near + x)
-        arrive(ids[1], got)
-        ids.append(send(got, got, x_mate, "dp"))
-
-    def dp_relay_last(ids, slot):
-        got = slot(2 * opposite + x)
-        arrive(ids[3], got)
-        ids.append(send(got, got, x_mate, "dp"))
-
-    def dp_gathered(ids, slot):
-        for index, k in zip((ids[2], ids[4], ids[5], ids[6]), (z, far, near, opposite)):
-            arrive(index, slot(2 * k + 1 - x))
-
-    def dp_first(name):
-        return [send(r.get("g_" + name).at[1 - x], r.get("x_" + name), x_mate, "dp")]
-
-    def dp_second(ids, name):
-        buf, from_x = r.get("g_" + name), r.get("x_" + name)
-        arrive(ids[0], from_x)
 
         def add_pair(half):
             def add(k, carry):
-                buf[x, half, k] = (buf[x, half, k].astype(F32) + from_x[half, k].astype(F32)).astype(BF16)
+                buf[bit, half, k] = (buf[bit, half, k].astype(F32) + got[half, k].astype(F32)).astype(BF16)
                 return carry
 
             lax.fori_loop(0, 2, add, 0)
 
-        add_pair(1 - z_low)
-        ids.append(send(buf.at[x, 1 - z_low], r.get("z_" + name).at[pl.ds(0, 2)], 2 * near + x, "dp"))
-        add_pair(z_low)
-
-    def dp_third(ids, name):
-        buf, from_z = r.get("g_" + name), r.get("z_" + name)
-        arrive(ids[1], from_z.at[pl.ds(0, 2)])
-        given = 1 - z_high
-        buf[x, z_low, given] = (buf[x, z_low, given].astype(F32) + from_z[given].astype(F32)).astype(BF16)
-        ids.append(send(buf.at[x, z_low, given], from_z.at[2], 2 * far + x, "dp"))
-
-    def dp_last(ids, name):
-        buf, from_z, out = r.get("g_" + name), r.get("z_" + name), r.get(name + "_o")
-        arrive(ids[2], from_z.at[2])
-        total = buf[x, z_low, z_high].astype(F32) + from_z[z_high].astype(F32) + from_z[2].astype(F32)
+        add_pair(1 - other)
+        ids.append(send(buf.at[bit, 1 - other], r.get("z_" + name).at[pl.ds(0, 2)], peer, "dp"))
+        add_pair(other)
+
+    def dp_third(name):
+        buf, got, ids = r.get("g_" + name), r.get("z_" + name), sum_ids[name]
+        (bit, _), (other, _), (last, peer) = orders[name]
+        arrive(ids[1], got.at[pl.ds(0, 2)])
+        given = 1 - last
+        buf[bit, other, given] = (buf[bit, other, given].astype(F32) + got[given].astype(F32)).astype(BF16)
+        ids.append(send(buf.at[bit, other, given], got.at[2], peer, "dp"))
+
+    def dp_last(name):
+        buf, got, ids = r.get("g_" + name), r.get("z_" + name), sum_ids[name]
+        (bit, _), (other, _), (last, _) = orders[name]
+        arrive(ids[2], got.at[2])
+        total = buf[bit, other, last].astype(F32) + got[last].astype(F32) + got[2].astype(F32)
         if name == "qkv":
             for part in range(3):
-                out[part] = total[:, part * local : (part + 1) * local]
+                r.qkv_v[part] = total[:, part * local : (part + 1) * local]
+        elif name == "outa":
+            r.outer_v[pl.ds(0, hid // 2), :] = total
+        elif name == "outb":
+            r.outer_v[pl.ds(hid // 2, hid // 2), :] = total
         else:
-            out[...] = total
+            r.get(name + "_v")[...] = total
+
+    leaving = []
+
+    def leave(name):
+        leaving.append(fetch(r.get(name + "_v"), r.get(name + "_o")))
 
     length = r.len_ref[0]
     c_own.wait()
@@ -317,7 +332,7 @@
     if inside:
         for g in range(4):
             for v in range(2):
-                r.xg[row, g, :, v * 128 : (v + 1) * 128] = phased[g][v].astype(BF16)
+                r.xg[z, g, :, v * 128 : (v + 1) * 128] = phased[g][v].astype(BF16)
         ids_x = dp_gather(xg_slot)
     else:
         r.xflat_o[...] = jnp.concatenate([r.flat[0], r.flat[1]], axis=1).astype(BF16)
@@ -420,18 +435,20 @@
         return slice(part * local + head * HEAD, part * local + (head + 1) * HEAD)
 
     for hp in range(2):
+        pair_columns = slice(hp * 128, (hp + 1) * 128)
+        r.keys_t[...] = r.proj[:, local + hp * 128 : local + (hp + 1) * 128].T
 
         def attend(b, carry):
             rows = aligned(b * block, block, block)
             outs = []
             for head in (2 * hp, 2 * hp + 1):
-                scores = nt(r.proj[rows, head_columns(0, head)], r.proj[:, head_columns(1, head)]) * scale
+                scores = nn(r.proj[rows, head_columns(0, head)], r.keys_t[pl.ds((head % 2) * HEAD, HEAD), :]) * scale
                 scores = jnp.where(live_keys, scores, NEGATIVE)
                 weights = jnp.exp(scores - jnp.max(scores, axis=-1, keepdims=True))
                 low = (weights * (1.0 / jnp.sum(weights, axis=-1, keepdims=True))).astype(BF16)
                 r.probs[head, rows, :] = low
                 outs.append(nn(low, r.proj[:, head_columns(2, head)]))
-            r.ctx[rows, hp * 128 : (hp + 1) * 128] = jnp.concatenate(outs, axis=1).astype(BF16)
+            r.ctx[rows, pair_columns] = jnp.concatenate(outs, axis=1).astype(BF16)
             return carry
 
         lax.fori_loop(0, slots // block, attend, 0)
@@ -524,28 +541,32 @@
     arrive(ids2[2], r.full2.at[rows_of(diag), :])
     feed(far_pair)
 
-    def grad_two_part(owner, columns):
-        return nt(r.grad_in[rows_of(owner), :], r.w_inner[columns, :])
-
-    def branch_part(owner, columns):
-        return nn(r.hidden[rows_of(owner), :], r.w_outer[:, columns])
-
-    sent(ids_a)
-    ids_b = scatter_start(grad_two_part, main_bufs)
-    scatter_own(grad_two_part)
-
-    def store_columns(dst, rows, value):
+    def store_columns(dst, rows, value, first_x=True):
         for k in range(4):
             for j in range(2):
                 start = (2 * k + j) * 128
-                dst[j, k % 2, k // 2, rows, :] = value[:, start : start + 128].astype(BF16)
-
-    def outer_tile(rows):
-        value = tn(r.hidden[:, rows], r.cot_full[...])
-        if inside:
-            store_columns(r.g_outer, rows, value)
-        else:
-            r.g_outer[rows, :] = value.astype(BF16)
+                place = (j, k % 2, k // 2) if first_x else (k % 2, k // 2, j)
+                dst[(*place, rows)] = value[:, start : start + 128].astype(BF16)
+
+    if inside:
+        half_hid = hid // 2
+
+        def outer_part(name, offset):
+            def tile(rows):
+                value = tn(r.hidden[:, aligned(offset + rows.start, 256, 256)], r.cot_full[...])
+                store_columns(r.get("g_" + name), rows, value, name == "outa")
+
+            tiles(half_hid, tile)
+            dp_first(name)
+
+        outer_part("outb", half_hid)
+        outer_part("outa", 0)
+    else:
+
+        def outer_tile(rows):
+            r.g_outer[rows, :] = tn(r.hidden[:, rows], r.cot_full[...]).astype(BF16)
+
+        tiles(hid, outer_tile)
 
     def grouped_rows(dst, left, right):
         def tile(b, carry):
@@ -560,9 +581,16 @@
 
         lax.fori_loop(0, width // 256, tile, 0)
 
-    tiles(hid, outer_tile)
-    if inside:
-        ids_outer = dp_first("outer")
+    def grad_two_part(owner, columns):
+        return nt(r.grad_in[rows_of(owner), :], r.w_inner[columns, :])
+
+    def branch_part(owner, columns):
+        return nn(r.hidden[rows_of(owner), :], r.w_outer[:, columns])
+
+    sent(ids_a)
+    ids_b = scatter_start(grad_two_part, main_bufs)
+    scatter_own(grad_two_part)
+
     scatter_end(ids_b, main_bufs)
 
     def put_sum(k, value):
@@ -590,7 +618,7 @@
 
     grouped_rows(r.g_inner, r.full2, r.grad_in)
     if inside:
-        ids_inner = dp_first("inner")
+        dp_first("inner")
     gather_relay(ids3, r.full3)
     ids_f = scatter_start(branch_part, ff_bufs)
 
@@ -600,18 +628,21 @@
     g_out = tn(r.ctx[...], r.full3[...])
     if inside:
         store_columns(r.g_out, pl.ds(0, local), g_out)
-        ids_out = dp_first("out")
+        dp_first("out")
+        dp_second("outb")
+        dp_second("outa")
     else:
         r.g_out[...] = g_out.astype(BF16)
 
     for hp in range(2):
+        r.keys_t[...] = r.proj[:, 2 * local + hp * 128 : 2 * local + (hp + 1) * 128].T
 
         def back_scores(b, carry):
             rows = aligned(b * block, block, block)
             outs = []
             for j, head in enumerate((2 * hp, 2 * hp + 1)):
                 p = r.probs[head, rows, :].astype(F32)
-                gp = nt(r.gctx[rows, head_columns(0, head)], r.proj[:, head_columns(2, head)])
+                gp = nn(r.gctx[rows, head_columns(0, head)], r.keys_t[pl.ds(j * HEAD, HEAD), :])
                 gs = (p * (gp - jnp.sum(p * gp, axis=-1, keepdims=True))).astype(BF16)
                 r.gscore[j, rows, :] = gs
                 outs.append(nn(gs, r.proj[:, head_columns(1, head)]))
@@ -619,12 +650,17 @@
             return carry
 
         lax.fori_loop(0, slots // block, back_scores, 0)
-        gk = [tn(r.gscore[j], r.proj[:, head_columns(0, 2 * hp + j)]) for j in range(2)]
-        r.gproj[:, local + hp * 128 : local + (hp + 1) * 128] = (jnp.concatenate(gk, axis=1) * scale).astype(BF16)
-        gv = [tn(r.probs[2 * hp + j], r.gctx[:, head_columns(0, 2 * hp + j)]) for j in range(2)]
-        r.gproj[:, 2 * local + hp * 128 : 2 * local + (hp + 1) * 128] = jnp.concatenate(gv, axis=1).astype(BF16)
+        columns = slice(local + hp * 128, local + (hp + 1) * 128)
+        queries_t = r.proj[:, hp * 128 : (hp + 1) * 128].T
+        gk = [nn(queries_t[j * HEAD : (j + 1) * HEAD], r.gscore[j]) for j in range(2)]
+        r.gproj[:, columns] = (jnp.concatenate(gk, axis=0) * scale).T.astype(BF16)
+        columns = slice(2 * local + hp * 128, 2 * local + (hp + 1) * 128)
+        gctx_t = r.gctx[:, hp * 128 : (hp + 1) * 128].T
+        gv = [nn(gctx_t[j * HEAD : (j + 1) * HEAD], r.probs[2 * hp + j]) for j in range(2)]
+        r.gproj[:, columns] = jnp.concatenate(gv, axis=0).T.astype(BF16)
         if inside and hp == 0:
-            dp_second(ids_outer, "outer")
+            dp_third("outb")
+            dp_third("outa")
 
     def grad_one_part(owner, columns):
         return nt(r.gproj[rows_of(owner), :], r.w_qkv[columns, :])
@@ -634,7 +670,8 @@
     scatter_own(grad_one_part)
     grouped_rows(r.g_qkv, r.full1, r.gproj)
     if inside:
-        ids_qkv = dp_first("qkv")
+        dp_first("qkv")
+        dp_second("inner")
     scatter_end(ids_c, main_bufs)
 
     def back_one(b):
@@ -648,16 +685,19 @@
     r.ga_recv[rows_of(me), :] = r.ga_send[:, columns_of(me)]
 
     if inside:
-        dp_third(ids_outer, "outer")
+        dp_last("outa")
+        dp_last("outb")
+        leave("outer")
 
     scatter_own(branch_part)
     scatter_end(ids_f, ff_bufs)
 
     def finish(b):
         rows = own(b)
-        r.output_o[rows, :] = (r.s2[rows, :] + summed(rows, ff_bufs) + vec_row(5)).astype(BF16)
+        r.output_v[rows, :] = (r.s2[rows, :] + summed(rows, ff_bufs) + vec_row(5)).astype(BF16)
 
     each_chunk(finish)
+    leave("output")
     ones = jnp.ones((8, slots), BF16)
     sums = nn(ones, r.gproj[...])
     r.small[pl.ds(7, 1), 0:local] = sums[0:1, 0:local]
@@ -678,7 +718,7 @@
             both.append(value)
             r.small[pl.ds(6, 1), g * 256 + v * 128 : g * 256 + (v + 1) * 128] = jnp.sum(value, axis=0, keepdims=True)
             if inside:
-                r.gt[g, lanes, aligned(row * steps, steps, steps)] = value.T.astype(BF16)
+                r.gt[g, lanes, aligned(z * steps, steps, steps)] = value.T.astype(BF16)
         grads.append(both)
 
     def gt_slot(e):
@@ -688,13 +728,9 @@
     between = [lambda: None] * 4
     if inside:
         ids_g = dp_gather(gt_slot)
-        dp_second(ids_inner, "inner")
-        between = [
-            lambda: dp_second(ids_out, "out"),
-            lambda: dp_third(ids_inner, "inner"),
-            lambda: dp_relay(ids_g, gt_slot),
-            lambda: dp_third(ids_out, "out"),
-        ]
+        dp_second("out")
+        between[2] = lambda: dp_relay(ids_g, gt_slot)
+        between[3] = lambda: [dp_third("inner"), dp_third("out")]
         i_mini = [send(r.small.at[pl.ds(0, 8), columns_of(p)], r.mini_t.at[me], p) for p in peers]
         r.mini_t[me] = r.small[pl.ds(0, 8), columns_of(me)]
     else:
@@ -712,7 +748,56 @@
     r.gx_recv[:, columns_of(me)] = r.gx_send[rows_of(me), :]
 
     if inside:
+        reach = 5
+        count = taps_n // 8
+        taps_width = count * HEAD
+
+        def build(owner):
+            for k in range(4):
+                for g in range(4):
+                    for v in range(2):
+                        lanes = slice(v * 128, (v + 1) * 128)
+                        r.padded[g, v, pl.ds(PAD, steps), :] = r.xg[k, g, :, lanes].astype(F32)
+                for a in range(reach):
+                    for g in range(4):
+                        for v in range(2):
+                            lanes = slice(v * 128, (v + 1) * 128)
+                            moved = r.padded[g, v, pl.ds(owner * (count // PHASES) + a, steps), :]
+                            start = ((a * 4 + g) * 4 + k) * steps
+                            r.wide[start : start + steps, lanes] = moved.astype(BF16)
+
+        def accumulate():
+            r.tap_acc[...] = jnp.zeros_like(r.tap_acc)
+
+            def one(index, carry):
+                a = index % reach
+                for half in range(2):
+                    g = 2 * (index // reach) + half
+                    value = nn(r.gt[g], r.wide[aligned((a * 4 + g) * 4 * steps, 4 * steps, steps), :])
+                    for s in range(PHASES):
+                        parity = s % 2
+                        start = (PHASES * a - s + 3 + (1 - parity)) * HEAD
+                        lanes = aligned(start, 256, 128)
+                        r.tap_acc[g, parity, :, lanes] = r.tap_acc[g, parity, :, lanes] + value[s * HEAD : (s + 1) * HEAD, :]
+                return carry
+
+            lax.fori_loop(0, 2 * reach, one, 0)
+
+        def tap_columns(v):
+            both = []
+            for g in (2 * v, 2 * v + 1):
+                even = r.tap_acc[g, 0, :, 256 : 256 + taps_width]
+                odd = pltpu.roll(r.tap_acc[g, 1], r.tap_acc.shape[3] - HEAD, 1)[:, 128 : 128 + taps_width]
+                both.append(even + odd)
+            return jnp.concatenate(both, axis=0).T
+
+        dp_second("qkv")
+        build(x_mate)
         dp_relay_last(ids_g, gt_slot)
+        accumulate()
+        for v in range(2):
+            r.tap_send[:, v * 128 : (v + 1) * 128] = tap_columns(v).astype(BF16)
+        i_tap = send(r.tap_send, r.tap_recv, x_mate, "dp")
 
         for index, p in zip(i_mini, peers):
             arrive(index, r.mini_t.at[p])
@@ -737,83 +822,45 @@
         arrive(i_mx, r.mini_x)
         r.mini_s[...] = r.mini[...] + r.mini_x[...]
         i_mz = [send(r.mini_s, r.mini_z.at[0], 2 * near + x, "dp")]
-        dp_second(ids_qkv, "qkv")
         arrive(i_mz[0], r.mini_z.at[0])
         r.mini_z[2] = r.mini_s[...] + r.mini_z[0]
         i_mz.append(send(r.mini_z.at[2], r.mini_z.at[1], 2 * far + x, "dp"))
-        dp_gathered(ids_x, xg_slot)
 
     for index, p in zip(i_gx, peers):
         arrive(index, r.gx_recv.at[:, columns_of(p)])
 
     def frames_back(b):
         rows = own(b)
-        r.frames_grad_o[rows, :] = jnp.where(live_rows(b), r.grad_one[rows, :] + r.gx_recv[rows, :].astype(F32), 0.0)
+        r.frames_grad_v[rows, :] = jnp.where(live_rows(b), r.grad_one[rows, :] + r.gx_recv[rows, :].astype(F32), 0.0)
 
     each_chunk(frames_back)
+    leave("frames_grad")
 
     if inside:
         arrive(i_mz[1], r.mini_z.at[1])
         r.small_o[me] = r.mini_z[2] + r.mini_z[1]
         i_mt = [send(r.small_o.at[me], r.small_o.at[me], p) for p in peers]
 
-        reach = 5
-        count = taps_n // 8
-
-        def build(column):
-            for k in range(4):
-                e = 2 * k + column
-                for g in range(4):
-                    for v in range(2):
-                        lanes = slice(v * 128, (v + 1) * 128)
-                        r.padded[g, v, pl.ds(PAD, steps), :] = r.xg[e, g, :, lanes].astype(F32)
-                for a in range(reach):
-                    for g in range(4):
-                        for v in range(2):
-                            lanes = slice(v * 128, (v + 1) * 128)
-                            moved = r.padded[g, v, pl.ds(row * (count // PHASES) + a, steps), :]
-                            start = ((a * 4 + g) * 4 + k) * steps
-                            r.wide[start : start + steps, lanes] = moved.astype(BF16)
-
-        def accumulate(column, first):
-            def one(index, carry):
-                g = index // reach
-                a = index % reach
-                left = jnp.concatenate([r.gt[g, :, aligned((2 * k + column) * steps, steps, steps)] for k in range(4)], axis=1)
-                value = nn(left, r.wide[aligned((a * 4 + g) * 4 * steps, 4 * steps, steps), :])
-                for s in range(PHASES):
-                    parity = s % 2
-                    start = (PHASES * a - s + 3 + (1 - parity)) * HEAD
-                    lanes = aligned(start, 256, 128)
-                    r.tap_acc[g, parity, :, lanes] = r.tap_acc[g, parity, :, lanes] + value[s * HEAD : (s + 1) * HEAD, :]
-                return carry
-
-            lax.fori_loop(0, 4 * reach, one, 0)
-
-        r.tap_acc[...] = jnp.zeros_like(r.tap_acc)
-        build(x)
-        accumulate(x, True)
-        dp_third(ids_qkv, "qkv")
-        build(1 - x)
-        dp_gathered(ids_g, gt_slot)
-        accumulate(1 - x, False)
-        taps_width = count * HEAD
+        build(row)
+        accumulate()
+        dp_third("qkv")
+        dp_last("inner")
+        leave("inner")
+        dp_last("out")
+        leave("out")
+        arrive(i_tap, r.tap_recv)
         for v in range(2):
-            both = []
-            for g in (2 * v, 2 * v + 1):
-                even = r.tap_acc[g, 0, :, 256 : 256 + taps_width]
-                odd = pltpu.roll(r.tap_acc[g, 1], r.tap_acc.shape[3] - HEAD, 1)[:, 128 : 128 + taps_width]
-                both.append(even + odd)
-            r.pos_o[:, v * 128 : (v + 1) * 128] = jnp.concatenate(both, axis=0).T
-
-        dp_last(ids_outer, "outer")
-        dp_last(ids_inner, "inner")
-        dp_last(ids_out, "out")
-        dp_last(ids_qkv, "qkv")
+            lanes = slice(v * 128, (v + 1) * 128)
+            r.pos_v[:, lanes] = tap_columns(v) + r.tap_recv[:, lanes].astype(F32)
+        leave("pos")
+        dp_last("qkv")
+        leave("qkv")
         for index, p in zip(i_mt, peers):
             arrive(index, r.small_o.at[p])
     else:
         r.small_o[...] = r.small[...]
+    for copy in leaving:
+        copy.wait()
     sent(list(pending))
 
 
@@ -828,7 +875,7 @@
     vmem = pl.BlockSpec(memory_space=pltpu.VMEM)
     inputs = ["len_ref", "frames_in", "cot_in", "taps_in", "qkv_in", "out_in", "inner_in", "outer_in"]
     inputs += ["v" + str(k) for k in range(7)] + ["qv_in", "pos_in"]
-    outs = [("output_o", (seg, width), BF16), ("frames_grad_o", (seg, width), F32)]
+    big = [("output", (seg, width), BF16), ("frames_grad", (seg, width), F32)]
     grads = {
         "outer": ((hid, 128), (hid, width)),
         "inner": ((128, hid), (width, hid)),
@@ -837,13 +884,19 @@
     }
     sums = []
     if inside:
-        outs += [("small_o", (4, 16, local), F32), ("pos_o", (taps_n // 8 * HEAD, local), F32)]
+        big += [("pos", (taps_n // 8 * HEAD, local), F32)]
         for name, (part, _) in grads.items():
-            outs.append((name + "_o", (3, part[0], local) if name == "qkv" else part, F32))
-            sums += [("g_" + name, (2, 2, 2) + part, BF16), ("x_" + name, (2, 2) + part, BF16), ("z_" + name, (3,) + part, BF16)]
+            big.append((name, (3, part[0], local) if name == "qkv" else part, F32))
+            pieces = [("outa", (hid // 2, 128)), ("outb", (hid // 2, 128))] if name == "outer" else [(name, part)]
+            for piece, shape in pieces:
+                sums += [("g_" + piece, (2, 2, 2) + shape, BF16), ("x_" + piece, (2, 2) + shape, BF16)]
+                sums += [("z_" + piece, (3,) + shape, BF16)]
+        outs = [("small_o", (4, 16, local), F32)]
         sums += [
-            ("xg", (8, 4, steps, 256), BF16),
-            ("gt", (4, 256, 8 * steps), BF16),
+            ("xg", (4, 4, steps, 256), BF16),
+            ("gt", (4, 256, 4 * steps), BF16),
+            ("tap_send", (taps_n // 8 * HEAD, local), BF16),
+            ("tap_recv", (taps_n // 8 * HEAD, local), BF16),
             ("tap_acc", (4, 2, HEAD, 12 * 128), F32),
             ("mini_t", (4, 8, local), F32),
             ("mini", (16, local), F32),
@@ -852,8 +905,12 @@
             ("mini_z", (3, 16, local), F32),
         ]
     else:
-        outs += [("small_o", (16, width), F32), ("xflat_o", (slots, local), BF16), ("gcflat_o", (slots, local), BF16)]
+        outs = [("small_o", (16, width), F32), ("xflat_o", (slots, local), BF16), ("gcflat_o", (slots, local), BF16)]
         outs += [("g_" + name, whole, BF16) for name, (_, whole) in grads.items()]
+    sums += [(name + "_v", shape, kind) for name, shape, kind in big]
+    any_outs = [(name + "_o", shape, kind) for name, shape, kind in big]
+    kept = len(outs)
+    outs = outs[:1] + any_outs + outs[1:]
     main = [("send", (2, seg, width)), ("core", (2, seg, width)), ("mid", (seg, width)), ("y", (seg, width))]
     scratch = [
         ("paired", (4, (taps_n + 7) * HEAD, 128), BF16),
@@ -875,6 +932,7 @@
         ("proj", (slots, 3 * local), BF16),
         ("probs", (4, slots, slots), BF16),
         ("ctx", (slots, local), BF16),
+        ("keys_t", (128, slots), BF16),
         ("keep", (seg, width), F32),
         *[("rs_" + name, shape, BF16) for name, shape in main],
         *[("rf_" + name, shape, BF16) for name, shape in main],
@@ -901,9 +959,9 @@
         functools.partial(layer_kernel, (slots, seg, width, local, hid, taps_n), names, inside),
         out_shape=[jax.ShapeDtypeStruct(shape, kind) for _, shape, kind in outs],
         in_specs=[pl.BlockSpec(memory_space=pltpu.SMEM)] + [any_spec] * 7 + [vmem] * 9,
-        out_specs=[vmem] * len(outs),
+        out_specs=[vmem] + [any_spec] * len(big) + [vmem] * (kept - 1),
         scratch_shapes=[pltpu.VMEM(shape, kind) for _, shape, kind in scratch]
-        + [pltpu.SemaphoreType.DMA((copies,)), pltpu.SemaphoreType.DMA((copies,)), pltpu.SemaphoreType.DMA((16,))],
+        + [pltpu.SemaphoreType.DMA((copies,)), pltpu.SemaphoreType.DMA((copies,)), pltpu.SemaphoreType.DMA((20,))],
         compiler_params=pltpu.CompilerParams(collective_id=0, has_side_effects=True, vmem_limit_bytes=VMEM_LIMIT),
         name="layer",
     )(lengths, frames, cot, taps, qkv, out_w, inner_w, outer_w, *vectors)
@@ -994,7 +1052,7 @@
         outer_weight,
         vectors,
     )
-    output, frames_grad, small = results[:3]
+    small, output, frames_grad = results[:3]
     if inside:
         pos_grad, g_outer, g_inner, g_out, g_qkv = results[3:]
         arrays = [output, frames_grad, pos_grad, g_outer, g_inner, g_out, g_qkv]

time: 209 us -> 196 us (0.938)
  Pallas kernels: 208 us -> 194 us
    pallas_call x1, Pallas kernels: 203 us -> 189 us  [run_layer(): pl.pallas_call(functools.partial(layer_kernel, (slots, seg, width, local,...]
where the time goes in v4:
time: 196 us; the launch traced here: 195 us
  Pallas kernels  194 us (99%)
    pallas_call x1, Pallas kernels, run_layer(): pl.pallas_call(functools.partial(layer_kernel, (slots, seg, width, local,...  189 us
    pallas_call x1, Pallas kernels, finish(): pl.pallas_call(functools.partial(finish_kernel, len(arrays)), out_shape=s...  4.56 us

profile of v4, /device:TPU:0, one launch (start us, length us, event | category | flops | bytes accessed | tf_op | source)
XLA Modules:
  0.0 195.4 jit_solution(15381122221658627896)
XLA Ops:
  1.3 189.4 %layer.1 = (f32[4,16,256]{2,1,0:T(8,128)}, bf16[128,1024]{1,0:T(8,128)(2,1)}, f32[128,1024]{1,0:T(8,128)}, f32[1024,256]{1,0:T(8,128)}, f32[1024,128]{1,0:T(8,12...) custom-call(s32[1]{0:T(128)S(6)} %copy.33.refs_0_, bf16[128,1024]{1,0:T(8,128)(2,1)} %bitcast.18, ...), custom_call_target="tpu_custom_call" | custom-call | tf_op jit(solution)/shard_map/layer/pallas_call | solution.py:958
  190.7 4.6 %finish.1 = (bf16[128,1024]{1,0:T(8,128)(2,1)}, f32[128,1024]{1,0:T(8,128)}, f32[1024,256]{1,0:T(8,128)}, f32[1024,128]{1,0:T(8,128)}, f32[128,1024]{1,0:T(8,128...) custom-call(bf16[128,1024]{1,0:T(8,128)(2,1)} %get-tuple-element.40., ...), custom_call_target="tpu_custom_call" | custom-call | tf_op jit(solution)/shard_map/finish/pallas_call | solution.py:1001

commit v5 on v4

--- a/solution.py
+++ b/solution.py
@@ -265,7 +265,7 @@
 
     x_order = ((x, x_mate), (z_low, 2 * near + x), (z_high, 2 * far + x))
     z_order = (x_order[1], x_order[2], x_order[0])
-    orders = {"outa": x_order, "outb": z_order, "inner": x_order, "out": x_order, "qkv": x_order}
+    orders = {"outa": x_order, "outb": z_order, "inner": x_order, "out": z_order, "qkv": x_order}
     sum_ids = {}
 
     def dp_first(name):
@@ -620,6 +620,9 @@
     if inside:
         dp_first("inner")
     gather_relay(ids3, r.full3)
+    if inside:
+        dp_second("outa")
+        dp_second("outb")
     ids_f = scatter_start(branch_part, ff_bufs)
 
     arrive(ids3[0], r.full3.at[rows_of(mate), :])
@@ -627,10 +630,8 @@
     r.gctx[...] = nt(r.full3[...], r.w_out[...]).astype(BF16)
     g_out = tn(r.ctx[...], r.full3[...])
     if inside:
-        store_columns(r.g_out, pl.ds(0, local), g_out)
+        store_columns(r.g_out, pl.ds(0, local), g_out, False)
         dp_first("out")
-        dp_second("outb")
-        dp_second("outa")
     else:
         r.g_out[...] = g_out.astype(BF16)
 
@@ -658,8 +659,7 @@
         gctx_t = r.gctx[:, hp * 128 : (hp + 1) * 128].T
         gv = [nn(gctx_t[j * HEAD : (j + 1) * HEAD], r.probs[2 * hp + j]) for j in range(2)]
         r.gproj[:, columns] = jnp.concatenate(gv, axis=0).T.astype(BF16)
-        if inside and hp == 0:
-            dp_third("outb")
+        if inside and hp == 1:
             dp_third("outa")
 
     def grad_one_part(owner, columns):
@@ -671,7 +671,8 @@
     grouped_rows(r.g_qkv, r.full1, r.gproj)
     if inside:
         dp_first("qkv")
-        dp_second("inner")
+        dp_third("outb")
+        dp_second("out")
     scatter_end(ids_c, main_bufs)
 
     def back_one(b):
@@ -685,9 +686,7 @@
     r.ga_recv[rows_of(me), :] = r.ga_send[:, columns_of(me)]
 
     if inside:
-        dp_last("outa")
-        dp_last("outb")
-        leave("outer")
+        dp_second("inner")
 
     scatter_own(branch_part)
     scatter_end(ids_f, ff_bufs)
@@ -728,9 +727,47 @@
     between = [lambda: None] * 4
     if inside:
         ids_g = dp_gather(gt_slot)
-        dp_second("out")
-        between[2] = lambda: dp_relay(ids_g, gt_slot)
-        between[3] = lambda: [dp_third("inner"), dp_third("out")]
+        i_small = []
+
+        def small_first():
+            for index, p in zip(i_mini, peers):
+                arrive(index, r.mini_t.at[p])
+            quarter = r.mini_t[0] + r.mini_t[1] + r.mini_t[2] + r.mini_t[3]
+            folded = []
+            for v in range(2):
+                parts = []
+                for g in (2 * v, 2 * v + 1):
+                    both = r.small[pl.ds(6, 1), g * 256 : g * 256 + 128] + r.small[pl.ds(6, 1), g * 256 + 128 : (g + 1) * 256]
+                    both = jnp.broadcast_to(both, (8, 128))
+                    parts.append(both + swap_halves(both))
+                folded.append(jnp.where(low_half(8), parts[0], parts[1])[0:1])
+            r.mini[pl.ds(0, 8), :] = quarter
+            r.mini[pl.ds(6, 1), :] = jnp.concatenate(folded, axis=1)
+            r.mini[pl.ds(7, 1), :] = r.small[pl.ds(7, 1), 0:local]
+            r.mini[pl.ds(8, 1), :] = r.small[pl.ds(7, 1), local : 2 * local]
+            for k in range(4):
+                r.mini[pl.ds(9 + k, 1), :] = r.small[pl.ds(8, 1), k * 256 : (k + 1) * 256]
+            r.mini[pl.ds(13, 3), :] = jnp.zeros((3, 256), F32)
+            i_small.append(send(r.mini, r.mini_x, x_mate, "dp"))
+
+        def small_second():
+            arrive(i_small[0], r.mini_x)
+            r.mini_s[...] = r.mini[...] + r.mini_x[...]
+            i_small.append(send(r.mini_s, r.mini_z.at[0], 2 * near + x, "dp"))
+
+        def small_third():
+            arrive(i_small[1], r.mini_z.at[0])
+            r.mini_z[2] = r.mini_s[...] + r.mini_z[0]
+            i_small.append(send(r.mini_z.at[2], r.mini_z.at[1], 2 * far + x, "dp"))
+
+        def small_last():
+            arrive(i_small[2], r.mini_z.at[1])
+            r.small_o[me] = r.mini_z[2] + r.mini_z[1]
+            return [send(r.small_o.at[me], r.small_o.at[me], p) for p in peers]
+
+        between[0] = small_first
+        between[1] = lambda: dp_third("out")
+        between[2] = lambda: [small_second(), dp_relay(ids_g, gt_slot), dp_second("qkv"), dp_third("inner")]
         i_mini = [send(r.small.at[pl.ds(0, 8), columns_of(p)], r.mini_t.at[me], p) for p in peers]
         r.mini_t[me] = r.small[pl.ds(0, 8), columns_of(me)]
     else:
@@ -791,41 +828,14 @@
                 both.append(even + odd)
             return jnp.concatenate(both, axis=0).T
 
-        dp_second("qkv")
         build(x_mate)
         dp_relay_last(ids_g, gt_slot)
         accumulate()
+        dp_last("outa")
         for v in range(2):
             r.tap_send[:, v * 128 : (v + 1) * 128] = tap_columns(v).astype(BF16)
         i_tap = send(r.tap_send, r.tap_recv, x_mate, "dp")
 
-        for index, p in zip(i_mini, peers):
-            arrive(index, r.mini_t.at[p])
-        quarter = r.mini_t[0] + r.mini_t[1] + r.mini_t[2] + r.mini_t[3]
-        folded = []
-        for v in range(2):
-            parts = []
-            for g in (2 * v, 2 * v + 1):
-                both = r.small[pl.ds(6, 1), g * 256 : g * 256 + 128] + r.small[pl.ds(6, 1), g * 256 + 128 : (g + 1) * 256]
-                both = jnp.broadcast_to(both, (8, 128))
-                parts.append(both + swap_halves(both))
-            folded.append(jnp.where(low_half(8), parts[0], parts[1])[0:1])
-        r.mini[pl.ds(0, 8), :] = quarter
-        r.mini[pl.ds(6, 1), :] = jnp.concatenate(folded, axis=1)
-        r.mini[pl.ds(7, 1), :] = r.small[pl.ds(7, 1), 0:local]
-        r.mini[pl.ds(8, 1), :] = r.small[pl.ds(7, 1), local : 2 * local]
-        for k in range(4):
-            r.mini[pl.ds(9 + k, 1), :] = r.small[pl.ds(8, 1), k * 256 : (k + 1) * 256]
-        r.mini[pl.ds(13, 3), :] = jnp.zeros((3, 256), F32)
-        i_mx = send(r.mini, r.mini_x, x_mate, "dp")
-
-        arrive(i_mx, r.mini_x)
-        r.mini_s[...] = r.mini[...] + r.mini_x[...]
-        i_mz = [send(r.mini_s, r.mini_z.at[0], 2 * near + x, "dp")]
-        arrive(i_mz[0], r.mini_z.at[0])
-        r.mini_z[2] = r.mini_s[...] + r.mini_z[0]
-        i_mz.append(send(r.mini_z.at[2], r.mini_z.at[1], 2 * far + x, "dp"))
-
     for index, p in zip(i_gx, peers):
         arrive(index, r.gx_recv.at[:, columns_of(p)])
 
@@ -837,13 +847,13 @@
     leave("frames_grad")
 
     if inside:
-        arrive(i_mz[1], r.mini_z.at[1])
-        r.small_o[me] = r.mini_z[2] + r.mini_z[1]
-        i_mt = [send(r.small_o.at[me], r.small_o.at[me], p) for p in peers]
-
+        small_third()
         build(row)
         accumulate()
+        i_mt = small_last()
         dp_third("qkv")
+        dp_last("outb")
+        leave("outer")
         dp_last("inner")
         leave("inner")
         dp_last("out")

time: 196 us -> 177 us (0.903)
  Pallas kernels: 194 us -> 176 us
    pallas_call x1, Pallas kernels: 189 us -> 171 us  [run_layer(): pl.pallas_call(functools.partial(layer_kernel, (slots, seg, width, local,...]
where the time goes in v5:
time: 177 us
  Pallas kernels  176 us (99%)
    pallas_call x1, Pallas kernels, run_layer(): pl.pallas_call(functools.partial(layer_kernel, (slots, seg, width, local,...  171 us
    pallas_call x1, Pallas kernels, finish(): pl.pallas_call(functools.partial(finish_kernel, len(arrays)), out_shape=s...  4.56 us

profile of v5, /device:TPU:0, one launch (start us, length us, event | category | flops | bytes accessed | tf_op | source)
XLA Modules:
  0.0 177.0 jit_solution(9203505926442142625)
XLA Ops:
  1.3 171.0 %layer.1 = (f32[4,16,256]{2,1,0:T(8,128)}, bf16[128,1024]{1,0:T(8,128)(2,1)}, f32[128,1024]{1,0:T(8,128)}, f32[1024,256]{1,0:T(8,128)}, f32[1024,128]{1,0:T(8,12...) custom-call(s32[1]{0:T(128)S(6)} %copy.33.refs_0_, bf16[128,1024]{1,0:T(8,128)(2,1)} %bitcast.18, ...), custom_call_target="tpu_custom_call" | custom-call | tf_op jit(solution)/shard_map/layer/pallas_call | solution.py:968
  172.3 4.6 %finish.1 = (bf16[128,1024]{1,0:T(8,128)(2,1)}, f32[128,1024]{1,0:T(8,128)}, f32[1024,256]{1,0:T(8,128)}, f32[1024,128]{1,0:T(8,128)}, f32[128,1024]{1,0:T(8,128...) custom-call(bf16[128,1024]{1,0:T(8,128)(2,1)} %get-tuple-element.40., ...), custom_call_target="tpu_custom_call" | custom-call | tf_op jit(solution)/shard_map/finish/pallas_call | solution.py:1011

commit v6 on v5

--- a/solution.py
+++ b/solution.py
@@ -216,10 +216,6 @@
     c_taps = fetch(r.taps_in, r.wide.at[pl.ds(0, taps_n * HEAD), :])
     c_frames = fetch(r.frames_in, r.frames_v)
     c_cot = fetch(r.cot_in, r.cot_full.at[rows_of(me), :])
-    c_qkv = [fetch(r.qkv_in.at[part], r.w_qkv.at[:, pl.ds(part * local, local)]) for part in range(3)]
-    c_out = fetch(r.out_in, r.w_out)
-    c_inner = fetch(r.inner_in, r.w_inner)
-    c_outer = fetch(r.outer_in, r.w_outer)
 
     barrier = pltpu.get_barrier_semaphore()
     greet = [("tensor", p) for p in peers]
@@ -250,6 +246,10 @@
         both = (jnp.where(low_half(8), half, other) if h == 0 else jnp.where(low_half(8), other, half))[0:1]
         r.vec[pl.ds(8, 1), g * 256 : (g + 1) * 256] = jnp.concatenate([both, both], axis=1)
     c_taps.wait()
+    c_qkv = [fetch(r.qkv_in.at[part], r.w_qkv.at[:, pl.ds(part * local, local)]) for part in range(3)]
+    c_out = fetch(r.out_in, r.w_out)
+    c_inner = fetch(r.inner_in, r.w_inner)
+    c_outer = fetch(r.outer_in, r.w_outer)
     pair_taps(r.wide, taps_n, r.paired)
 
     def dp_gather(slot):
@@ -471,10 +471,15 @@
             return send(send_buf.at[slot], core_buf.at[slot], mate)
 
         ids = [to(1, diag), to(0, mate)]
+
+        def early(columns):
+            r.keep[:, columns] = partial(across, columns)
+
+        tiles(width, early)
         arrive(ids[0], core_buf.at[1])
 
         def tile(columns):
-            mid_buf[:, columns] = (partial(across, columns) + core_buf[1, :, columns].astype(F32)).astype(BF16)
+            mid_buf[:, columns] = (r.keep[:, columns] + core_buf[1, :, columns].astype(F32)).astype(BF16)
 
         tiles(width, tile)
         ids.append(send(mid_buf, y_buf, across))
@@ -762,8 +767,8 @@
 
         def small_last():
             arrive(i_small[2], r.mini_z.at[1])
-            r.small_o[me] = r.mini_z[2] + r.mini_z[1]
-            return [send(r.small_o.at[me], r.small_o.at[me], p) for p in peers]
+            r.small_v[me] = r.mini_z[2] + r.mini_z[1]
+            return [send(r.small_v.at[me], r.small_v.at[me], p) for p in peers]
 
         between[0] = small_first
         between[1] = lambda: dp_third("out")
@@ -858,6 +863,9 @@
         leave("inner")
         dp_last("out")
         leave("out")
+        for index, p in zip(i_mt, peers):
+            arrive(index, r.small_v.at[p])
+        leave("small")
         arrive(i_tap, r.tap_recv)
         for v in range(2):
             lanes = slice(v * 128, (v + 1) * 128)
@@ -865,8 +873,6 @@
         leave("pos")
         dp_last("qkv")
         leave("qkv")
-        for index, p in zip(i_mt, peers):
-            arrive(index, r.small_o.at[p])
     else:
         r.small_o[...] = r.small[...]
     for copy in leaving:
@@ -901,7 +907,8 @@
             for piece, shape in pieces:
                 sums += [("g_" + piece, (2, 2, 2) + shape, BF16), ("x_" + piece, (2, 2) + shape, BF16)]
                 sums += [("z_" + piece, (3,) + shape, BF16)]
-        outs = [("small_o", (4, 16, local), F32)]
+        outs = []
+        big.insert(0, ("small", (4, 16, local), F32))
         sums += [
             ("xg", (4, 4, steps, 256), BF16),
             ("gt", (4, 256, 4 * steps), BF16),
@@ -920,7 +927,8 @@
     sums += [(name + "_v", shape, kind) for name, shape, kind in big]
     any_outs = [(name + "_o", shape, kind) for name, shape, kind in big]
     kept = len(outs)
-    outs = outs[:1] + any_outs + outs[1:]
+    first = 0 if inside else 1
+    outs = outs[:first] + any_outs + outs[first:]
     main = [("send", (2, seg, width)), ("core", (2, seg, width)), ("mid", (seg, width)), ("y", (seg, width))]
     scratch = [
         ("paired", (4, (taps_n + 7) * HEAD, 128), BF16),
@@ -969,25 +977,26 @@
         functools.partial(layer_kernel, (slots, seg, width, local, hid, taps_n), names, inside),
         out_shape=[jax.ShapeDtypeStruct(shape, kind) for _, shape, kind in outs],
         in_specs=[pl.BlockSpec(memory_space=pltpu.SMEM)] + [any_spec] * 7 + [vmem] * 9,
-        out_specs=[vmem] + [any_spec] * len(big) + [vmem] * (kept - 1),
+        out_specs=[vmem] * first + [any_spec] * len(big) + [vmem] * (kept - first),
         scratch_shapes=[pltpu.VMEM(shape, kind) for _, shape, kind in scratch]
-        + [pltpu.SemaphoreType.DMA((copies,)), pltpu.SemaphoreType.DMA((copies,)), pltpu.SemaphoreType.DMA((20,))],
+        + [pltpu.SemaphoreType.DMA((copies,)), pltpu.SemaphoreType.DMA((copies,)), pltpu.SemaphoreType.DMA((22,))],
         compiler_params=pltpu.CompilerParams(collective_id=0, has_side_effects=True, vmem_limit_bytes=VMEM_LIMIT),
         name="layer",
     )(lengths, frames, cot, taps, qkv, out_w, inner_w, outer_w, *vectors)
 
 
 def finish_kernel(count, *refs):
-    ins, small = refs[:count], refs[count]
-    outs, bias = refs[count + 1 : 2 * count + 1], refs[2 * count + 1 : 2 * count + 10]
-    staged, sems = refs[2 * count + 10 : -1], refs[-1]
+    ins = refs[: count + 1]
+    outs, bias_outs = refs[count + 1 : 2 * count + 1], refs[2 * count + 1 : 2 * count + 10]
+    staged, small, bias = refs[2 * count + 10 : 3 * count + 10], refs[3 * count + 10], refs[3 * count + 11 : -1]
+    sems = refs[-1]
+    first = pltpu.make_async_copy(ins[count], small, sems.at[2 * count])
+    first.start()
     loads = [pltpu.make_async_copy(a, b, sems.at[k]) for k, (a, b) in enumerate(zip(ins, staged))]
     stores = [pltpu.make_async_copy(a, b, sems.at[count + k]) for k, (a, b) in enumerate(zip(staged, outs))]
     for copy in loads:
         copy.start()
-    for load, store in zip(loads, stores):
-        load.wait()
-        store.start()
+    first.wait()
     local = small.shape[2]
     for t in range(small.shape[0]):
         for k in range(7):
@@ -997,13 +1006,18 @@
         for k in range(4):
             start = (4 * t + k) * local
             bias[8][0:1, start : start + local] = small[t, pl.ds(9 + k, 1), :]
+    for k in range(9):
+        stores.append(pltpu.make_async_copy(bias[k], bias_outs[k], sems.at[2 * count + 1 + k]))
+        stores[-1].start()
+    for load, store in zip(loads, stores):
+        load.wait()
+        store.start()
     for store in stores:
         store.wait()
 
 
 def finish(arrays, small):
     any_spec = pl.BlockSpec(memory_space=pl.ANY)
-    vmem = pl.BlockSpec(memory_space=pltpu.VMEM)
     width = small.shape[0] * small.shape[2]
     shapes = [jax.ShapeDtypeStruct(a.shape, a.dtype) for a in arrays]
     shapes += [jax.ShapeDtypeStruct((1, width), F32)] * 7
@@ -1011,9 +1025,10 @@
     results = pl.pallas_call(
         functools.partial(finish_kernel, len(arrays)),
         out_shape=shapes,
-        in_specs=[any_spec] * len(arrays) + [vmem],
-        out_specs=[any_spec] * len(arrays) + [vmem] * 9,
-        scratch_shapes=[pltpu.VMEM(a.shape, a.dtype) for a in arrays] + [pltpu.SemaphoreType.DMA((2 * len(arrays),))],
+        in_specs=[any_spec] * (len(arrays) + 1),
+        out_specs=[any_spec] * (len(arrays) + 9),
+        scratch_shapes=[pltpu.VMEM(a.shape, a.dtype) for a in [*arrays, small, *shapes[len(arrays) :]]]
+        + [pltpu.SemaphoreType.DMA((2 * len(arrays) + 10,))],
         compiler_params=pltpu.CompilerParams(vmem_limit_bytes=VMEM_LIMIT),
         name="finish",
     )(*arrays, small)

time: 177 us -> 173 us (0.977)
  Pallas kernels: 176 us -> 171 us
    pallas_call x1, Pallas kernels: 171 us -> 168 us  [run_layer(): pl.pallas_call(functools.partial(layer_kernel, (slots, seg, width, local,...]
where the time goes in v6:
time: 173 us
  Pallas kernels  171 us (99%)
    pallas_call x1, Pallas kernels, run_layer(): pl.pallas_call(functools.partial(layer_kernel, (slots, seg, width, local,...  168 us

profile of v6, /device:TPU:0, one launch (start us, length us, event | category | flops | bytes accessed | tf_op | source)
XLA Modules:
  0.0 172.7 jit_solution(6095715647567382535)
XLA Ops:
  1.3 168.0 %layer.1 = (f32[4,16,256]{2,1,0:T(8,128)}, bf16[128,1024]{1,0:T(8,128)(2,1)}, f32[128,1024]{1,0:T(8,128)}, f32[1024,256]{1,0:T(8,128)}, f32[1024,128]{1,0:T(8,12...) custom-call(s32[1]{0:T(128)S(6)} %copy.33.refs_0_, bf16[128,1024]{1,0:T(8,128)(2,1)} %bitcast.18, ...), custom_call_target="tpu_custom_call" | custom-call | tf_op jit(solution)/shard_map/layer/pallas_call | solution.py:976
  169.4 3.2 %finish.1 = (bf16[128,1024]{1,0:T(8,128)(2,1)}, f32[128,1024]{1,0:T(8,128)}, f32[1024,256]{1,0:T(8,128)}, f32[1024,128]{1,0:T(8,128)}, f32[128,1024]{1,0:T(8,128...) custom-call(bf16[128,1024]{1,0:T(8,128)(2,1)} %get-tuple-element.40., ...), custom_call_target="tpu_custom_call" | custom-call | tf_op jit(solution)/shard_map/finish/pallas_call | solution.py:1025
